TPU v7x, 32 devices: a whole 2x2x4 slice. The times are simulated.
32 devices in a mesh: nodes: 16 (over z, y, core), hid: 2 (over x).
Axes of the slice: x: 2, y: 2, z: 4, core: 2. Of those that a mesh axis runs over, the one named last changes fastest.
Arguments:
- features: bfloat16 [24576, 512], P(('nodes', 'hid')), may hold values from -6 to 6
- levels: int32 [24576], P(('nodes', 'hid')), may hold values from 0 to 1
- neighbour_index: int32 [24576, 16], P(('nodes', 'hid')), may hold values from 0 to 24575, as said below
- neighbour_count: int32 [24576], P(('nodes', 'hid')), may hold values from 2 to 16
- cotangent: bfloat16 [24576, 512], P(('nodes', 'hid')), may hold values from -6 to 6
- attention_weight: float32 [4, 512, 512], replicated
- up_weight: float32 [512, 2048], P(None, 'hid'), may hold values from -0.25 to 0.25
- down_weight: float32 [2048, 512], P('hid'), may hold values from -0.125 to 0.125
- modulation: float32 [2, 4, 512], replicated, may hold values from -0.5 to 0.5
- attention_moment: float32 [4, 512, 512], P(None, 'hid')
- up_moment: float32 [512, 2048], P(None, 'hid')
- down_moment: float32 [2048, 512], P('hid')
- modulation_moment: float32 [2, 4, 512], P(None, 'hid')
Outputs:
- output: bfloat16 [24576, 512], P(('nodes', 'hid'))
- features_grad: float32 [24576, 512], P(('nodes', 'hid'))
- attention_moment_new: float32 [4, 512, 512], P(None, 'hid')
- attention_new: float32 [4, 512, 512], P(None, 'hid')
- up_moment_new: float32 [512, 2048], P(None, 'hid')
- up_new: float32 [512, 2048], P(None, 'hid')
- down_moment_new: float32 [2048, 512], P('hid')
- down_new: float32 [2048, 512], P('hid')
- modulation_moment_new: float32 [2, 4, 512], P(None, 'hid')
- modulation_new: float32 [2, 4, 512], P(None, 'hid')
Inputs may be any that keep to these rules, and one draw needn't show every extreme that they name: `neighbour_index`: slot 0 of every node names the node itself; every slot names a node whose index is at most 192 from the node's own, and slot 1 names the node exactly 192 away wherever that index exists. Slots past a node's count also hold valid indices.
All inputs are finite; a program needn't handle non-finite values.
Results may differ from a plain program's by a relative error of at most 0.018.
The roundings to bfloat16 on the way count: a program that leaves them out, or rounds other values in their place, can miss the bound.
Values may be sent and summed in bfloat16 or wider, within the bound.
No kernel may reach another device: no remote copies, remote signals or barrier semaphores. Data moves between devices by JAX's collectives and lax.ppermute only.
A program may use at most 192 MiB of HBM per device.

v0:
```python
import functools
import math

import jax
import jax.numpy as jnp
from jax import lax
from jax.experimental import pallas as pl
from jax.experimental.pallas import tpu as pltpu
from jax.sharding import PartitionSpec as P

D = 512
HEADS = 4
HD = 128
FF = 2048
K = 16
NS_STEPS = 4
HALO = 192
BLOCK = 128
SPAN = BLOCK + 2 * HALO
RIM = 256
CHUNK = 512
TABLE_ROWS = 16

f32 = jnp.float32
bf16 = jnp.bfloat16
ns_first = 3.4445
ns_second = -4.775
ns_third = 2.0315
momentum_rate = 0.95
vector_rate = 0.9
muon_rate = 0.2
decay_rate = 0.1
score_scale = 1.0 / math.sqrt(HD)
AXES = ("nodes", "hid")
VMEM = pl.BlockSpec(memory_space=pltpu.VMEM)
SMEM = pl.BlockSpec(memory_space=pltpu.SMEM)


def nn(a, b):
    return lax.dot_general(a, b, (((1,), (0,)), ((), ())), preferred_element_type=f32)


def nt(a, b):
    return lax.dot_general(a, b, (((1,), (1,)), ((), ())), preferred_element_type=f32)


def tn(a, b):
    return lax.dot_general(a, b, (((0,), (0,)), ((), ())), preferred_element_type=f32)


def struct(shape, dtype):
    return jax.ShapeDtypeStruct(shape, dtype)


def rows_of(start, size):
    return pl.ds(pl.multiple_of(start, size), size)


def cost(flops, data):
    return pl.CostEstimate(flops=int(flops), bytes_accessed=int(data), transcendentals=0)


def room(mebibytes):
    return pltpu.CompilerParams(vmem_limit_bytes=mebibytes << 20)


def norm_parts(field):
    average = jnp.mean(field, axis=-1, keepdims=True)
    centred = field - average
    variance = jnp.mean(centred * centred, axis=-1, keepdims=True)
    inverse = lax.rsqrt(variance + 1e-06)
    return centred * inverse, inverse


def table_rows(mod_ref, level, column):
    return jnp.where(level > 0.5, mod_ref[1, column : column + 1, :], mod_ref[0, column : column + 1, :])


def modulated(field, level, mod_ref, column):
    normed, _ = norm_parts(field)
    return normed * (1.0 + table_rows(mod_ref, level, column)) + table_rows(
        mod_ref, level, column + 1
    )


def norm_back(grad_out, field, level, mod_ref, column):
    normed, inverse = norm_parts(field)
    grad_norm = grad_out * (1.0 + table_rows(mod_ref, level, column))
    grad_in = inverse * (
        grad_norm
        - jnp.mean(grad_norm, axis=-1, keepdims=True)
        - normed * jnp.mean(grad_norm * normed, axis=-1, keepdims=True)
    )
    return grad_in, grad_out * normed


def add_table(table_ref, column, level, scale_term, shift_term):
    upper = level > 0.5
    for term, place in ((scale_term, column), (shift_term, column + 1)):
        low_part = jnp.sum(jnp.where(upper, 0.0, term), axis=0, keepdims=True)
        high_part = jnp.sum(jnp.where(upper, term, 0.0), axis=0, keepdims=True)
        table_ref[place : place + 1, :] += low_part
        table_ref[4 + place : 5 + place, :] += high_part


def slot_counts(pack, row_count, width, shift):
    pieces = []
    for left in range(0, width, 128):
        lanes = lax.broadcasted_iota(jnp.int32, (row_count, 128), 1)
        rows = lax.broadcasted_iota(jnp.int32, (row_count, 128), 0)
        place = (lanes - rows + (left - shift)).astype(f32)
        total = jnp.zeros((row_count, 128), f32)
        for slot in range(K):
            total = total + jnp.where(place == pack[:, slot : slot + 1], 1.0, 0.0)
        pieces.append(total)
    return jnp.concatenate(pieces, axis=1).astype(bf16)


def quarter_kernel(scalars, up, down, rounded):
    rounded[0] = up[...].astype(bf16)
    rounded[1] = down[...].astype(bf16)


def past_kernel(scalars, up, down, attention, large_past, small_past):
    large_past[...] = jnp.where(scalars[0] == 0, up[...], down[...].T)
    small_past[...] = attention[0]


def project_kernel(features, pack, mod, weights, first_in, qkv, counts, rounded):
    row_count = features.shape[0]
    turn = pl.program_id(0)

    @pl.when(turn == 0)
    def _():
        for start in range(0, row_count, 256):
            rows = slice(start, start + 256)
            level = pack[rows, K : K + 1]
            first_in[rows, :] = modulated(features[rows, :].astype(f32), level, mod, 0).astype(bf16)

    weight = weights[0].astype(bf16)
    rounded[0] = weight

    @pl.when(turn < 3)
    def _():
        qkv[turn] = nn(first_in[...], weight).astype(bf16)
        share = row_count // BLOCK // 3

        def count_step(b, carry):
            rows = rows_of(b * BLOCK, BLOCK)
            counts[rows, :] = slot_counts(pack[rows, :], BLOCK, SPAN, HALO)
            return carry

        lax.fori_loop(turn * share, (turn + 1) * share, count_step, 0)


def forward_kernel(
    rim_low,
    rim_high,
    features,
    pack,
    mod,
    weights,
    qkv,
    counts,
    attended,
    stream,
    second_in,
    padded,
    rim_queries,
    rim_counts,
    log_totals,
    rim_in,
):
    row_count = features.shape[0]
    for side, rim in enumerate((rim_low, rim_high)):

        def rim_step(b, carry):
            rows = rows_of(b * 64, 64)
            target = pl.ds(pl.multiple_of(side * HALO + b * 64, 64), 64)
            info = rim[rows, D:].astype(f32)
            rim_in[target, :] = modulated(
                rim[rows, :D].astype(f32), info[:, K : K + 1], mod, 0
            ).astype(bf16)
            rim_counts[target, :] = slot_counts(
                info, 64, RIM, b * 64 + (-HALO if side == 0 else RIM)
            )
            return carry

        lax.fori_loop(0, HALO // 64, rim_step, 0)
    rim_queries[...] = nn(rim_in[...], weights[0]).astype(bf16)
    for p in range(2):
        piece = nn(rim_in[...], weights[1 + p]).astype(bf16)
        padded[p, :HALO, :] = piece[:HALO]
        padded[p, HALO + row_count :, :] = piece[HALO:]
        padded[p, HALO : HALO + row_count, :] = qkv[1 + p]

    def step(b, carry):
        rows = rows_of(b * BLOCK, BLOCK)
        span = pl.ds(pl.multiple_of(b * BLOCK, BLOCK), SPAN)
        count = counts[rows, :].astype(f32)
        live = count > 0.0
        columns = [slice(h * HD, (h + 1) * HD) for h in range(HEADS)]
        scores = [nt(qkv[0, rows, cols], padded[0, span, cols]) * score_scale for cols in columns]
        lanes = lax.broadcasted_iota(jnp.int32, (BLOCK, 128), 1)
        stats = jnp.zeros((BLOCK, 128), f32)
        for h, cols in enumerate(columns):
            masked = jnp.where(live, scores[h], -1e30)
            peak = jnp.max(masked, axis=-1, keepdims=True)
            exponent = jnp.exp(masked - peak)
            total = jnp.sum(exponent * count, axis=-1, keepdims=True)
            probs = (exponent / total).astype(bf16)
            spread = (probs.astype(f32) * count).astype(bf16)
            attended[rows, cols] = nn(spread, padded[1, span, cols]).astype(bf16)
            stats = jnp.where(lanes == h, peak + jnp.log(total), stats)
        log_totals[rows, :] = stats
        return carry

    lax.fori_loop(0, row_count // BLOCK, step, 0)
    for start in range(0, row_count, 256):
        rows = slice(start, start + 256)
        field = features[rows, :].astype(f32) + nn(attended[rows, :], weights[3])
        stream[rows, :] = field
        second_in[rows, :] = modulated(field, pack[rows, K : K + 1], mod, 2).astype(bf16)


def mlp_chunk(
    scalars, second_in, cotangent, up, down, branch_in, grad_in, branch, grad_second, acts, grads, kept, sent
):
    row_count = second_in.shape[0]
    for start in range(0, row_count, 256):
        rows = slice(start, start + 256)
        preact = nn(second_in[rows, :], up)
        grad_act = nt(cotangent[rows, :], down)
        sigmoid = 0.5 * jnp.tanh(0.5 * preact) + 0.5
        act = (preact * sigmoid).astype(bf16)
        acts[rows, :] = act
        grad_pre = (grad_act * (sigmoid * (1.0 + preact * (1.0 - sigmoid)))).astype(bf16)
        grads[rows, :] = grad_pre
        branch[rows, :] = branch_in[rows, :] + nn(act, down)
        grad_second[rows, :] = grad_in[rows, :] + nt(grad_pre, up)
    first, z1, z2 = scalars[0] == 0, scalars[2], scalars[3]
    for out, swapped in ((kept, False), (sent, True)):
        ups = jnp.logical_not(first) if swapped else first
        product = tn(
            jnp.where(ups, second_in[...], cotangent[...]), jnp.where(ups, grads[...], acts[...])
        )
        for q in range(4):
            out[0, (q // 2) ^ z1, (q % 2) ^ z2] = product[q * 128 : (q + 1) * 128].astype(bf16)


def mlp_own_kernel(
    scalars, second_in, cotangent, up, down, branch, grad_second, kept, sent, acts, grads
):
    @pl.when(pl.program_id(0) == 0)
    def _():
        branch[...] = jnp.zeros_like(branch)
        grad_second[...] = jnp.zeros_like(grad_second)

    mlp_chunk(
        scalars,
        second_in,
        cotangent,
        up[...].astype(bf16),
        down[...].astype(bf16),
        branch,
        grad_second,
        branch,
        grad_second,
        acts,
        grads,
        kept,
        sent,
    )


def mlp_near_kernel(
    scalars, second_in, cotangent, near, branch_in, grad_in, branch, grad_second, kept, sent, acts, grads
):
    mlp_chunk(
        scalars,
        second_in,
        cotangent,
        near[0],
        near[1],
        branch_in,
        grad_in,
        branch,
        grad_second,
        acts,
        grads,
        kept,
        sent,
    )


def mlp_far_kernel(
    scalars,
    second_in,
    cotangent,
    far,
    branch_in,
    grad_in,
    stream,
    pack,
    mod,
    weights,
    attended,
    log_totals,
    kept_in,
    sent_in,
    kept,
    sent,
    output,
    grad_stream,
    grad_attended,
    stats,
    edge_low,
    edge_high,
    table,
    branch,
    grad_second,
    acts,
    grads,
):
    row_count = second_in.shape[0]
    mlp_chunk(
        scalars,
        second_in,
        cotangent,
        far[0],
        far[1],
        branch_in,
        grad_in,
        branch,
        grad_second,
        acts,
        grads,
        kept,
        sent,
    )
    table[...] = jnp.zeros_like(table)

    for start in range(0, row_count, 256):
        rows = slice(start, start + 256)
        field = stream[rows, :]
        level = pack[rows, K : K + 1]
        output[rows, :] = (field + branch[rows, :]).astype(bf16)
        gradient = grad_second[rows, :]
        grad_field, scale_term = norm_back(gradient, field, level, mod, 2)
        add_table(table, 2, level, scale_term, gradient)
        total = cotangent[rows, :].astype(f32) + grad_field
        grad_stream[rows, :] = total
        back = nt(total.astype(bf16), weights[3]).astype(bf16)
        grad_attended[rows, :] = back
        product = back.astype(f32) * attended[rows, :].astype(f32)
        lanes = lax.broadcasted_iota(jnp.int32, (256, 128), 1)
        kept_stats = log_totals[rows, :]
        for h in range(HEADS):
            delta = jnp.sum(product[:, h * HD : (h + 1) * HD], axis=-1, keepdims=True)
            kept_stats = jnp.where(lanes == HEADS + h, delta, kept_stats)
        stats[rows, :] = kept_stats
    for edge, first in ((edge_low, 0), (edge_high, row_count - HALO)):
        rows = slice(first, first + HALO)
        edge[:, :D] = grad_attended[rows, :]
        known = stats[rows, :]
        upper = known.astype(bf16)
        lower = (known - upper.astype(f32)).astype(bf16).astype(f32)
        edge[:, D:] = (upper.astype(f32) + pltpu.roll(lower, 2 * HEADS, 1)).astype(bf16)


def attention_terms(scores, grad_probs, count, log_total, delta):
    probs = jnp.exp(jnp.where(count > 0.0, scores * score_scale, -1e30) - log_total)
    slopes = (probs * (grad_probs - delta)).astype(bf16).astype(f32)
    spread = (probs.astype(bf16).astype(f32) * count).astype(bf16)
    return (slopes * count).astype(bf16), spread


def backward_kernel(qkv, padded, grad, stats, counts, token, grad_query, keys_total, values_total):
    keys_total[...] = jnp.zeros_like(keys_total)
    values_total[...] = jnp.zeros_like(values_total)

    def step(b, carry):
        rows = rows_of(b * BLOCK, BLOCK)
        span = pl.ds(pl.multiple_of(b * BLOCK, BLOCK), SPAN)
        count = counts[rows, :].astype(f32)
        columns = [slice(h * HD, (h + 1) * HD) for h in range(HEADS)]
        products = [
            (nt(qkv[0, rows, cols], padded[0, span, cols]), nt(grad[rows, cols], padded[1, span, cols]))
            for cols in columns
        ]
        terms = [
            attention_terms(
                *products[h],
                count,
                stats[rows, h : h + 1],
                stats[rows, HEADS + h : HEADS + h + 1],
            )
            for h in range(HEADS)
        ]
        for (slopes, spread), cols in zip(terms, columns):
            grad_query[rows, cols] = (nn(slopes, padded[0, span, cols]) * score_scale).astype(bf16)
            keys_total[span, cols] += tn(slopes, qkv[0, rows, cols])
            values_total[span, cols] += tn(spread, grad[rows, cols])
        return carry

    lax.fori_loop(0, counts.shape[0] // BLOCK, step, 0)


def weights_kernel(
    scalars,
    token,
    queries_in,
    keys_in,
    values_in,
    padded,
    rim_query,
    rim_counts,
    grad_low,
    grad_high,
    first_in,
    attended,
    grad_stream,
    features,
    pack,
    mod,
    weights,
    table_two,
    features_grad,
    kept,
    sent,
    gathered,
    table,
    keys_total,
    values_total,
    blocks,
):
    row_count = first_in.shape[0]
    columns = [slice(h * HD, (h + 1) * HD) for h in range(HEADS)]
    own = slice(HALO, HALO + row_count)
    keys_total[...] = keys_in[own, :]
    values_total[...] = values_in[own, :]
    for side, grads in enumerate((grad_low, grad_high)):
        first = 0 if side == 0 else row_count - RIM
        own_span = slice(first, first + RIM)
        span = slice(HALO + first, HALO + first + RIM)
        rows = slice(side * HALO, (side + 1) * HALO)
        known = grads[:, D:].astype(f32)
        count = rim_counts[rows, :].astype(f32)
        products = [
            (nt(rim_query[rows, cols], padded[0, span, cols]), nt(grads[:, cols], padded[1, span, cols]))
            for cols in columns
        ]
        terms = []
        for h in range(HEADS):
            numbers = [known[:, i * HEADS + h : i * HEADS + h + 1] for i in range(4)]
            terms.append(
                attention_terms(*products[h], count, numbers[0] + numbers[2], numbers[1] + numbers[3])
            )
        for (slopes, spread), cols in zip(terms, columns):
            keys_total[own_span, cols] += tn(slopes, rim_query[rows, cols])
            values_total[own_span, cols] += tn(spread, grads[:, cols])
    gathered[0] = queries_in[...]
    gathered[1] = (keys_total[...] * score_scale).astype(bf16)
    gathered[2] = values_total[...].astype(bf16)
    table[...] = table_two[...]
    for start in range(0, row_count, 256):
        rows = slice(start, start + 256)
        level = pack[rows, K : K + 1]
        gradient = nt(gathered[0, rows, :], weights[0])
        for p in range(1, 3):
            gradient = gradient + nt(gathered[p, rows, :], weights[p])
        grad_field, scale_term = norm_back(gradient, features[rows, :].astype(f32), level, mod, 0)
        add_table(table, 0, level, scale_term, gradient)
        total = grad_stream[rows, :]
        features_grad[rows, :] = total + grad_field
        gathered[3, rows, :] = total.astype(bf16)
    core, slot_bit, z1, z2, hid = (scalars[i] for i in range(5))

    def product_step(n, carry):
        away, slot = n // 2, n % 2
        target = core ^ away
        p = 2 * target + slot
        product = tn(jnp.where(p < 3, first_in[...], attended[...]), gathered[p])
        for half in range(2):
            for q in range(4):
                slot_at, hid_at, row_half = slot ^ slot_bit, half ^ hid, (q // 2) ^ z1
                index = (
                    away,
                    jnp.where(target == 0, hid_at, slot_at),
                    jnp.where(target == 0, slot_at, row_half),
                    jnp.where(target == 0, row_half, hid_at),
                    (q % 2) ^ z2,
                )
                start = half * 256 + q * 64
                blocks[index + (slice(0, 64),)] = product[start : start + 64].astype(bf16)
                row = (q // 2) * 4 + 2 * half + q % 2
                known = jnp.broadcast_to(table[row : row + 1, :], (TABLE_ROWS, D))
                blocks[index + (slice(64, 80),)] = jnp.where(p == 0, known, 0.0).astype(bf16)
        return carry

    lax.fori_loop(0, 4, product_step, 0)
    kept[...] = blocks[0]
    sent[...] = blocks[1]


def large_sum_kernel(scalars, own, own_got, rest, rest_got, keep, send):
    first = scalars[0] == 0
    for away, out in ((0, keep), (1, send)):
        for source, got, h in ((own, own_got, 0), (rest, rest_got, 1)):
            for i in range(2):
                where_from = (jnp.where(first, away, i), jnp.where(first, i, away))
                where_to = (jnp.where(first, h, i), jnp.where(first, i, h))
                total = source[where_from].astype(f32) + got[where_from].astype(f32)
                out[where_to] = total.astype(out.dtype)


def receive_kernel(*refs):
    kept, got, keep, send = refs[0], refs[1], refs[-2], refs[-1]
    keep[...] = kept[0].astype(f32) + got[0].astype(f32)
    send[...] = (kept[1].astype(f32) + got[1].astype(f32)).astype(bf16)


def blend_kernel(*refs):
    kept, got, past, part = refs[0], refs[1], refs[2], refs[-1]
    rows = past.shape[0]
    total = kept[...] + got[...].astype(f32)
    blended = (1.0 + momentum_rate) * total[:rows] + momentum_rate * momentum_rate * past[...]
    part[:rows, :] = blended.astype(bf16)
    if rows < part.shape[0]:
        part[rows:, :] = total[rows:].astype(bf16)


def join_kernel(*refs):
    part, got, pieces = refs[0], refs[1], refs[-1]
    pieces[0] = part[...]
    pieces[1] = got[...]


def newton_schulz(groups, polys, rows_first, scales):
    blocks = [[[ref[i] for i in half] for half in halves] for ref, halves in groups]
    grams = []
    for halves, scale in zip(blocks, scales):
        sums = []
        for half in halves:
            total = None
            for block in half:
                term = tn(block, block) if rows_first else nt(block, block)
                total = term if total is None else total + term
            sums.append((total if scale is None else total * (scale * scale)).astype(bf16))
        grams.append((sums[0].astype(f32) + sums[1].astype(f32)).astype(bf16))
    for gram, poly in zip(grams, polys):
        poly[...] = (ns_second * gram.astype(f32) + ns_third * nn(gram, gram)).astype(bf16)
    for (ref, halves), values, poly, scale in zip(groups, blocks, polys, scales):
        for half, half_values in zip(halves, values):
            for i, block in zip(half, half_values):
                other = nn(block, poly[...]) if rows_first else nn(poly[...], block)
                total = ns_first * block.astype(f32) + other
                ref[i] = (total if scale is None else total * scale).astype(bf16)


def large_start_kernel(scalars, kept, got, work, poly):
    core, slot_bit, z1, z2 = (scalars[i] for i in range(4))
    total = jnp.zeros((8, D), f32)
    for n in range(16):
        b1, b2, b3, b4 = n // 8, (n // 4) % 2, (n // 2) % 2, n % 2
        source = kept if b1 == 0 else got
        block = source[b2, b3, b4]
        value = block.astype(f32)
        total = total + jnp.sum((value * value).reshape(16, 8, D), axis=0)
        slot = jnp.where(core == 0, b1, b2)
        half = jnp.where(core == 0, b2, b3)
        row_half = jnp.where(core == 0, b3, b1)
        start = ((row_half ^ z1) * 2 + (b4 ^ z2)) * 128
        work[half * 2 + (slot ^ slot_bit), rows_of(start, 128), :] = block
    return 1.0 / (jnp.sqrt(jnp.sum(total)) + 1e-07)


large_halves = ((0, 1), (2, 3))


def large_first_kernel(scalars, kept, got, token, work, blend, poly):
    scale = large_start_kernel(scalars, kept, got, work, poly)
    for s in range(2):
        blend[s] = work[s]

    def step(i, factor):
        newton_schulz([(work, large_halves)], [poly], False, [factor])
        return jnp.ones((), f32)

    lax.fori_loop(0, NS_STEPS // 2, step, scale)


def large_next_kernel(given, token, result, work, poly):
    work[...] = given[...]

    def step(i, carry):
        newton_schulz([(work, large_halves)], [poly], False, [None])
        return carry

    lax.fori_loop(NS_STEPS // 2, NS_STEPS, step, 0)
    for s in range(2):
        result[s] = work[s]


def small_start_kernel(scalars, kept, got, token, work, blend, table):
    core, slot_bit, z1, z2 = (scalars[i] for i in range(4))
    for n in range(16):
        b1, b2, b3, b4 = n // 8, (n // 4) % 2, (n // 2) % 2, n % 2
        source = kept if b1 == 0 else got
        block = source[b2, b3, b4]
        slot = jnp.where(core == 0, b2, b1) ^ slot_bit
        half = jnp.where(core == 0, b1, b3)
        row_half = jnp.where(core == 0, b3, b2)
        quarter = (row_half ^ z1) * 2 + (b4 ^ z2)
        work[slot, half, rows_of(quarter * 64, 64), :] = block[:64]

        @pl.when((half == 0) & (slot == 0))
        def _():
            table[pl.ds(quarter, 1), :] = block[64:].astype(f32)[:1]

    table[4:, :] = jnp.zeros((4, D), f32)
    for s in range(2):
        blend[s] = work[s, 0]


def small_kernel(given, result, first, second, poly_first, poly_second):
    works = (first, second)
    scales = []
    for s, work in enumerate(works):
        total = jnp.zeros((8, D), f32)
        for half in range(2):
            block = given[s, half]
            work[half] = block
            value = block.astype(f32)
            total = total + jnp.sum((value * value).reshape(32, 8, D), axis=0)
        scales.append(1.0 / (jnp.sqrt(jnp.sum(total)) + 1e-07))
    groups = [(work, ((0,), (1,))) for work in works]
    polys = [poly_first, poly_second]

    def step(i, factors):
        newton_schulz(groups, polys, True, factors)
        return (jnp.ones((), f32),) * 2

    lax.fori_loop(0, NS_STEPS, step, tuple(scales))
    for s, work in enumerate(works):
        result[s] = work[0]


def new_moment(blend, moment):
    share = 1.0 / (1.0 + momentum_rate)
    return share * blend + (momentum_rate - share * momentum_rate * momentum_rate) * moment


def new_weight(weight, ortho, longest):
    return weight - muon_rate * (0.2 * math.sqrt(longest) * ortho + decay_rate * weight)


def large_moment_kernel(scalars, own, got, up_moment, down_moment, token, up_moment_new, down_moment_new, done):
    done[...] = jnp.zeros_like(done)
    first = scalars[0] == 0
    mine, other = own[0].astype(f32), got[0].astype(f32)
    up_moment_new[...] = new_moment(jnp.where(first, mine, other), up_moment[...])
    down_moment_new[...] = new_moment(jnp.where(first, other, mine).T, down_moment[...])


def large_weight_kernel(
    scalars,
    own,
    got,
    up_weight,
    down_weight,
    mix,
    mix_got,
    moment,
    table,
    table_got,
    modulation,
    held_moment,
    token,
    up_new,
    down_new,
    moment_new,
    held_moment_new,
    held_new,
    done,
    *,
    nodes,
):
    done[...] = jnp.zeros_like(done)
    core, turn = scalars[0], pl.program_id(0)
    first = core == 0
    mine, other = own[0].astype(f32), got[0].astype(f32)
    up_new[...] = new_weight(up_weight[...], jnp.where(first, mine, other), FF)
    down_new[...] = new_weight(down_weight[...], jnp.where(first, other, mine).T, FF)
    blend = jnp.where(core == turn // 2, mix[0].astype(f32), mix_got[0].astype(f32))
    moment_new[0] = new_moment(blend, moment[0])

    @pl.when(turn == 0)
    def _():
        total = jnp.where(first, table[...], table_got[...])
        for level in range(2):
            for column in range(2):
                row = level * 2 + column
                at = (slice(level, level + 1), slice(column, column + 1))
                value = vector_rate * held_moment[at] + total[row : row + 1, :].reshape(1, 1, D)
                held = modulation[level : level + 1, pl.ds(scalars[4] * 2 + column, 1)]
                held_moment_new[at] = value
                held_new[at] = held - 0.2 / math.sqrt(nodes) * value


def small_weight_kernel(scalars, own, got, weight, token, weight_new):
    mine = scalars[0] == pl.program_id(0) // 2
    ortho = jnp.where(mine, own[0].astype(f32), got[0].astype(f32))
    weight_new[0] = new_weight(weight[0], ortho, D)


def on_device(
    features,
    levels,
    neighbour_index,
    neighbour_count,
    cotangent,
    attention_weight,
    up_weight,
    down_weight,
    modulation,
    attention_moment,
    up_moment,
    down_moment,
    modulation_moment,
):
    row_count = features.shape[0]
    device_count = lax.axis_size(AXES)
    me = lax.axis_index(AXES)
    first_row = me * row_count

    def bit(place):
        return (me >> place) & 1

    hid, core, slot_bit, z1, z2 = (bit(place) for place in range(5))
    scalars = jnp.stack([core, slot_bit, z1, z2, hid]).astype(jnp.int32)
    is_first = core == 0

    def along(value, distance):
        pairs = [(i, i + distance) for i in range(device_count) if 0 <= i + distance < device_count]
        return lax.ppermute(value, AXES, pairs)

    def after(value, *others):
        return lax.optimization_barrier((value,) + others)[0]

    def swap(value, mask, other=None):
        masks = (mask, mask if other is None else other)
        pairs = [(i, i ^ masks[(i // 2) % 2]) for i in range(device_count)]
        return lax.ppermute(value, AXES, pairs)

    live = jnp.arange(K, dtype=jnp.int32)[None, :] < neighbour_count[:, None]
    row_ids = first_row + jnp.arange(row_count, dtype=jnp.int32)[:, None]
    offsets = jnp.where(live, neighbour_index - row_ids, 512)
    pack = jnp.concatenate(
        [offsets, levels[:, None], jnp.zeros((row_count, 128 - K - 1), jnp.int32)], axis=1
    ).astype(f32)
    rims = jnp.concatenate([features, pack.astype(bf16)], axis=1)
    rim_low = along(rims[row_count - HALO :], 1)
    rim_high = along(rims[:HALO], -1)

    pack, scalars, is_first = lax.optimization_barrier((pack, scalars, is_first))
    mod = modulation

    def past_row(s):
        return s[2] * 2 + s[3]

    quarter = pl.pallas_call(
        quarter_kernel,
        grid_spec=pltpu.PrefetchScalarGridSpec(
            num_scalar_prefetch=1,
            grid=(1,),
            in_specs=[
                pl.BlockSpec((D, CHUNK), lambda g, s: (0, s[0])),
                pl.BlockSpec((CHUNK, D), lambda g, s: (s[0], 0)),
            ],
            out_specs=pl.BlockSpec((2, D, CHUNK), lambda g, s: (0, 0, 0)),
        ),
        out_shape=struct((2, D, CHUNK), bf16),
        cost_estimate=cost(1e6, 3e6),
        name="quarter",
        compiler_params=room(8),
    )(scalars, up_weight, down_weight)
    large_past, small_past = pl.pallas_call(
        past_kernel,
        grid_spec=pltpu.PrefetchScalarGridSpec(
            num_scalar_prefetch=1,
            grid=(1,),
            in_specs=[
                pl.BlockSpec((128, CHUNK), lambda g, s: (past_row(s), s[1])),
                pl.BlockSpec((CHUNK, 128), lambda g, s: (s[1], past_row(s))),
                pl.BlockSpec((1, 64, D), lambda g, s: (s[0] * 2 + s[1], past_row(s), 0)),
            ],
            out_specs=(
                pl.BlockSpec((128, CHUNK), lambda g, s: (0, 0)),
                pl.BlockSpec((64, D), lambda g, s: (0, 0)),
            ),
        ),
        out_shape=(struct((128, CHUNK), f32), struct((64, D), f32)),
        cost_estimate=cost(1e6, 1e6),
        name="past",
        compiler_params=room(4),
    )(scalars, up_moment, down_moment, attention_moment)
    first_in, qkv, counts, attn_bf = pl.pallas_call(
        project_kernel,
        grid=(4,),
        out_shape=(
            struct((row_count, D), bf16),
            struct((3, row_count, D), bf16),
            struct((row_count, SPAN), bf16),
            struct((4, D, D), bf16),
        ),
        in_specs=[
            pl.BlockSpec((row_count, D), lambda g: (0, 0)),
            pl.BlockSpec((row_count, 128), lambda g: (0, 0)),
            pl.BlockSpec((2, 4, D), lambda g: (0, 0, 0)),
            pl.BlockSpec((1, D, D), lambda g: (g, 0, 0)),
        ],
        out_specs=(
            pl.BlockSpec((row_count, D), lambda g: (0, 0)),
            pl.BlockSpec((3, row_count, D), lambda g: (0, 0, 0)),
            pl.BlockSpec((row_count, SPAN), lambda g: (0, 0)),
            pl.BlockSpec((1, D, D), lambda g: (g, 0, 0)),
        ),
        cost_estimate=cost(4e9, 4e6),
        name="project",
        compiler_params=room(10),
    )(features, pack, mod, attention_weight)

    near = swap(after(quarter, rim_low, rim_high, large_past), 1)

    attended, stream, second_in, padded, rim_queries, rim_counts, log_totals = pl.pallas_call(
        forward_kernel,
        out_shape=(
            struct((row_count, D), bf16),
            struct((row_count, D), f32),
            struct((row_count, D), bf16),
            struct((2, row_count + 2 * HALO, D), bf16),
            struct((2 * HALO, D), bf16),
            struct((2 * HALO, RIM), bf16),
            struct((row_count, 128), f32),
        ),
        in_specs=[VMEM] * 8,
        out_specs=(VMEM,) * 7,
        scratch_shapes=[pltpu.VMEM((2 * HALO, D), bf16)],
        cost_estimate=cost(6e9, 8e6),
        name="attend",
        compiler_params=room(12),
    )(rim_low, rim_high, features, pack, mod, attn_bf, qkv, counts)

    def whole(*shape):
        return pl.BlockSpec(shape, lambda g, s: (0,) * len(shape))

    chunk_shape = struct((2, 2, 2, 128, CHUNK), bf16)
    branch, grad_second, own_kept, own_sent = pl.pallas_call(
        mlp_own_kernel,
        out_shape=(struct((row_count, D), f32), struct((row_count, D), f32), chunk_shape, chunk_shape),
        grid_spec=pltpu.PrefetchScalarGridSpec(
            num_scalar_prefetch=1,
            grid=(2,),
            in_specs=[
                whole(row_count, D),
                whole(row_count, D),
                pl.BlockSpec((D, CHUNK), lambda g, s: (0, g)),
                pl.BlockSpec((CHUNK, D), lambda g, s: (g, 0)),
            ],
            out_specs=(
                whole(row_count, D),
                whole(row_count, D),
                pl.BlockSpec((1, 2, 2, 128, CHUNK), lambda g, s: (g ^ s[1], 0, 0, 0, 0)),
                pl.BlockSpec((1, 2, 2, 128, CHUNK), lambda g, s: (g ^ s[1], 0, 0, 0, 0)),
            ),
            scratch_shapes=[pltpu.VMEM((row_count, CHUNK), bf16)] * 2,
        ),
        cost_estimate=cost(5e9, 8e6),
        name="mlp_own",
        compiler_params=room(14),
    )(scalars, second_in, cotangent, up_weight, down_weight)

    def part(away):
        return pl.BlockSpec(
            (1, 2, 2, 128, CHUNK), lambda g, s: (away ^ s[0] ^ s[1], 0, 0, 0, 0)
        )

    branch, grad_second, near_kept, near_sent = pl.pallas_call(
        mlp_near_kernel,
        out_shape=(struct((row_count, D), f32), struct((row_count, D), f32), chunk_shape, chunk_shape),
        grid_spec=pltpu.PrefetchScalarGridSpec(
            num_scalar_prefetch=1,
            grid=(1,),
            in_specs=[
                whole(row_count, D),
                whole(row_count, D),
                whole(2, D, CHUNK),
                whole(row_count, D),
                whole(row_count, D),
            ],
            out_specs=(whole(row_count, D), whole(row_count, D), part(0), part(0)),
            scratch_shapes=[pltpu.VMEM((row_count, CHUNK), bf16)] * 2,
        ),
        cost_estimate=cost(2.5e9, 4e6),
        name="mlp_near",
        compiler_params=room(10),
    )(scalars, second_in, cotangent, near, branch, grad_second)
    far = swap(after(near, own_kept), 2)
    (
        rest_kept,
        rest_sent,
        output,
        grad_stream,
        grad_attended,
        stats,
        edge_low,
        edge_high,
        table_two,
    ) = pl.pallas_call(
        mlp_far_kernel,
        out_shape=(
            chunk_shape,
            chunk_shape,
            struct((row_count, D), bf16),
            struct((row_count, D), f32),
            struct((row_count, D), bf16),
            struct((row_count, 128), f32),
            struct((HALO, D + 128), bf16),
            struct((HALO, D + 128), bf16),
            struct((8, D), f32),
        ),
        grid_spec=pltpu.PrefetchScalarGridSpec(
            num_scalar_prefetch=1,
            grid=(1,),
            in_specs=[
                whole(row_count, D),
                whole(row_count, D),
                whole(2, D, CHUNK),
                whole(row_count, D),
                whole(row_count, D),
                whole(row_count, D),
                whole(row_count, 128),
                whole(2, 4, D),
                whole(4, D, D),
                whole(row_count, D),
                whole(row_count, 128),
                pl.BlockSpec(memory_space=pl.ANY),
                pl.BlockSpec(memory_space=pl.ANY),
            ],
            out_specs=(
                part(1),
                part(1),
                whole(row_count, D),
                whole(row_count, D),
                whole(row_count, D),
                whole(row_count, 128),
                whole(HALO, D + 128),
                whole(HALO, D + 128),
                whole(8, D),
            ),
            scratch_shapes=[
                pltpu.VMEM((row_count, D), f32),
                pltpu.VMEM((row_count, D), f32),
                pltpu.VMEM((row_count, CHUNK), bf16),
                pltpu.VMEM((row_count, CHUNK), bf16),
            ],
        ),
        input_output_aliases={12: 0, 13: 1},
        cost_estimate=cost(4e9, 8e6),
        name="mlp_far",
        compiler_params=room(16),
    )(
        scalars,
        second_in,
        cotangent,
        far,
        branch,
        grad_second,
        stream,
        pack,
        mod,
        attn_bf,
        attended,
        log_totals,
        near_kept,
        near_sent,
    )

    grad_low = along(edge_high, 1)
    grad_high = along(edge_low, -1)

    large_shape = (2, 2, 2, 128, CHUNK)
    large_keep, large_send = pl.pallas_call(
        large_sum_kernel,
        out_shape=(struct(large_shape, f32), struct(large_shape, bf16)),
        in_specs=[SMEM] + [VMEM] * 4,
        out_specs=(VMEM,) * 2,
        cost_estimate=cost(1e3, 1e3),
        name="large_sum",
        compiler_params=room(12),
    )(scalars, own_kept, swap(own_sent, 2), rest_kept, swap(rest_sent, 2))

    def ordered(kernel, values, tokens, shapes, name):
        return pl.pallas_call(
            kernel,
            out_shape=shapes,
            in_specs=[VMEM] * len(values) + [pl.BlockSpec(memory_space=pl.ANY)] * len(tokens),
            out_specs=jax.tree.map(lambda _: VMEM, shapes),
            cost_estimate=cost(3e10, 1e3),
            name=name,
            compiler_params=room(8),
        )(*values, *tokens)

    def receive(keep, got, *tokens):
        rows = math.prod(keep.shape[1:-1])
        flat = (2, rows, D)
        keep, send = ordered(
            receive_kernel,
            (keep.reshape(flat), got.reshape(flat)),
            tokens,
            (struct((rows, D), f32), struct((rows, D), bf16)),
            "receive",
        )
        half = (2, rows // 2, D) if rows > 128 else (rows, D)
        return keep.reshape(half), send.reshape(half)

    def blend(keep, got, past, *tokens):
        mask = 32
        if mask < device_count:
            keep = keep + got.astype(f32)
            while mask < device_count:
                rounded = keep.astype(bf16)
                keep, got = rounded.astype(f32), swap(rounded, mask)
                mask *= 2
                if mask < device_count:
                    keep = keep + got.astype(f32)
        return ordered(blend_kernel, (keep, got, past), tokens, struct(keep.shape, bf16), "blend")

    def join(part, got, *tokens):
        rows = math.prod(part.shape[:-1])
        return ordered(
            join_kernel,
            (part.reshape(rows, D), got.reshape(rows, D)),
            tokens,
            struct((2, rows, D), bf16),
            "join",
        ).reshape(2 * rows, D)

    large_routes = ((4, 8), (1, 4), (8, 1), (16, 16))
    small_routes = ((1, 4), (4, 8), (8, 1), (16, 16))

    padded_rows = row_count + 2 * HALO
    large_got = swap(large_send, *large_routes[0])
    grad_queries, keys_total, values_total = pl.pallas_call(
        backward_kernel,
        out_shape=(struct((row_count, D), bf16),) + (struct((padded_rows, D), f32),) * 2,
        in_specs=[VMEM] * 5 + [pl.BlockSpec(memory_space=pl.ANY)],
        out_specs=(VMEM,) * 3,
        cost_estimate=cost(8e9, 9e6),
        name="attend_back",
        compiler_params=room(10),
    )(qkv, padded, grad_attended, stats, counts, large_send)
    large_keep, large_send = receive(large_keep, large_got, grad_queries)
    large_got = swap(large_send, *large_routes[1])
    piece_shape = struct((2, 2, 2, 2, 80, D), bf16)
    features_grad, small_kept, small_sent = pl.pallas_call(
        weights_kernel,
        out_shape=(struct((row_count, D), f32), piece_shape, piece_shape),
        in_specs=[SMEM, pl.BlockSpec(memory_space=pl.ANY)] + [VMEM] * 16,
        out_specs=(VMEM,) * 3,
        scratch_shapes=[
            pltpu.VMEM((4, row_count, D), bf16),
            pltpu.VMEM((8, D), f32),
            pltpu.VMEM((row_count, D), f32),
            pltpu.VMEM((row_count, D), f32),
            pltpu.VMEM((2, 2, 2, 2, 2, 80, D), bf16),
        ],
        cost_estimate=cost(6e9, 9e6),
        name="attend_weights",
        compiler_params=room(16),
    )(
        scalars,
        large_send,
        grad_queries,
        keys_total,
        values_total,
        padded,
        rim_queries,
        rim_counts,
        grad_low,
        grad_high,
        first_in,
        attended,
        grad_stream,
        features,
        pack,
        mod,
        attn_bf,
        table_two,
    )
    def chain_large(step, *tokens):
        nonlocal large_keep, large_send, large_got
        large_keep, large_send = receive(large_keep, large_got, *tokens)
        large_got = swap(large_send, *large_routes[step])

    def chain_small(step, *tokens):
        nonlocal small_keep, small_send, small_got
        small_keep, small_send = receive(small_keep, small_got, *tokens)
        small_got = swap(small_send, *small_routes[step])

    small_keep, small_send = small_kept, small_sent
    small_got = swap(small_send, 2)
    chain_large(2, small_sent)
    chain_small(0, large_send)
    chain_large(3, small_send)
    chain_small(1, large_send)
    large_part = blend(large_keep, large_got, large_past, small_send)
    large_got = swap(large_part, *large_routes[3])
    chain_small(2, large_part)
    large_part = join(large_part, large_got, small_send)
    large_got = swap(large_part, *large_routes[2])
    chain_small(3, large_part)
    large_part = join(large_part, large_got, small_send)
    large_got = swap(large_part, *large_routes[1])
    small_part = blend(small_keep, small_got, small_past, large_part)
    small_got = swap(small_part, *small_routes[3])
    small_part = join(small_part, small_got, large_part)
    small_got = swap(small_part, *small_routes[2])
    large_part = join(large_part, large_got, small_part)
    large_got = swap(large_part, *large_routes[0])
    small_part = join(small_part, small_got, large_part)
    small_got = swap(small_part, *small_routes[1])

    any_space = pl.BlockSpec(memory_space=pl.ANY)
    gathered_shape = (2, 2, 2, 128, CHUNK)
    large_work, large_mix = pl.pallas_call(
        large_first_kernel,
        out_shape=(struct((4, D, CHUNK), bf16), struct((2, D, CHUNK), bf16)),
        in_specs=[SMEM, VMEM, VMEM, any_space],
        out_specs=(VMEM,) * 2,
        scratch_shapes=[pltpu.VMEM((D, D), bf16)],
        cost_estimate=cost(5e9, 6e6),
        name="ortho_large",
        compiler_params=room(10),
    )(scalars, large_part.reshape(gathered_shape), large_got.reshape(gathered_shape), small_part)
    small_part = join(small_part, small_got, large_work)
    small_got = swap(small_part, *small_routes[0])
    mix_got = swap(large_mix, 2)
    large_result = pl.pallas_call(
        large_next_kernel,
        out_shape=struct((2, D, CHUNK), bf16),
        in_specs=[VMEM, any_space],
        out_specs=VMEM,
        scratch_shapes=[pltpu.VMEM((4, D, CHUNK), bf16), pltpu.VMEM((D, D), bf16)],
        cost_estimate=cost(5e9, 4e6),
        name="ortho_large",
        compiler_params=room(10),
    )(large_work, small_part)
    result_got = swap(large_result, 2)

    across = pl.BlockSpec((1, D, 256), lambda g: (g // 2, 0, g % 2))
    left_right = pl.BlockSpec((D, 256), lambda g: (0, g))
    top_bottom = pl.BlockSpec((256, D), lambda g: (g, 0))
    large_shapes = (struct((D, 2 * CHUNK), f32), struct((2 * CHUNK, D), f32))
    small_token = struct((8, 128), f32)
    token_block = pl.BlockSpec((8, 128), lambda g: (0, 0))
    up_moment_new, down_moment_new, moments_done = pl.pallas_call(
        large_moment_kernel,
        grid=(4,),
        out_shape=large_shapes + (small_token,),
        in_specs=[SMEM, across, across, left_right, top_bottom, any_space],
        out_specs=(left_right, top_bottom, token_block),
        cost_estimate=cost(1e7, 1e7),
        name="moment_large",
        compiler_params=room(8),
    )(scalars, large_mix, mix_got, up_moment, down_moment, large_result)
    small_work, small_mix, table_own = pl.pallas_call(
        small_start_kernel,
        out_shape=(
            struct((2, 2, 256, D), bf16),
            struct((2, 256, D), bf16),
            struct((8, D), f32),
        ),
        in_specs=[SMEM, VMEM, VMEM, any_space],
        out_specs=(VMEM,) * 3,
        cost_estimate=cost(1e6, 4e6),
        name="unpack_small",
        compiler_params=room(6),
    )(
        scalars,
        small_part.reshape(2, 2, 2, 80, D),
        small_got.reshape(2, 2, 2, 80, D),
        moments_done,
    )
    small_result = pl.pallas_call(
        small_kernel,
        out_shape=struct((2, 256, D), bf16),
        in_specs=[VMEM],
        out_specs=VMEM,
        scratch_shapes=[pltpu.VMEM((2, 256, D), bf16)] * 2 + [pltpu.VMEM((D, D), bf16)] * 2,
        cost_estimate=cost(6e9, 4e6),
        name="ortho_small",
        compiler_params=room(10),
    )(small_work)
    small_other = swap(small_result, 2)
    mix_other = swap(small_mix, 2)
    table_other = swap(table_own, 2)

    def fixed(*shape):
        return pl.BlockSpec(shape, lambda g: (0,) * len(shape))

    def one(index):
        return pl.BlockSpec((1, 256, D), index)

    up_new, down_new, attention_moment_new, modulation_moment_new, modulation_new, large_done = pl.pallas_call(
        functools.partial(large_weight_kernel, nodes=row_count * device_count),
        grid=(4,),
        out_shape=large_shapes + (struct((4, 256, D), f32),) + (struct((2, 2, D), f32),) * 2 + (small_token,),
        in_specs=[
            SMEM,
            across,
            across,
            left_right,
            top_bottom,
            one(lambda g: (g % 2, 0, 0)),
            one(lambda g: (g % 2, 0, 0)),
            one(lambda g: (g, 0, 0)),
            fixed(8, D),
            fixed(8, D),
            fixed(2, 4, D),
            fixed(2, 2, D),
            any_space,
        ],
        out_specs=(left_right, top_bottom, one(lambda g: (g, 0, 0)), fixed(2, 2, D), fixed(2, 2, D), token_block),
        cost_estimate=cost(1e7, 2e7),
        name="update_large",
        compiler_params=room(12),
    )(
        scalars,
        large_result,
        result_got,
        up_weight,
        down_weight,
        small_mix,
        mix_other,
        attention_moment,
        table_own,
        table_other,
        modulation,
        modulation_moment,
        small_result,
    )
    attention_new = pl.pallas_call(
        small_weight_kernel,
        grid_spec=pltpu.PrefetchScalarGridSpec(
            num_scalar_prefetch=1,
            grid=(4,),
            in_specs=[
                pl.BlockSpec((1, 256, D), lambda g, s: (g % 2, 0, 0)),
                pl.BlockSpec((1, 256, D), lambda g, s: (g % 2, 0, 0)),
                pl.BlockSpec((1, 256, D), lambda g, s: (g, s[4], 0)),
                any_space,
            ],
            out_specs=pl.BlockSpec((1, 256, D), lambda g, s: (g, 0, 0)),
        ),
        out_shape=struct((4, 256, D), f32),
        cost_estimate=cost(1e7, 6e6),
        name="update_small",
        compiler_params=room(6),
    )(scalars, small_result, small_other, attention_weight, large_done)
    return (
        output,
        features_grad,
        attention_moment_new,
        attention_new,
        up_moment_new,
        up_new,
        down_moment_new,
        down_new,
        modulation_moment_new,
        modulation_new,
    )


def solution(mesh):
    placed = (
        P(("nodes", "hid"), None),
        P(("nodes", "hid")),
        P(("nodes", "hid"), None),
        P(("nodes", "hid")),
        P(("nodes", "hid"), None),
        P(),
        P(None, "hid"),
        P("hid", None),
        P(),
        P(None, "hid", None),
        P(None, "hid"),
        P("hid", None),
        P(None, "hid", None),
    )
    return jax.shard_map(
        on_device,
        mesh=mesh,
        in_specs=placed,
        out_specs=(
            P(("nodes", "hid"), None),
            P(("nodes", "hid"), None),
            P(None, "hid", None),
            P(None, "hid", None),
            P(None, "hid"),
            P(None, "hid"),
            P("hid", None),
            P("hid", None),
            P(None, "hid", None),
            P(None, "hid", None),
        ),
        check_vma=False,
    )
```

profile of v0, /device:TPU:0, one launch (start us, length us, event | category | flops | bytes accessed | tf_op | source)
XLA Modules:
  0.0 184.9 jit_solution(16812089775078407385)
XLA Ops:
  0.7 0.9 broadcast_subtract_fusion
  1.8 0.8 broadcast_in_dim.16
  2.6 0.9 fusion
  3.7 0.8 pad_maximum_fusion
  4.5 1.3 collective-permute-start.1
  5.8 6.2 %collective-permute-start = (bf16[192,640]{1,0:T(8,128)(2,1)}, bf16[192,640]{1,0:T(8,128)(2,1)}, u32[]{:S(2)}, u32[]{:S(2)}) collective-permute-start(bf16[192,640]{1,0:T(8,128)(2,1)} %get-tuple-element.153), channel_id=1, source_target_pairs={{0,1},{1,2},{2,3},{3,4},{4,5},{5,6},{6,7},{7,8},{8,9},{9,10},{10,1... | collective-permute-start | bytes 737288 | tf_op jit(solution)/shard_map/ppermute | solution.py:746
  12.1 1.6 copy-done.5
  13.7 1.6 copy-done.8
  15.3 0.6 quarter.1
  15.9 0.9 copy-done
  16.9 0.6 copy-done.2
  17.5 0.7 past.1
  18.2 1.9 %collective-permute-done.rim_low = bf16[192,640]{1,0:T(8,128)(2,1)} collective-permute-done((bf16[192,640]{1,0:T(8,128)(2,1)}, bf16[192,640]{1,0:T(8,128)(2,1)}, u32[]{:S(2)}, u32[]{:S(2)}) %collective-permute-start) | collective-permute-done | bytes 245792 | tf_op jit(solution)/shard_map/ppermute | solution.py:746
  20.0 2.5 %collective-permute-start.2 = (bf16[2,512,512]{2,1,0:T(8,128)(2,1)S(1)}, bf16[2,512,512]{2,1,0:T(8,128)(2,1)S(1)}, u32[]{:S(2)}, u32[]{:S(2)}) collective-permute-start(bf16[2,512,512]{2,1,0:T(8,128)(2,1)S(1)} %quarter.1), channel_id=1, source_target_pairs={{0,1},{1,0},{2,3},{3,2},{4,5},{5,4},{6,7},{7,6},{8,9},{9,8},{10,11... | collective-permute-start | bytes 3145736 | tf_op jit(solution)/shard_map/ppermute | solution.py:754
  22.5 5.9 %project.1 = (bf16[768,512]{1,0:T(8,128)(2,1)S(1)}, bf16[3,768,512]{2,1,0:T(8,128)(2,1)S(1)}, bf16[768,512]{1,0:T(8,128)(2,1)S(1)}, bf16[4,512,512]{2,1,0:T(8,128)(2,1)S(1)}) custom-call(bf16[768,512]{1,0:T(8,128)(2,1)S(1)} %copy-done.13, f32[768,128]{1,0:T(8,128)S(1)} %get-tuple-element.81.pack, f32[2,4,512]{2,1,0:T(4,128)S(1)} %copy-done.14, ...), custom_call_target="tpu_custom_call" | custom-call | flops 4000000000 | bytes 4000000 | tf_op jit(solution)/shard_map/project/pallas_call | solution.py:808
  28.5 9.9 %attend.1 = (bf16[768,512]{1,0:T(8,128)(2,1)S(1)}, f32[768,512]{1,0:T(8,128)S(1)}, bf16[768,512]{1,0:T(8,128)(2,1)S(1)}, bf16[2,1152,512]{2,1,0:T(8,128)(2,1)S(1...) custom-call(bf16[192,640]{1,0:T(8,128)(2,1)} %collective-permute-done.rim_low, ...), custom_call_target="tpu_custom_call" | custom-call | flops 6000000000 | bytes 8000000 | tf_op jit(solution)/shard_map/attend/pallas_call | solution.py:836
  38.5 6.8 %mlp_own.1 = (f32[768,512]{1,0:T(8,128)S(1)}, f32[768,512]{1,0:T(8,128)S(1)}, bf16[2,2,2,128,512]{4,3,2,1,0:T(8,128)(2,1)S(1)}, bf16[2,2,2,128,512]{4,3,2,1,0:T(8,128)(2,1)S(1)}) custom-call(s32[5]{0:T(128)S(1)} %stack.23.scalars, bf16[768,512]{1,0:T(8,128)(2,1)S(1)} %get-tuple-element.85.second_in, bf16[768,512]{1,0:T(8,128)(2,1)S(1)} %copy-done.16, ...), custom_call_target="tpu_custom_call" | custom-call | flops 5000000000 | bytes 8000000 | tf_op jit(solution)/shard_map/mlp_own/pallas_call | solution.py:859
  45.2 1.1 collective-permute-done.2.near
  46.3 0.5 collective-permute-start.4
  46.9 3.4 %mlp_near.1 = (f32[768,512]{1,0:T(8,128)S(1)}, f32[768,512]{1,0:T(8,128)S(1)}, bf16[2,2,2,128,512]{4,3,2,1,0:T(8,128)(2,1)S(1)}, bf16[2,2,2,128,512]{4,3,2,1,0:T(8,128)(2,1)S(1)}) custom-call(s32[5]{0:T(128)S(1)} %stack.23.scalars, bf16[768,512]{1,0:T(8,128)(2,1)S(1)} %get-tuple-element.85.second_in, bf16[768,512]{1,0:T(8,128)(2,1)S(1)} %copy-done.16, ...), custom_call_target="tpu_custom_call" | custom-call | flops 2500000000 | bytes 4000000 | tf_op jit(solution)/shard_map/mlp_near/pallas_call | solution.py:889
  50.3 5.8 %mlp_far.1 = (bf16[2,2,2,128,512]{4,3,2,1,0:T(8,128)(2,1)S(1)}, bf16[2,2,2,128,512]{4,3,2,1,0:T(8,128)(2,1)S(1)}, bf16[768,512]{1,0:T(8,128)(2,1)}, f32[768,512]...) custom-call(s32[5]{0:T(128)S(1)} %stack.23.scalars, ...), custom_call_target="tpu_custom_call", output_to_operand_aliasing={{0}: (12, {}), {1}: (13, {})} | custom-call | flops 4000000000 | bytes 8000000 | tf_op jit(solution)/shard_map/mlp_far/pallas_call | solution.py:920
  56.1 2.6 %collective-permute-done.5.rest_got = bf16[2,2,2,128,512]{4,3,2,1,0:T(8,128)(2,1)S(1)} collective-permute-done((bf16[2,2,2,128,512]{4,3,2,1,0:T(8,128)(2,1)S(1)}, bf16[2,2,2,128,512]{4,3,2,1,0:T(8,128)(2,1)S(1)}, u32[]{:S(2)}, u32[]{:S(2)}) %collective-permute-start.5) | collective-permute-done | bytes 1048608 | tf_op jit(solution)/shard_map/ppermute | solution.py:754
  58.7 1.0 large_sum.1
  59.7 1.8 collective-permute-start.6
  61.5 3.7 %collective-permute-start.7 = (bf16[192,640]{1,0:T(8,128)(2,1)S(1)}, bf16[192,640]{1,0:T(8,128)(2,1)S(1)}, u32[]{:S(2)}, u32[]{:S(2)}) collective-permute-start(bf16[192,640]{1,0:T(8,128)(2,1)S(1)} %get-tuple-element.114), channel_id=1, source_target_pairs={{0,1},{1,2},{2,3},{3,4},{4,5},{5,6},{6,7},{7,8},{8,9},{9,10},{10,1... | collective-permute-start | bytes 737288 | tf_op jit(solution)/shard_map/ppermute | solution.py:746
  65.2 1.3 collective-permute-start.8
  66.5 8.7 %attend_back.1 = (bf16[768,512]{1,0:T(8,128)(2,1)S(1)}, f32[1152,512]{1,0:T(8,128)S(1)}, f32[1152,512]{1,0:T(8,128)S(1)}) custom-call(bf16[3,768,512]{2,1,0:T(8,128)(2,1)S(1)} %get-tuple-element.83.qkv, bf16[2,1152,512]{2,1,0:T(8,128)(2,1)S(1)} %get-tuple-element.105.padded, bf16[768,512]{1,0:T(8,128)(2,1)S(1)} %get-tuple-element.106.grad, ...), custom_call_target="tpu_custom_call" | custom-call | flops 8000000000 | bytes 9000000 | tf_op jit(solution)/shard_map/attend_back/pallas_call | solution.py:1055
  75.2 1.3 collective-permute-done.6
  76.6 2.6 %collective-permute-start.9 = (bf16[2,256,512]{2,1,0:T(8,128)(2,1)S(1)}, bf16[2,256,512]{2,1,0:T(8,128)(2,1)S(1)}, u32[]{:S(2)}, u32[]{:S(2)}) collective-permute-start(bf16[2,256,512]{2,1,0:T(8,128)(2,1)S(1)} %bitcast.42), channel_id=1, source_target_pairs={{0,1},{1,0},{2,6},{3,7},{4,5},{5,4},{6,2},{7,3},{8,9},{9,8},{10,14... | collective-permute-start | bytes 1572872 | tf_op jit(solution)/shard_map/ppermute | solution.py:754
  79.2 8.3 %attend_weights.1 = (f32[768,512]{1,0:T(8,128)}, bf16[2,2,2,2,80,512]{5,4,3,2,1,0:T(8,128)(2,1)S(1)}, bf16[2,2,2,2,80,512]{5,4,3,2,1,0:T(8,128)(2,1)S(1)}) custom-call(s32[5]{0:T(128)S(1)} %stack.23.scalars, bf16[2,256,512]{2,1,0:T(8,128)(2,1)S(1)} %bitcast.43, bf16[768,512]{1,0:T(8,128)(2,1)S(1)} %get-tuple-element.108.refs_2_.queries_in, ...), custom_call_target="tpu_custom_call" | custom-call | flops 6000000000 | bytes 9000000 | tf_op jit(solution)/shard_map/attend_weights/pallas_call | solution.py:1067
  87.6 1.6 collective-permute-start.10
  89.3 1.3 collective-permute-done.11
  90.5 0.3 receive.9
  90.9 3.2 %collective-permute-done.10.refs_1_ = bf16[2,128,512]{2,1,0:T(8,128)(2,1)S(1)} collective-permute-done((bf16[2,128,512]{2,1,0:T(8,128)(2,1)S(1)}, bf16[2,128,512]{2,1,0:T(8,128)(2,1)S(1)}, u32[]{:S(2)}, u32[]{:S(2)}) %collective-permute-start.10) | collective-permute-done | bytes 262176 | tf_op jit(solution)/shard_map/ppermute | solution.py:754
  94.1 2.7 %collective-permute-start.12 = (bf16[128,512]{1,0:T(8,128)(2,1)S(1)}, bf16[128,512]{1,0:T(8,128)(2,1)S(1)}, u32[]{:S(2)}, u32[]{:S(2)}) collective-permute-start(bf16[128,512]{1,0:T(8,128)(2,1)S(1)} %get-tuple-element.127.refs_2_), channel_id=1, source_target_pairs={{0,16},{1,17},{2,18},{3,19},{4,20},{5,21},{6,22},{7,23},{8,24},{9,... | collective-permute-start | bytes 393224 | tf_op jit(solution)/shard_map/ppermute | solution.py:754
  96.8 4.7 %collective-permute-done.13.refs_1_ = bf16[2,320,512]{2,1,0:T(8,128)(2,1)S(1)} collective-permute-done((bf16[2,320,512]{2,1,0:T(8,128)(2,1)S(1)}, bf16[2,320,512]{2,1,0:T(8,128)(2,1)S(1)}, u32[]{:S(2)}, u32[]{:S(2)}) %collective-permute-start.13) | collective-permute-done | bytes 655392 | tf_op jit(solution)/shard_map/ppermute | solution.py:754
  101.6 1.8 collective-permute-start.15
  103.4 2.6 %collective-permute-start.14 = (bf16[128,512]{1,0:T(8,128)(2,1)S(1)}, bf16[128,512]{1,0:T(8,128)(2,1)S(1)}, u32[]{:S(2)}, u32[]{:S(2)}) collective-permute-start(bf16[128,512]{1,0:T(8,128)(2,1)S(1)} %blend.2.refs_2_.refs_0_), channel_id=1, source_target_pairs={{0,16},{1,17},{2,18},{3,19},{4,20},{5,21},{6,22},{7,23},{8,24},{9,... | collective-permute-start | bytes 393224 | tf_op jit(solution)/shard_map/ppermute | solution.py:754
  106.1 2.6 %collective-permute-done.15.refs_1_ = bf16[2,160,512]{2,1,0:T(8,128)(2,1)S(1)} collective-permute-done((bf16[2,160,512]{2,1,0:T(8,128)(2,1)S(1)}, bf16[2,160,512]{2,1,0:T(8,128)(2,1)S(1)}, u32[]{:S(2)}, u32[]{:S(2)}) %collective-permute-start.15) | collective-permute-done | bytes 327712 | tf_op jit(solution)/shard_map/ppermute | solution.py:754
  108.8 1.6 collective-permute-start.17
  110.4 1.8 collective-permute-done.14.refs_1_
  112.2 0.4 collective-permute-start.16
  112.6 1.6 collective-permute-done.17.refs_1_
  114.2 2.7 %collective-permute-start.19 = (bf16[80,512]{1,0:T(8,128)(2,1)S(1)}, bf16[80,512]{1,0:T(8,128)(2,1)S(1)}, u32[]{:S(2)}, u32[]{:S(2)}) collective-permute-start(bf16[80,512]{1,0:T(8,128)(2,1)S(1)} %get-tuple-element.133.refs_2_), channel_id=1, source_target_pairs={{0,16},{1,17},{2,18},{3,19},{4,20},{5,21},{6,22},{7,23},{8,24},{9,... | collective-permute-start | bytes 245768 | tf_op jit(solution)/shard_map/ppermute | solution.py:754
  116.9 3.6 %collective-permute-done.16.refs_1_ = bf16[256,512]{1,0:T(8,128)(2,1)S(1)} collective-permute-done((bf16[256,512]{1,0:T(8,128)(2,1)S(1)}, bf16[256,512]{1,0:T(8,128)(2,1)S(1)}, u32[]{:S(2)}, u32[]{:S(2)}) %collective-permute-start.16) | collective-permute-done | bytes 262176 | tf_op jit(solution)/shard_map/ppermute | solution.py:754
  120.5 1.9 %collective-permute-start.20 = (bf16[80,512]{1,0:T(8,128)(2,1)S(1)}, bf16[80,512]{1,0:T(8,128)(2,1)S(1)}, u32[]{:S(2)}, u32[]{:S(2)}) collective-permute-start(bf16[80,512]{1,0:T(8,128)(2,1)S(1)} %blend.3.refs_0_), channel_id=1, source_target_pairs={{0,16},{1,17},{2,18},{3,19},{4,20},{5,21},{6,22},{7,23},{8,24},{9,... | collective-permute-start | bytes 245768 | tf_op jit(solution)/shard_map/ppermute | solution.py:754
  122.4 0.7 collective-permute-start.18
  123.1 2.9 %collective-permute-done.20.refs_1_ = bf16[80,512]{1,0:T(8,128)(2,1)S(1)} collective-permute-done((bf16[80,512]{1,0:T(8,128)(2,1)S(1)}, bf16[80,512]{1,0:T(8,128)(2,1)S(1)}, u32[]{:S(2)}, u32[]{:S(2)}) %collective-permute-start.20) | collective-permute-done | bytes 81952 | tf_op jit(solution)/shard_map/ppermute | solution.py:754
  126.0 1.5 collective-permute-start.22
  127.5 5.8 %collective-permute-done.18.refs_1_ = bf16[512,512]{1,0:T(8,128)(2,1)S(1)} collective-permute-done((bf16[512,512]{1,0:T(8,128)(2,1)S(1)}, bf16[512,512]{1,0:T(8,128)(2,1)S(1)}, u32[]{:S(2)}, u32[]{:S(2)}) %collective-permute-start.18) | collective-permute-done | bytes 524320 | tf_op jit(solution)/shard_map/ppermute | solution.py:754
  133.4 1.8 collective-permute-start.21
  135.2 0.4 collective-permute-start.23
  135.6 12.7 %collective-permute-done.21 = bf16[1024,512]{1,0:T(8,128)(2,1)S(1)} collective-permute-done((bf16[1024,512]{1,0:T(8,128)(2,1)S(1)}, bf16[1024,512]{1,0:T(8,128)(2,1)S(1)}, u32[]{:S(2)}, u32[]{:S(2)}) %collective-permute-start.21) | collective-permute-done | bytes 1048608 | tf_op jit(solution)/shard_map/ppermute | solution.py:754
  148.3 6.5 %ortho_large.2 = (bf16[4,512,512]{2,1,0:T(8,128)(2,1)S(1)}, bf16[2,512,512]{2,1,0:T(8,128)(2,1)S(1)}) custom-call(s32[5]{0:T(128)S(1)} %stack.23.scalars, bf16[2,2,2,128,512]{4,3,2,1,0:T(8,128)(2,1)S(1)} %bitcast.38, bf16[2,2,2,128,512]{4,3,2,1,0:T(8,128)(2,1)S(1)} %bitcast.39, bf16[320,512]{1,0:T(8,128)(2,1)S(1)} %bitcast.49), custom_call_target="tpu_custom_call" | custom-call | flops 5000000000 | bytes 6000000 | tf_op jit(solution)/shard_map/ortho_large/pallas_call | solution.py:1137
  155.0 0.7 collective-permute-start.25
  155.7 5.9 %ortho_large.3.token.own = bf16[2,512,512]{2,1,0:T(8,128)(2,1)S(1)} custom-call(bf16[4,512,512]{2,1,0:T(8,128)(2,1)S(1)} %get-tuple-element.136.refs_2_.given, bf16[640,512]{1,0:T(8,128)(2,1)S(1)} %bitcast.30), custom_call_target="tpu_custom_call" | custom-call | flops 5000000000 | bytes 4000000 | tf_op jit(solution)/shard_map/ortho_large/pallas_call | solution.py:1150
  161.6 1.3 collective-permute-start.24
  162.9 3.3 %moment_large.1 = (f32[512,1024]{1,0:T(8,128)}, f32[1024,512]{1,0:T(8,128)}, f32[8,128]{1,0:T(8,128)S(1)}) custom-call(s32[5]{0:T(128)S(1)} %stack.23.scalars, bf16[2,512,512]{2,1,0:T(8,128)(2,1)S(1)} %get-tuple-element.137.own, bf16[2,512,512]{2,1,0:T(8,128)(2,1)S(1)} %collective-permute-done.26.got, f32[512,1024]{1,0:T(8,128)S(1)} %copy-done.1, ...), custom_call_target="tpu_custom_call" | custom-call | flops 10000000 | bytes 10000000 | tf_op jit(solution)/shard_map/moment_large/pallas_call | solution.py:1168
  166.3 0.7 unpack_small.1
  167.1 8.6 %ortho_small.1.token.own = bf16[2,256,512]{2,1,0:T(8,128)(2,1)S(1)} custom-call(bf16[2,2,256,512]{3,2,1,0:T(8,128)(2,1)S(1)} %get-tuple-element.141.given), custom_call_target="tpu_custom_call" | custom-call | flops 6000000000 | bytes 4000000 | tf_op jit(solution)/shard_map/ortho_small/pallas_call | solution.py:1196
  175.7 0.5 collective-permute-start.29
  176.4 1.5 collective-permute-done.28.table_got
  177.9 4.4 %update_large.1 = (f32[512,1024]{1,0:T(8,128)}, f32[1024,512]{1,0:T(8,128)}, f32[4,256,512]{2,1,0:T(8,128)}, f32[2,2,512]{2,1,0:T(2,128)}, f32[2,2,512]{2,1,0:T(2,128)}, /*index=5*/f32[8,128]{1,0:T(8,128)S(1)}) custom-call(s32[5]{0:T(128)S(1)} %stack.23.scalars, bf16[2,512,512]{2,1,0:T(8,128)(2,1)S(1)} %ortho_large.3.token.own, ...), custom_call_target="tpu_custom_call" | custom-call | flops 10000000 | bytes 20000000 | tf_op jit(solution)/shard_map/update_large/pallas_call | solution.py:1216
  182.3 2.6 %update_small.1 = f32[4,256,512]{2,1,0:T(8,128)} custom-call(s32[5]{0:T(128)S(1)} %stack.23.scalars, bf16[2,256,512]{2,1,0:T(8,128)(2,1)S(1)} %ortho_small.1.token.own, bf16[2,256,512]{2,1,0:T(8,128)(2,1)S(1)} %collective-permute-done.29.got, f32[4,512,512]{2,1,0:T(8,128)S(1)} %copy-done.12, f32[8,128]{1,0:T(8,128)S(1)} %get-tuple-element.143.token), custom_call_target="tpu_custom_call" | custom-call | flops 10000000 | bytes 6000000 | tf_op jit(solution)/shard_map/update_small/pallas_call | solution.py:1254
  (72 shorter events, 1.9 us)
Async XLA Ops:
  0.6 3.0 %copy-start.13 = (bf16[768,512]{1,0:T(8,128)(2,1)S(1)}, bf16[768,512]{1,0:T(8,128)(2,1)}, u32[]{:S(2)}) copy-start(bf16[768,512]{1,0:T(8,128)(2,1)} %features.5) | copy-start | bytes 2359300
  3.7 12.2 %copy-start.4 = (f32[4,256,512]{2,1,0:T(8,128)S(1)}, f32[4,256,512]{2,1,0:T(8,128)}, u32[]{:S(2)}) copy-start(f32[4,256,512]{2,1,0:T(8,128)} %moment.1) | copy-start | bytes 6291460
  4.5 13.7 %collective-permute-start.1 = (bf16[192,640]{1,0:T(8,128)(2,1)}, bf16[192,640]{1,0:T(8,128)(2,1)S(1)}, u32[]{:S(2)}, u32[]{:S(2)}) collective-permute-start(bf16[192,640]{1,0:T(8,128)(2,1)} %get-tuple-element.152), channel_id=1, source_target_pairs={{1,0},{2,1},{3,2},{4,3},{5,4},{6,5},{7,6},{8,7},{9,8},{10,9},{11,1... | collective-permute-start | bytes 737288 | tf_op jit(solution)/shard_map/ppermute | solution.py:746
  5.8 14.2 %collective-permute-start = (bf16[192,640]{1,0:T(8,128)(2,1)}, bf16[192,640]{1,0:T(8,128)(2,1)}, u32[]{:S(2)}, u32[]{:S(2)}) collective-permute-start(bf16[192,640]{1,0:T(8,128)(2,1)} %get-tuple-element.153), channel_id=1, source_target_pairs={{0,1},{1,2},{2,3},{3,4},{4,5},{5,6},{6,7},{7,8},{8,9},{9,10},{10,1... | collective-permute-start | bytes 737288 | tf_op jit(solution)/shard_map/ppermute | solution.py:746
  12.1 1.6 copy-start.5
  13.7 1.6 copy-start.8
  15.3 1.6 copy-start
  15.3 2.2 %copy-start.2 = (f32[1024,512]{1,0:T(8,128)S(1)}, f32[1024,512]{1,0:T(8,128)}, u32[]{:S(2)}) copy-start(f32[1024,512]{1,0:T(8,128)} %down_moment.1) | copy-start | bytes 6291460
  17.5 5.0 %copy-start.11 = (f32[4,512,512]{2,1,0:T(8,128)S(1)}, f32[4,512,512]{2,1,0:T(8,128)}, u32[]{:S(2)}) copy-start(f32[4,512,512]{2,1,0:T(8,128)} %weight.1) | copy-start | bytes 12582916
  17.5 5.0 %copy-start.14 = (f32[2,4,512]{2,1,0:T(4,128)S(1)}, f32[2,4,512]{2,1,0:T(4,128)}, u32[]{:S(2)}) copy-start(f32[2,4,512]{2,1,0:T(4,128)} %modulation.1) | copy-start | bytes 49156
  20.0 26.3 %collective-permute-start.2 = (bf16[2,512,512]{2,1,0:T(8,128)(2,1)S(1)}, bf16[2,512,512]{2,1,0:T(8,128)(2,1)S(1)}, u32[]{:S(2)}, u32[]{:S(2)}) collective-permute-start(bf16[2,512,512]{2,1,0:T(8,128)(2,1)S(1)} %quarter.1), channel_id=1, source_target_pairs={{0,1},{1,0},{2,3},{3,2},{4,5},{5,4},{6,7},{7,6},{8,9},{9,8},{10,11... | collective-permute-start | bytes 3145736 | tf_op jit(solution)/shard_map/ppermute | solution.py:754
  28.4 10.0 %copy-start.6 = (f32[512,1024]{1,0:T(8,128)S(1)}, f32[512,1024]{1,0:T(8,128)}, u32[]{:S(2)}) copy-start(f32[512,1024]{1,0:T(8,128)} %up_weight.1) | copy-start | bytes 6291460
  28.4 10.0 %copy-start.9 = (f32[1024,512]{1,0:T(8,128)S(1)}, f32[1024,512]{1,0:T(8,128)}, u32[]{:S(2)}) copy-start(f32[1024,512]{1,0:T(8,128)} %down_weight.1) | copy-start | bytes 6291460
  28.5 10.0 %copy-start.16 = (bf16[768,512]{1,0:T(8,128)(2,1)S(1)}, bf16[768,512]{1,0:T(8,128)(2,1)}, u32[]{:S(2)}) copy-start(bf16[768,512]{1,0:T(8,128)(2,1)} %cotangent.5) | copy-start | bytes 2359300
  46.3 3.9 %collective-permute-start.3 = (bf16[2,512,512]{2,1,0:T(8,128)(2,1)S(1)}, bf16[2,512,512]{2,1,0:T(8,128)(2,1)S(1)}, u32[]{:S(2)}, u32[]{:S(2)}) collective-permute-start(bf16[2,512,512]{2,1,0:T(8,128)(2,1)S(1)} %collective-permute-done.2.near), channel_id=1, source_target_pairs={{0,2},{1,3},{2,0},{3,1},{4,6},{5,7},{6,4},{7,5},{8,10},{9,11},{10,... | collective-permute-start | bytes 3145736 | tf_op jit(solution)/shard_map/ppermute | solution.py:754
  46.3 9.7 %collective-permute-start.4 = (bf16[2,2,2,128,512]{4,3,2,1,0:T(8,128)(2,1)S(1)}, bf16[2,2,2,128,512]{4,3,2,1,0:T(8,128)(2,1)S(1)}, u32[]{:S(2)}, u32[]{:S(2)}) collective-permute-start(bf16[2,2,2,128,512]{4,3,2,1,0:T(8,128)(2,1)S(1)} %get-tuple-element.100), channel_id=1, source_target_pairs={{0,2},{1,3},{2,0},{3,1},{4,6},{5,7},{6,4},{7,5},{8,10},{9,11},{10,... | collective-permute-start | bytes 3145736 | tf_op jit(solution)/shard_map/ppermute | solution.py:754
  56.0 2.7 %collective-permute-start.5 = (bf16[2,2,2,128,512]{4,3,2,1,0:T(8,128)(2,1)S(1)}, bf16[2,2,2,128,512]{4,3,2,1,0:T(8,128)(2,1)S(1)}, u32[]{:S(2)}, u32[]{:S(2)}) collective-permute-start(bf16[2,2,2,128,512]{4,3,2,1,0:T(8,128)(2,1)S(1)} %get-tuple-element.102), channel_id=1, source_target_pairs={{0,2},{1,3},{2,0},{3,1},{4,6},{5,7},{6,4},{7,5},{8,10},{9,11},{10,... | collective-permute-start | bytes 3145736 | tf_op jit(solution)/shard_map/ppermute | solution.py:754
  59.7 16.7 %collective-permute-start.6 = (bf16[2,2,2,128,512]{4,3,2,1,0:T(8,128)(2,1)S(1)}, bf16[2,2,2,128,512]{4,3,2,1,0:T(8,128)(2,1)S(1)}, u32[]{:S(2)}, u32[]{:S(2)}) collective-permute-start(bf16[2,2,2,128,512]{4,3,2,1,0:T(8,128)(2,1)S(1)} %get-tuple-element.104.token), channel_id=1, source_target_pairs={{0,4},{1,5},{2,10},{3,11},{4,0},{5,1},{6,14},{7,15},{8,12},{9,13},... | collective-permute-start | bytes 3145736 | tf_op jit(solution)/shard_map/ppermute | solution.py:754
  61.5 17.7 %collective-permute-start.7 = (bf16[192,640]{1,0:T(8,128)(2,1)S(1)}, bf16[192,640]{1,0:T(8,128)(2,1)S(1)}, u32[]{:S(2)}, u32[]{:S(2)}) collective-permute-start(bf16[192,640]{1,0:T(8,128)(2,1)S(1)} %get-tuple-element.114), channel_id=1, source_target_pairs={{0,1},{1,2},{2,3},{3,4},{4,5},{5,6},{6,7},{7,8},{8,9},{9,10},{10,1... | collective-permute-start | bytes 737288 | tf_op jit(solution)/shard_map/ppermute | solution.py:746
  65.2 14.0 %collective-permute-start.8 = (bf16[192,640]{1,0:T(8,128)(2,1)S(1)}, bf16[192,640]{1,0:T(8,128)(2,1)S(1)}, u32[]{:S(2)}, u32[]{:S(2)}) collective-permute-start(bf16[192,640]{1,0:T(8,128)(2,1)S(1)} %get-tuple-element.115), channel_id=1, source_target_pairs={{1,0},{2,1},{3,2},{4,3},{5,4},{6,5},{7,6},{8,7},{9,8},{10,9},{11,1... | collective-permute-start | bytes 737288 | tf_op jit(solution)/shard_map/ppermute | solution.py:746
  76.6 10.9 %collective-permute-start.9 = (bf16[2,256,512]{2,1,0:T(8,128)(2,1)S(1)}, bf16[2,256,512]{2,1,0:T(8,128)(2,1)S(1)}, u32[]{:S(2)}, u32[]{:S(2)}) collective-permute-start(bf16[2,256,512]{2,1,0:T(8,128)(2,1)S(1)} %bitcast.42), channel_id=1, source_target_pairs={{0,1},{1,0},{2,6},{3,7},{4,5},{5,4},{6,2},{7,3},{8,9},{9,8},{10,14... | collective-permute-start | bytes 1572872 | tf_op jit(solution)/shard_map/ppermute | solution.py:754
  87.5 3.0 %collective-permute-start.11 = (bf16[2,2,2,2,80,512]{5,4,3,2,1,0:T(8,128)(2,1)S(1)}, bf16[2,2,2,2,80,512]{5,4,3,2,1,0:T(8,128)(2,1)S(1)}, u32[]{:S(2)}, u32[]{:S(2)}) collective-permute-start(bf16[2,2,2,2,80,512]{5,4,3,2,1,0:T(8,128)(2,1)S(1)} %get-tuple-element.121.refs_2_), channel_id=1, source_target_pairs={{0,2},{1,3},{2,0},{3,1},{4,6},{5,7},{6,4},{7,5},{8,10},{9,11},{10,... | collective-permute-start | bytes 3932168 | tf_op jit(solution)/shard_map/ppermute | solution.py:754
  87.6 6.4 %collective-permute-start.10 = (bf16[2,128,512]{2,1,0:T(8,128)(2,1)S(1)}, bf16[2,128,512]{2,1,0:T(8,128)(2,1)S(1)}, u32[]{:S(2)}, u32[]{:S(2)}) collective-permute-start(bf16[2,128,512]{2,1,0:T(8,128)(2,1)S(1)} %bitcast.56), channel_id=1, source_target_pairs={{0,8},{1,9},{2,3},{3,2},{4,12},{5,13},{6,7},{7,6},{8,0},{9,1},{10,... | collective-permute-start | bytes 786440 | tf_op jit(solution)/shard_map/ppermute | solution.py:754
  90.8 10.7 %collective-permute-start.13 = (bf16[2,320,512]{2,1,0:T(8,128)(2,1)S(1)}, bf16[2,320,512]{2,1,0:T(8,128)(2,1)S(1)}, u32[]{:S(2)}, u32[]{:S(2)}) collective-permute-start(bf16[2,320,512]{2,1,0:T(8,128)(2,1)S(1)} %bitcast.40), channel_id=1, source_target_pairs={{0,1},{1,0},{2,6},{3,7},{4,5},{5,4},{6,2},{7,3},{8,9},{9,8},{10,14... | collective-permute-start | bytes 1966088 | tf_op jit(solution)/shard_map/ppermute | solution.py:754
  94.1 9.2 %collective-permute-start.12 = (bf16[128,512]{1,0:T(8,128)(2,1)S(1)}, bf16[128,512]{1,0:T(8,128)(2,1)S(1)}, u32[]{:S(2)}, u32[]{:S(2)}) collective-permute-start(bf16[128,512]{1,0:T(8,128)(2,1)S(1)} %get-tuple-element.127.refs_2_), channel_id=1, source_target_pairs={{0,16},{1,17},{2,18},{3,19},{4,20},{5,21},{6,22},{7,23},{8,24},{9,... | collective-permute-start | bytes 393224 | tf_op jit(solution)/shard_map/ppermute | solution.py:754
  101.6 7.1 %collective-permute-start.15 = (bf16[2,160,512]{2,1,0:T(8,128)(2,1)S(1)}, bf16[2,160,512]{2,1,0:T(8,128)(2,1)S(1)}, u32[]{:S(2)}, u32[]{:S(2)}) collective-permute-start(bf16[2,160,512]{2,1,0:T(8,128)(2,1)S(1)} %bitcast.51), channel_id=1, source_target_pairs={{0,4},{1,5},{2,10},{3,11},{4,0},{5,1},{6,14},{7,15},{8,12},{9,13},... | collective-permute-start | bytes 983048 | tf_op jit(solution)/shard_map/ppermute | solution.py:754
  103.4 8.8 %collective-permute-start.14 = (bf16[128,512]{1,0:T(8,128)(2,1)S(1)}, bf16[128,512]{1,0:T(8,128)(2,1)S(1)}, u32[]{:S(2)}, u32[]{:S(2)}) collective-permute-start(bf16[128,512]{1,0:T(8,128)(2,1)S(1)} %blend.2.refs_2_.refs_0_), channel_id=1, source_target_pairs={{0,16},{1,17},{2,18},{3,19},{4,20},{5,21},{6,22},{7,23},{8,24},{9,... | collective-permute-start | bytes 393224 | tf_op jit(solution)/shard_map/ppermute | solution.py:754
  108.8 5.4 %collective-permute-start.17 = (bf16[2,80,512]{2,1,0:T(8,128)(2,1)S(1)}, bf16[2,80,512]{2,1,0:T(8,128)(2,1)S(1)}, u32[]{:S(2)}, u32[]{:S(2)}) collective-permute-start(bf16[2,80,512]{2,1,0:T(8,128)(2,1)S(1)} %bitcast.61), channel_id=1, source_target_pairs={{0,8},{1,9},{2,3},{3,2},{4,12},{5,13},{6,7},{7,6},{8,0},{9,1},{10,... | collective-permute-start | bytes 491528 | tf_op jit(solution)/shard_map/ppermute | solution.py:754
  112.2 8.2 %collective-permute-start.16 = (bf16[256,512]{1,0:T(8,128)(2,1)S(1)}, bf16[256,512]{1,0:T(8,128)(2,1)S(1)}, u32[]{:S(2)}, u32[]{:S(2)}) collective-permute-start(bf16[256,512]{1,0:T(8,128)(2,1)S(1)} %bitcast.53), channel_id=1, source_target_pairs={{0,8},{1,9},{2,3},{3,2},{4,12},{5,13},{6,7},{7,6},{8,0},{9,1},{10,... | collective-permute-start | bytes 786440 | tf_op jit(solution)/shard_map/ppermute | solution.py:754
  114.2 6.3 %collective-permute-start.19 = (bf16[80,512]{1,0:T(8,128)(2,1)S(1)}, bf16[80,512]{1,0:T(8,128)(2,1)S(1)}, u32[]{:S(2)}, u32[]{:S(2)}) collective-permute-start(bf16[80,512]{1,0:T(8,128)(2,1)S(1)} %get-tuple-element.133.refs_2_), channel_id=1, source_target_pairs={{0,16},{1,17},{2,18},{3,19},{4,20},{5,21},{6,22},{7,23},{8,24},{9,... | collective-permute-start | bytes 245768 | tf_op jit(solution)/shard_map/ppermute | solution.py:754
  120.5 5.4 %collective-permute-start.20 = (bf16[80,512]{1,0:T(8,128)(2,1)S(1)}, bf16[80,512]{1,0:T(8,128)(2,1)S(1)}, u32[]{:S(2)}, u32[]{:S(2)}) collective-permute-start(bf16[80,512]{1,0:T(8,128)(2,1)S(1)} %blend.3.refs_0_), channel_id=1, source_target_pairs={{0,16},{1,17},{2,18},{3,19},{4,20},{5,21},{6,22},{7,23},{8,24},{9,... | collective-permute-start | bytes 245768 | tf_op jit(solution)/shard_map/ppermute | solution.py:754
  122.4 10.9 %collective-permute-start.18 = (bf16[512,512]{1,0:T(8,128)(2,1)S(1)}, bf16[512,512]{1,0:T(8,128)(2,1)S(1)}, u32[]{:S(2)}, u32[]{:S(2)}) collective-permute-start(bf16[512,512]{1,0:T(8,128)(2,1)S(1)} %bitcast.45), channel_id=1, source_target_pairs={{0,1},{1,0},{2,6},{3,7},{4,5},{5,4},{6,2},{7,3},{8,9},{9,8},{10,14... | collective-permute-start | bytes 1572872 | tf_op jit(solution)/shard_map/ppermute | solution.py:754
  126.0 9.2 %collective-permute-start.22 = (bf16[160,512]{1,0:T(8,128)(2,1)S(1)}, bf16[160,512]{1,0:T(8,128)(2,1)S(1)}, u32[]{:S(2)}, u32[]{:S(2)}) collective-permute-start(bf16[160,512]{1,0:T(8,128)(2,1)S(1)} %bitcast.58), channel_id=1, source_target_pairs={{0,8},{1,9},{2,3},{3,2},{4,12},{5,13},{6,7},{7,6},{8,0},{9,1},{10,... | collective-permute-start | bytes 491528 | tf_op jit(solution)/shard_map/ppermute | solution.py:754
  133.4 14.9 %collective-permute-start.21 = (bf16[1024,512]{1,0:T(8,128)(2,1)S(1)}, bf16[1024,512]{1,0:T(8,128)(2,1)S(1)}, u32[]{:S(2)}, u32[]{:S(2)}) collective-permute-start(bf16[1024,512]{1,0:T(8,128)(2,1)S(1)} %bitcast.36), channel_id=1, source_target_pairs={{0,4},{1,5},{2,10},{3,11},{4,0},{5,1},{6,14},{7,15},{8,12},{9,13},... | collective-permute-start | bytes 3145736 | tf_op jit(solution)/shard_map/ppermute | solution.py:754
  135.2 19.6 %collective-permute-start.23 = (bf16[320,512]{1,0:T(8,128)(2,1)S(1)}, bf16[320,512]{1,0:T(8,128)(2,1)S(1)}, u32[]{:S(2)}, u32[]{:S(2)}) collective-permute-start(bf16[320,512]{1,0:T(8,128)(2,1)S(1)} %bitcast.48), channel_id=1, source_target_pairs={{0,4},{1,5},{2,10},{3,11},{4,0},{5,1},{6,14},{7,15},{8,12},{9,13},... | collective-permute-start | bytes 983048 | tf_op jit(solution)/shard_map/ppermute | solution.py:754
  154.8 8.1 %collective-permute-start.26 = (bf16[2,512,512]{2,1,0:T(8,128)(2,1)S(1)}, bf16[2,512,512]{2,1,0:T(8,128)(2,1)S(1)}, u32[]{:S(2)}, u32[]{:S(2)}) collective-permute-start(bf16[2,512,512]{2,1,0:T(8,128)(2,1)S(1)} %get-tuple-element.137.own), channel_id=1, source_target_pairs={{0,2},{1,3},{2,0},{3,1},{4,6},{5,7},{6,4},{7,5},{8,10},{9,11},{10,... | collective-permute-start | bytes 3145736 | tf_op jit(solution)/shard_map/ppermute | solution.py:754
  154.9 8.0 %copy-start.1 = (f32[512,1024]{1,0:T(8,128)S(1)}, f32[512,1024]{1,0:T(8,128)}, u32[]{:S(2)}) copy-start(f32[512,1024]{1,0:T(8,128)} %up_moment.1) | copy-start | bytes 6291460
  154.9 8.0 %copy-start.3 = (f32[1024,512]{1,0:T(8,128)S(1)}, f32[1024,512]{1,0:T(8,128)}, u32[]{:S(2)}) copy-start(f32[1024,512]{1,0:T(8,128)} %down_moment.1) | copy-start | bytes 6291460
  155.0 11.3 %collective-permute-start.25 = (bf16[640,512]{1,0:T(8,128)(2,1)S(1)}, bf16[640,512]{1,0:T(8,128)(2,1)S(1)}, u32[]{:S(2)}, u32[]{:S(2)}) collective-permute-start(bf16[640,512]{1,0:T(8,128)(2,1)S(1)} %bitcast.29), channel_id=1, source_target_pairs={{0,1},{1,0},{2,6},{3,7},{4,5},{5,4},{6,2},{7,3},{8,9},{9,8},{10,14... | collective-permute-start | bytes 1966088 | tf_op jit(solution)/shard_map/ppermute | solution.py:754
  161.6 14.8 %collective-permute-start.24 = (bf16[2,512,512]{2,1,0:T(8,128)(2,1)S(1)}, bf16[2,512,512]{2,1,0:T(8,128)(2,1)S(1)}, u32[]{:S(2)}, u32[]{:S(2)}) collective-permute-start(bf16[2,512,512]{2,1,0:T(8,128)(2,1)S(1)} %ortho_large.3.token.own), channel_id=1, source_target_pairs={{0,2},{1,3},{2,0},{3,1},{4,6},{5,7},{6,4},{7,5},{8,10},{9,11},{10,... | collective-permute-start | bytes 3145736 | tf_op jit(solution)/shard_map/ppermute | solution.py:754
  167.0 10.9 %collective-permute-start.27 = (bf16[2,256,512]{2,1,0:T(8,128)(2,1)S(1)}, bf16[2,256,512]{2,1,0:T(8,128)(2,1)S(1)}, u32[]{:S(2)}, u32[]{:S(2)}) collective-permute-start(bf16[2,256,512]{2,1,0:T(8,128)(2,1)S(1)} %get-tuple-element.139.mix), channel_id=1, source_target_pairs={{0,2},{1,3},{2,0},{3,1},{4,6},{5,7},{6,4},{7,5},{8,10},{9,11},{10,... | collective-permute-start | bytes 1572872 | tf_op jit(solution)/shard_map/ppermute | solution.py:754
  167.1 10.8 %copy-start.7 = (f32[512,1024]{1,0:T(8,128)S(1)}, f32[512,1024]{1,0:T(8,128)}, u32[]{:S(2)}) copy-start(f32[512,1024]{1,0:T(8,128)} %up_weight.1) | copy-start | bytes 6291460
  167.1 10.8 %copy-start.10 = (f32[1024,512]{1,0:T(8,128)S(1)}, f32[1024,512]{1,0:T(8,128)}, u32[]{:S(2)}) copy-start(f32[1024,512]{1,0:T(8,128)} %down_weight.1) | copy-start | bytes 6291460
  167.1 10.8 %copy-start.15 = (f32[2,2,512]{2,1,0:T(2,128)S(1)}, f32[2,2,512]{2,1,0:T(2,128)}, u32[]{:S(2)}) copy-start(f32[2,2,512]{2,1,0:T(2,128)} %held_moment.1) | copy-start | bytes 24580
  175.7 6.6 %collective-permute-start.29 = (bf16[2,256,512]{2,1,0:T(8,128)(2,1)S(1)}, bf16[2,256,512]{2,1,0:T(8,128)(2,1)S(1)}, u32[]{:S(2)}, u32[]{:S(2)}) collective-permute-start(bf16[2,256,512]{2,1,0:T(8,128)(2,1)S(1)} %ortho_small.1.token.own), channel_id=1, source_target_pairs={{0,2},{1,3},{2,0},{3,1},{4,6},{5,7},{6,4},{7,5},{8,10},{9,11},{10,... | collective-permute-start | bytes 1572872 | tf_op jit(solution)/shard_map/ppermute | solution.py:754
  176.3 1.6 collective-permute-start.28
  177.9 4.5 %copy-start.12 = (f32[4,512,512]{2,1,0:T(8,128)S(1)}, f32[4,512,512]{2,1,0:T(8,128)}, u32[]{:S(2)}) copy-start(f32[4,512,512]{2,1,0:T(8,128)} %weight.1) | copy-start | bytes 12582916
where the time goes:
time: 185 us
  Pallas kernels  84.4 us (46%)
  waiting for transfers between devices  48.5 us (26%)
  starting transfers between devices  42.4 us (23%)
  local copies, waits for them, and re-layouts  5.98 us (3%)
  other arithmetic  2.71 us (1%)
    ppermute x26, waiting for transfers between devices, swap(): return lax.ppermute(value, AXES, pairs)  46.6 us
    ppermute x26, starting transfers between devices, swap(): return lax.ppermute(value, AXES, pairs)  29.9 us
    ppermute x4, starting transfers between devices, along(): return lax.ppermute(value, AXES, pairs)  12.4 us
    pallas_call x1, Pallas kernels, on_device(): pl.pallas_call(forward_kernel, out_shape=(struct((row_count, D), bf16), s...  9.94 us
    pallas_call x1, Pallas kernels, on_device(): pl.pallas_call(backward_kernel, out_shape=(struct((row_count, D), bf16),)...  8.72 us
    pallas_call x1, Pallas kernels, on_device(): pl.pallas_call(small_kernel, out_shape=struct((2, 256, D), bf16), in_spec...  8.63 us
    pallas_call x1, Pallas kernels, on_device(): pl.pallas_call(weights_kernel, out_shape=(struct((row_count, D), f32), pi...  8.28 us
    pallas_call x1, Pallas kernels, on_device(): pl.pallas_call(mlp_own_kernel, out_shape=(struct((row_count, D), f32), st...  6.79 us
  transfers between devices with their start and end apart: 30, of which 15 were waited for; matrix products, arithmetic and copies ran while one was open for 0% of the time, Pallas kernels for 44%

commit v1 on v0

--- a/solution.py
+++ b/solution.py
@@ -122,8 +122,11 @@
 
 
 def past_kernel(scalars, up, down, attention, large_past, small_past):
-    large_past[...] = jnp.where(scalars[0] == 0, up[...], down[...].T)
-    small_past[...] = attention[0]
+    z2 = scalars[3]
+    large = jnp.where(scalars[0] == 0, up[...], down[...].T)
+    for j in range(2):
+        large_past[j ^ z2] = large[j * 128 : (j + 1) * 128]
+        small_past[j ^ z2] = attention[0, j * 64 : (j + 1) * 64, :]
 
 
 def project_kernel(features, pack, mod, weights, first_in, qkv, counts, rounded):
@@ -486,9 +489,9 @@
                 slot_at, hid_at, row_half = slot ^ slot_bit, half ^ hid, (q // 2) ^ z1
                 index = (
                     away,
-                    jnp.where(target == 0, hid_at, slot_at),
                     jnp.where(target == 0, slot_at, row_half),
-                    jnp.where(target == 0, row_half, hid_at),
+                    hid_at,
+                    jnp.where(target == 0, row_half, slot_at),
                     (q % 2) ^ z2,
                 )
                 start = half * 256 + q * 64
@@ -520,14 +523,20 @@
     send[...] = (kept[1].astype(f32) + got[1].astype(f32)).astype(bf16)
 
 
-def blend_kernel(*refs):
+def total_kernel(*refs):
+    kept, got, total = refs[0], refs[1], refs[-1]
+    total[...] = (kept[...] + got[...].astype(f32)).astype(bf16)
+
+
+def blend_kernel(flip, *refs):
     kept, got, past, part = refs[0], refs[1], refs[2], refs[-1]
-    rows = past.shape[0]
-    total = kept[...] + got[...].astype(f32)
-    blended = (1.0 + momentum_rate) * total[:rows] + momentum_rate * momentum_rate * past[...]
-    part[:rows, :] = blended.astype(bf16)
-    if rows < part.shape[0]:
-        part[rows:, :] = total[rows:].astype(bf16)
+    rows = past.shape[1]
+    for j in range(2):
+        total = kept[j].astype(f32) + got[j ^ flip].astype(f32)
+        blended = (1.0 + momentum_rate) * total[:rows] + momentum_rate * momentum_rate * past[j]
+        part[j, :rows, :] = blended.astype(bf16)
+        if rows < part.shape[1]:
+            part[j, rows:, :] = total[rows:].astype(bf16)
 
 
 def join_kernel(*refs):
@@ -603,72 +612,92 @@
 
 
 def small_start_kernel(scalars, kept, got, token, work, blend, table):
+    table[...] = jnp.zeros_like(table)
     core, slot_bit, z1, z2 = (scalars[i] for i in range(4))
     for n in range(16):
         b1, b2, b3, b4 = n // 8, (n // 4) % 2, (n // 2) % 2, n % 2
         source = kept if b1 == 0 else got
         block = source[b2, b3, b4]
-        slot = jnp.where(core == 0, b2, b1) ^ slot_bit
-        half = jnp.where(core == 0, b1, b3)
-        row_half = jnp.where(core == 0, b3, b2)
+        slot = jnp.where(core == 0, b1, b3) ^ slot_bit
+        half = b2
+        row_half = jnp.where(core == 0, b3, b1)
         quarter = (row_half ^ z1) * 2 + (b4 ^ z2)
         work[slot, half, rows_of(quarter * 64, 64), :] = block[:64]
 
-        @pl.when((half == 0) & (slot == 0))
+        @pl.when((slot == 0) & (half == 0))
         def _():
             table[pl.ds(quarter, 1), :] = block[64:].astype(f32)[:1]
 
-    table[4:, :] = jnp.zeros((4, D), f32)
     for s in range(2):
-        blend[s] = work[s, 0]
-
-
-def small_kernel(given, result, first, second, poly_first, poly_second):
-    works = (first, second)
-    scales = []
-    for s, work in enumerate(works):
-        total = jnp.zeros((8, D), f32)
-        for half in range(2):
-            block = given[s, half]
-            work[half] = block
-            value = block.astype(f32)
-            total = total + jnp.sum((value * value).reshape(32, 8, D), axis=0)
-        scales.append(1.0 / (jnp.sqrt(jnp.sum(total)) + 1e-07))
-    groups = [(work, ((0,), (1,))) for work in works]
-    polys = [poly_first, poly_second]
-
-    def step(i, factors):
-        newton_schulz(groups, polys, True, factors)
-        return (jnp.ones((), f32),) * 2
-
-    lax.fori_loop(0, NS_STEPS, step, tuple(scales))
-    for s, work in enumerate(works):
-        result[s] = work[0]
-
-
-def new_moment(blend, moment):
-    share = 1.0 / (1.0 + momentum_rate)
-    return share * blend + (momentum_rate - share * momentum_rate * momentum_rate) * moment
-
-
-def new_weight(weight, ortho, longest):
-    return weight - muon_rate * (0.2 * math.sqrt(longest) * ortho + decay_rate * weight)
-
-
-def large_moment_kernel(scalars, own, got, up_moment, down_moment, token, up_moment_new, down_moment_new, done):
-    done[...] = jnp.zeros_like(done)
-    first = scalars[0] == 0
-    mine, other = own[0].astype(f32), got[0].astype(f32)
-    up_moment_new[...] = new_moment(jnp.where(first, mine, other), up_moment[...])
-    down_moment_new[...] = new_moment(jnp.where(first, other, mine).T, down_moment[...])
-
-
-def large_weight_kernel(
+        blend[s, :256, :] = work[s, 0]
+        blend[s, 256:, :] = table[...].astype(bf16)
+
+
+def small_kernel(
     scalars,
+    given,
     own,
     got,
     up_weight,
     down_weight,
+    token,
+    result,
+    up_new,
+    down_new,
+    first,
+    second,
+    poly_first,
+    poly_second,
+    factors,
+):
+    turn = pl.program_id(0)
+    works = (first, second)
+
+    @pl.when(turn == 0)
+    def _():
+        for s, work in enumerate(works):
+            total = jnp.zeros((8, D), f32)
+            for half in range(2):
+                block = given[s, half]
+                work[half] = block
+                value = block.astype(f32)
+                total = total + jnp.sum((value * value).reshape(32, 8, D), axis=0)
+            factors[s] = 1.0 / (jnp.sqrt(jnp.sum(total)) + 1e-07)
+
+    groups = [(work, ((0,), (1,))) for work in works]
+    scales = [jnp.where(turn == 0, factors[s], 1.0) for s in range(2)]
+    newton_schulz(groups, [poly_first, poly_second], True, scales)
+    is_up = scalars[0] == 0
+    ups = jnp.where(is_up, own[0], got[0])
+    downs = jnp.where(is_up, got[0], own[0])
+    up_new[...] = new_weight(up_weight[...], ups.astype(f32), FF)
+    down_new[...] = new_weight(down_weight[...], downs.T.astype(f32), FF)
+
+    @pl.when(turn == NS_STEPS - 1)
+    def _():
+        for s, work in enumerate(works):
+            result[s] = work[0]
+
+
+def new_moment(blend, moment):
+    share = 1.0 / (1.0 + momentum_rate)
+    return share * blend + (momentum_rate - share * momentum_rate * momentum_rate) * moment
+
+
+def new_weight(weight, ortho, longest):
+    return weight - muon_rate * (0.2 * math.sqrt(longest) * ortho + decay_rate * weight)
+
+
+def large_moment_kernel(scalars, own, got, up_moment, down_moment, token, up_moment_new, down_moment_new, done):
+    done[...] = jnp.zeros_like(done)
+    first = scalars[0] == 0
+    ups, downs = jnp.where(first, own[0], got[0]), jnp.where(first, got[0], own[0])
+    up_moment_new[...] = new_moment(ups.astype(f32), up_moment[...])
+    down_moment_new[...] = new_moment(downs.T.astype(f32), down_moment[...])
+
+
+def small_moment_kernel(
+    scalars,
     mix,
     mix_got,
     moment,
@@ -677,8 +706,6 @@
     modulation,
     held_moment,
     token,
-    up_new,
-    down_new,
     moment_new,
     held_moment_new,
     held_new,
@@ -688,16 +715,12 @@
 ):
     done[...] = jnp.zeros_like(done)
     core, turn = scalars[0], pl.program_id(0)
-    first = core == 0
-    mine, other = own[0].astype(f32), got[0].astype(f32)
-    up_new[...] = new_weight(up_weight[...], jnp.where(first, mine, other), FF)
-    down_new[...] = new_weight(down_weight[...], jnp.where(first, other, mine).T, FF)
-    blend = jnp.where(core == turn // 2, mix[0].astype(f32), mix_got[0].astype(f32))
+    blend = jnp.where(core == turn // 2, mix[0], mix_got[0]).astype(f32)
     moment_new[0] = new_moment(blend, moment[0])
 
     @pl.when(turn == 0)
     def _():
-        total = jnp.where(first, table[...], table_got[...])
+        total = jnp.where(core == 0, table[0], table_got[0]).astype(f32)
         for level in range(2):
             for column in range(2):
                 row = level * 2 + column
@@ -765,9 +788,6 @@
 
     pack, scalars, is_first = lax.optimization_barrier((pack, scalars, is_first))
     mod = modulation
-
-    def past_row(s):
-        return s[2] * 2 + s[3]
 
     quarter = pl.pallas_call(
         quarter_kernel,
@@ -791,16 +811,16 @@
             num_scalar_prefetch=1,
             grid=(1,),
             in_specs=[
-                pl.BlockSpec((128, CHUNK), lambda g, s: (past_row(s), s[1])),
-                pl.BlockSpec((CHUNK, 128), lambda g, s: (s[1], past_row(s))),
-                pl.BlockSpec((1, 64, D), lambda g, s: (s[0] * 2 + s[1], past_row(s), 0)),
+                pl.BlockSpec((256, CHUNK), lambda g, s: (s[2], s[1])),
+                pl.BlockSpec((CHUNK, 256), lambda g, s: (s[1], s[2])),
+                pl.BlockSpec((1, 128, D), lambda g, s: (s[0] * 2 + s[1], s[2], 0)),
             ],
             out_specs=(
-                pl.BlockSpec((128, CHUNK), lambda g, s: (0, 0)),
-                pl.BlockSpec((64, D), lambda g, s: (0, 0)),
+                pl.BlockSpec((2, 128, CHUNK), lambda g, s: (0, 0, 0)),
+                pl.BlockSpec((2, 64, D), lambda g, s: (0, 0, 0)),
             ),
         ),
-        out_shape=(struct((128, CHUNK), f32), struct((64, D), f32)),
+        out_shape=(struct((2, 128, CHUNK), f32), struct((2, 64, D), f32)),
         cost_estimate=cost(1e6, 1e6),
         name="past",
         compiler_params=room(4),
@@ -1001,13 +1021,13 @@
         compiler_params=room(12),
     )(scalars, own_kept, swap(own_sent, 2), rest_kept, swap(rest_sent, 2))
 
-    def ordered(kernel, values, tokens, shapes, name):
+    def ordered(kernel, values, tokens, shapes, name, work=1e10):
         return pl.pallas_call(
             kernel,
             out_shape=shapes,
             in_specs=[VMEM] * len(values) + [pl.BlockSpec(memory_space=pl.ANY)] * len(tokens),
             out_specs=jax.tree.map(lambda _: VMEM, shapes),
-            cost_estimate=cost(3e10, 1e3),
+            cost_estimate=cost(work, 1e3),
             name=name,
             compiler_params=room(8),
         )(*values, *tokens)
@@ -1022,22 +1042,29 @@
             (struct((rows, D), f32), struct((rows, D), bf16)),
             "receive",
         )
-        half = (2, rows // 2, D) if rows > 128 else (rows, D)
+        half = (2, rows // 2, D)
         return keep.reshape(half), send.reshape(half)
 
-    def blend(keep, got, past, *tokens):
-        mask = 32
-        if mask < device_count:
-            keep = keep + got.astype(f32)
-            while mask < device_count:
-                rounded = keep.astype(bf16)
-                keep, got = rounded.astype(f32), swap(rounded, mask)
-                mask *= 2
-                if mask < device_count:
-                    keep = keep + got.astype(f32)
-        return ordered(blend_kernel, (keep, got, past), tokens, struct(keep.shape, bf16), "blend")
-
-    def join(part, got, *tokens):
+    def rounded_total(keep, got, *tokens):
+        return ordered(total_kernel, (keep, got), tokens, struct(keep.shape, bf16), "total")
+
+    def blend(total, got, past, *tokens, work=1e10):
+        flip, mask = 1, 32
+        while mask < device_count:
+            mine = total.astype(f32) + (got[::-1] if flip else got).astype(f32)
+            total, flip = mine.astype(bf16), 0
+            got = swap(total, mask)
+            mask *= 2
+        return ordered(
+            functools.partial(blend_kernel, flip),
+            (total, got, past),
+            tokens,
+            struct(total.shape, bf16),
+            "blend",
+            work,
+        ).reshape(-1, D)
+
+    def join(part, got, *tokens, work=1e10):
         rows = math.prod(part.shape[:-1])
         return ordered(
             join_kernel,
@@ -1045,10 +1072,11 @@
             tokens,
             struct((2, rows, D), bf16),
             "join",
+            work,
         ).reshape(2 * rows, D)
 
     large_routes = ((4, 8), (1, 4), (8, 1), (16, 16))
-    small_routes = ((1, 4), (4, 8), (8, 1), (16, 16))
+    small_routes = ((4, 8), (1, 1), (8, 4), (16, 16))
 
     padded_rows = row_count + 2 * HALO
     large_got = swap(large_send, *large_routes[0])
@@ -1113,23 +1141,21 @@
     small_got = swap(small_send, 2)
     chain_large(2, small_sent)
     chain_small(0, large_send)
-    chain_large(3, small_send)
-    chain_small(1, large_send)
-    large_part = blend(large_keep, large_got, large_past, small_send)
-    large_got = swap(large_part, *large_routes[3])
+    large_total = rounded_total(large_keep, large_got, small_send)
+    large_got = swap(large_total, *large_routes[3])
+    chain_small(1, large_total)
+    large_part = blend(large_total, large_got, large_past, small_send)
+    large_got = swap(large_part, *large_routes[2])
     chain_small(2, large_part)
     large_part = join(large_part, large_got, small_send)
-    large_got = swap(large_part, *large_routes[2])
-    chain_small(3, large_part)
-    large_part = join(large_part, large_got, small_send)
     large_got = swap(large_part, *large_routes[1])
-    small_part = blend(small_keep, small_got, small_past, large_part)
-    small_got = swap(small_part, *small_routes[3])
-    small_part = join(small_part, small_got, large_part)
+    small_total = rounded_total(small_keep, small_got, large_part)
+    small_got = swap(small_total, *small_routes[3])
+    large_part = join(large_part, large_got, small_total)
+    large_got = swap(large_part, *large_routes[0])
+    small_part = blend(small_total, small_got, small_past, large_part, work=8e9)
     small_got = swap(small_part, *small_routes[2])
-    large_part = join(large_part, large_got, small_part)
-    large_got = swap(large_part, *large_routes[0])
-    small_part = join(small_part, small_got, large_part)
+    small_part = join(small_part, small_got, work=1e3)
     small_got = swap(small_part, *small_routes[1])
 
     any_space = pl.BlockSpec(memory_space=pl.ANY)
@@ -1140,20 +1166,20 @@
         in_specs=[SMEM, VMEM, VMEM, any_space],
         out_specs=(VMEM,) * 2,
         scratch_shapes=[pltpu.VMEM((D, D), bf16)],
-        cost_estimate=cost(5e9, 6e6),
+        cost_estimate=cost(1e3, 1e3),
         name="ortho_large",
         compiler_params=room(10),
     )(scalars, large_part.reshape(gathered_shape), large_got.reshape(gathered_shape), small_part)
+    mix_got = swap(large_mix, 2)
     small_part = join(small_part, small_got, large_work)
     small_got = swap(small_part, *small_routes[0])
-    mix_got = swap(large_mix, 2)
     large_result = pl.pallas_call(
         large_next_kernel,
         out_shape=struct((2, D, CHUNK), bf16),
         in_specs=[VMEM, any_space],
         out_specs=VMEM,
         scratch_shapes=[pltpu.VMEM((4, D, CHUNK), bf16), pltpu.VMEM((D, D), bf16)],
-        cost_estimate=cost(5e9, 4e6),
+        cost_estimate=cost(1e3, 1e3),
         name="ortho_large",
         compiler_params=room(10),
     )(large_work, small_part)
@@ -1171,20 +1197,21 @@
         out_shape=large_shapes + (small_token,),
         in_specs=[SMEM, across, across, left_right, top_bottom, any_space],
         out_specs=(left_right, top_bottom, token_block),
-        cost_estimate=cost(1e7, 1e7),
+        cost_estimate=cost(1e3, 1e3),
         name="moment_large",
         compiler_params=room(8),
     )(scalars, large_mix, mix_got, up_moment, down_moment, large_result)
-    small_work, small_mix, table_own = pl.pallas_call(
+
+    small_work, small_mix = pl.pallas_call(
         small_start_kernel,
         out_shape=(
             struct((2, 2, 256, D), bf16),
-            struct((2, 256, D), bf16),
-            struct((8, D), f32),
+            struct((2, 256 + TABLE_ROWS, D), bf16),
         ),
         in_specs=[SMEM, VMEM, VMEM, any_space],
-        out_specs=(VMEM,) * 3,
-        cost_estimate=cost(1e6, 4e6),
+        out_specs=(VMEM,) * 2,
+        scratch_shapes=[pltpu.VMEM((TABLE_ROWS, D), f32)],
+        cost_estimate=cost(3e10, 1e3),
         name="unpack_small",
         compiler_params=room(6),
     )(
@@ -1193,19 +1220,7 @@
         small_got.reshape(2, 2, 2, 80, D),
         moments_done,
     )
-    small_result = pl.pallas_call(
-        small_kernel,
-        out_shape=struct((2, 256, D), bf16),
-        in_specs=[VMEM],
-        out_specs=VMEM,
-        scratch_shapes=[pltpu.VMEM((2, 256, D), bf16)] * 2 + [pltpu.VMEM((D, D), bf16)] * 2,
-        cost_estimate=cost(6e9, 4e6),
-        name="ortho_small",
-        compiler_params=room(10),
-    )(small_work)
-    small_other = swap(small_result, 2)
     mix_other = swap(small_mix, 2)
-    table_other = swap(table_own, 2)
 
     def fixed(*shape):
         return pl.BlockSpec(shape, lambda g: (0,) * len(shape))
@@ -1213,40 +1228,47 @@
     def one(index):
         return pl.BlockSpec((1, 256, D), index)
 
-    up_new, down_new, attention_moment_new, modulation_moment_new, modulation_new, large_done = pl.pallas_call(
-        functools.partial(large_weight_kernel, nodes=row_count * device_count),
+    small_result, up_new, down_new = pl.pallas_call(
+        small_kernel,
+        grid=(NS_STEPS,),
+        out_shape=(struct((2, 256, D), bf16),) + large_shapes,
+        in_specs=[SMEM, fixed(2, 2, 256, D), across, across, left_right, top_bottom, any_space],
+        out_specs=(fixed(2, 256, D), left_right, top_bottom),
+        scratch_shapes=[pltpu.VMEM((2, 256, D), bf16)] * 2
+        + [pltpu.VMEM((D, D), bf16)] * 2
+        + [pltpu.SMEM((2,), f32)],
+        cost_estimate=cost(6e9, 1e7),
+        name="ortho_small",
+        compiler_params=room(16),
+    )(scalars, small_work, large_result, result_got, up_weight, down_weight, moments_done)
+    small_other = swap(small_result, 2)
+    table_block = pl.BlockSpec((1, TABLE_ROWS, D), lambda g: (0, 256 // TABLE_ROWS, 0))
+    attention_moment_new, modulation_moment_new, modulation_new, moment_done = pl.pallas_call(
+        functools.partial(small_moment_kernel, nodes=row_count * device_count),
         grid=(4,),
-        out_shape=large_shapes + (struct((4, 256, D), f32),) + (struct((2, 2, D), f32),) * 2 + (small_token,),
+        out_shape=(struct((4, 256, D), f32),) + (struct((2, 2, D), f32),) * 2 + (small_token,),
         in_specs=[
             SMEM,
-            across,
-            across,
-            left_right,
-            top_bottom,
             one(lambda g: (g % 2, 0, 0)),
             one(lambda g: (g % 2, 0, 0)),
             one(lambda g: (g, 0, 0)),
-            fixed(8, D),
-            fixed(8, D),
+            table_block,
+            table_block,
             fixed(2, 4, D),
             fixed(2, 2, D),
             any_space,
         ],
-        out_specs=(left_right, top_bottom, one(lambda g: (g, 0, 0)), fixed(2, 2, D), fixed(2, 2, D), token_block),
-        cost_estimate=cost(1e7, 2e7),
-        name="update_large",
-        compiler_params=room(12),
+        out_specs=(one(lambda g: (g, 0, 0)), fixed(2, 2, D), fixed(2, 2, D), token_block),
+        cost_estimate=cost(1e10, 1e7),
+        name="moment_small",
+        compiler_params=room(8),
     )(
         scalars,
-        large_result,
-        result_got,
-        up_weight,
-        down_weight,
         small_mix,
         mix_other,
         attention_moment,
-        table_own,
-        table_other,
+        small_mix,
+        mix_other,
         modulation,
         modulation_moment,
         small_result,
@@ -1268,7 +1290,7 @@
         cost_estimate=cost(1e7, 6e6),
         name="update_small",
         compiler_params=room(6),
-    )(scalars, small_result, small_other, attention_weight, large_done)
+    )(scalars, small_result, small_other, attention_weight, moment_done)
     return (
         output,
         features_grad,

time: 185 us -> 177 us (0.957)
  waiting for transfers between devices: 48.5 us -> 38.3 us
    ppermute x26 -> x23, waiting for transfers between devices: 46.6 us -> 36.6 us  [swap(): return lax.ppermute(value, AXES, pairs)]
    unnamed x34 -> x36, local copies, waits for them, and re-layouts: 4.81 us -> 5.98 us
    ppermute x26 -> x23, starting transfers between devices: 29.9 us -> 30.2 us  [swap(): return lax.ppermute(value, AXES, pairs)]
  transfers between devices with their start and end apart: 30 -> 27, of which waited for: 15 -> 14; matrix products, arithmetic and copies ran while one was open for 0% -> 0% of each run, Pallas kernels for 44% -> 46%
where the time goes in v1:
time: 177 us
  Pallas kernels  85.2 us (48%)
  starting transfers between devices  42.6 us (24%)
  waiting for transfers between devices  38.3 us (22%)
  local copies, waits for them, and re-layouts  7.14 us (4%)
  other arithmetic  2.71 us (2%)
    ppermute x23, waiting for transfers between devices, swap(): return lax.ppermute(value, AXES, pairs)  36.6 us
    ppermute x23, starting transfers between devices, swap(): return lax.ppermute(value, AXES, pairs)  30.2 us
    ppermute x4, starting transfers between devices, along(): return lax.ppermute(value, AXES, pairs)  12.4 us
    pallas_call x1, Pallas kernels, on_device(): pl.pallas_call(small_kernel, grid=(NS_STEPS,), out_shape=(struct((2, 256,...  11.3 us
    pallas_call x1, Pallas kernels, on_device(): pl.pallas_call(forward_kernel, out_shape=(struct((row_count, D), bf16), s...  9.94 us
    pallas_call x1, Pallas kernels, on_device(): pl.pallas_call(backward_kernel, out_shape=(struct((row_count, D), bf16),)...  8.72 us
    pallas_call x1, Pallas kernels, on_device(): pl.pallas_call(weights_kernel, out_shape=(struct((row_count, D), f32), pi...  8.28 us
    pallas_call x1, Pallas kernels, on_device(): pl.pallas_call(mlp_own_kernel, out_shape=(struct((row_count, D), f32), st...  6.78 us
  transfers between devices with their start and end apart: 27, of which 14 were waited for; matrix products, arithmetic and copies ran while one was open for 0% of the time, Pallas kernels for 46%

profile of v1, /device:TPU:0, one launch (start us, length us, event | category | flops | bytes accessed | tf_op | source)
XLA Modules:
  0.0 177.0 jit_solution(10282473278693712647)
XLA Ops:
  0.7 0.9 broadcast_subtract_fusion
  1.8 0.8 broadcast_in_dim.16
  2.6 0.9 fusion
  3.7 0.8 pad_maximum_fusion
  4.5 1.3 collective-permute-start.1
  5.8 6.2 %collective-permute-start = (bf16[192,640]{1,0:T(8,128)(2,1)}, bf16[192,640]{1,0:T(8,128)(2,1)}, u32[]{:S(2)}, u32[]{:S(2)}) collective-permute-start(bf16[192,640]{1,0:T(8,128)(2,1)} %get-tuple-element.145), channel_id=1, source_target_pairs={{0,1},{1,2},{2,3},{3,4},{4,5},{5,6},{6,7},{7,8},{8,9},{9,10},{10,1... | collective-permute-start | bytes 737288 | tf_op jit(solution)/shard_map/ppermute | solution.py:769
  12.1 1.6 copy-done.7
  13.7 1.6 copy-done.10
  15.3 0.6 quarter.1
  15.9 0.9 copy-done
  16.9 0.6 copy-done.2
  17.5 0.8 past.1
  18.3 1.8 collective-permute-done.rim_low
  20.0 2.5 %collective-permute-start.2 = (bf16[2,512,512]{2,1,0:T(8,128)(2,1)S(1)}, bf16[2,512,512]{2,1,0:T(8,128)(2,1)S(1)}, u32[]{:S(2)}, u32[]{:S(2)}) collective-permute-start(bf16[2,512,512]{2,1,0:T(8,128)(2,1)S(1)} %quarter.1), channel_id=1, source_target_pairs={{0,1},{1,0},{2,3},{3,2},{4,5},{5,4},{6,7},{7,6},{8,9},{9,8},{10,11... | collective-permute-start | bytes 3145736 | tf_op jit(solution)/shard_map/ppermute | solution.py:777
  22.5 5.9 %project.1 = (bf16[768,512]{1,0:T(8,128)(2,1)S(1)}, bf16[3,768,512]{2,1,0:T(8,128)(2,1)S(1)}, bf16[768,512]{1,0:T(8,128)(2,1)S(1)}, bf16[4,512,512]{2,1,0:T(8,128)(2,1)S(1)}) custom-call(bf16[768,512]{1,0:T(8,128)(2,1)S(1)} %copy-done.13, f32[768,128]{1,0:T(8,128)S(1)} %get-tuple-element.77.pack, f32[2,4,512]{2,1,0:T(4,128)S(1)} %copy-done.15, ...), custom_call_target="tpu_custom_call" | custom-call | flops 4000000000 | bytes 4000000 | tf_op jit(solution)/shard_map/project/pallas_call | solution.py:828
  28.5 9.9 %attend.1 = (bf16[768,512]{1,0:T(8,128)(2,1)S(1)}, f32[768,512]{1,0:T(8,128)S(1)}, bf16[768,512]{1,0:T(8,128)(2,1)S(1)}, bf16[2,1152,512]{2,1,0:T(8,128)(2,1)S(1...) custom-call(bf16[192,640]{1,0:T(8,128)(2,1)} %collective-permute-done.rim_low, ...), custom_call_target="tpu_custom_call" | custom-call | flops 6000000000 | bytes 8000000 | tf_op jit(solution)/shard_map/attend/pallas_call | solution.py:856
  38.5 6.8 %mlp_own.1 = (f32[768,512]{1,0:T(8,128)S(1)}, f32[768,512]{1,0:T(8,128)S(1)}, bf16[2,2,2,128,512]{4,3,2,1,0:T(8,128)(2,1)S(1)}, bf16[2,2,2,128,512]{4,3,2,1,0:T(8,128)(2,1)S(1)}) custom-call(s32[5]{0:T(128)S(1)} %stack.23.scalars, bf16[768,512]{1,0:T(8,128)(2,1)S(1)} %get-tuple-element.81.second_in, bf16[768,512]{1,0:T(8,128)(2,1)S(1)} %copy-done.14, ...), custom_call_target="tpu_custom_call" | custom-call | flops 5000000000 | bytes 8000000 | tf_op jit(solution)/shard_map/mlp_own/pallas_call | solution.py:879
  45.2 1.1 collective-permute-done.2.near
  46.3 0.5 collective-permute-start.4
  46.9 3.4 %mlp_near.1 = (f32[768,512]{1,0:T(8,128)S(1)}, f32[768,512]{1,0:T(8,128)S(1)}, bf16[2,2,2,128,512]{4,3,2,1,0:T(8,128)(2,1)S(1)}, bf16[2,2,2,128,512]{4,3,2,1,0:T(8,128)(2,1)S(1)}) custom-call(s32[5]{0:T(128)S(1)} %stack.23.scalars, bf16[768,512]{1,0:T(8,128)(2,1)S(1)} %get-tuple-element.81.second_in, bf16[768,512]{1,0:T(8,128)(2,1)S(1)} %copy-done.14, ...), custom_call_target="tpu_custom_call" | custom-call | flops 2500000000 | bytes 4000000 | tf_op jit(solution)/shard_map/mlp_near/pallas_call | solution.py:909
  50.3 5.8 %mlp_far.1 = (bf16[2,2,2,128,512]{4,3,2,1,0:T(8,128)(2,1)S(1)}, bf16[2,2,2,128,512]{4,3,2,1,0:T(8,128)(2,1)S(1)}, bf16[768,512]{1,0:T(8,128)(2,1)}, f32[768,512]...) custom-call(s32[5]{0:T(128)S(1)} %stack.23.scalars, ...), custom_call_target="tpu_custom_call", output_to_operand_aliasing={{0}: (12, {}), {1}: (13, {})} | custom-call | flops 4000000000 | bytes 8000000 | tf_op jit(solution)/shard_map/mlp_far/pallas_call | solution.py:940
  56.1 2.6 %collective-permute-done.5.rest_got = bf16[2,2,2,128,512]{4,3,2,1,0:T(8,128)(2,1)S(1)} collective-permute-done((bf16[2,2,2,128,512]{4,3,2,1,0:T(8,128)(2,1)S(1)}, bf16[2,2,2,128,512]{4,3,2,1,0:T(8,128)(2,1)S(1)}, u32[]{:S(2)}, u32[]{:S(2)}) %collective-permute-start.5) | collective-permute-done | bytes 1048608 | tf_op jit(solution)/shard_map/ppermute | solution.py:777
  58.7 1.0 large_sum.1
  59.7 1.8 %collective-permute-start.6 = (bf16[2,2,2,128,512]{4,3,2,1,0:T(8,128)(2,1)S(1)}, bf16[2,2,2,128,512]{4,3,2,1,0:T(8,128)(2,1)S(1)}, u32[]{:S(2)}, u32[]{:S(2)}) collective-permute-start(bf16[2,2,2,128,512]{4,3,2,1,0:T(8,128)(2,1)S(1)} %get-tuple-element.100.token), channel_id=1, source_target_pairs={{0,4},{1,5},{2,10},{3,11},{4,0},{5,1},{6,14},{7,15},{8,12},{9,13},... | collective-permute-start | bytes 3145736 | tf_op jit(solution)/shard_map/ppermute | solution.py:777
  61.5 3.7 %collective-permute-start.7 = (bf16[192,640]{1,0:T(8,128)(2,1)S(1)}, bf16[192,640]{1,0:T(8,128)(2,1)S(1)}, u32[]{:S(2)}, u32[]{:S(2)}) collective-permute-start(bf16[192,640]{1,0:T(8,128)(2,1)S(1)} %get-tuple-element.110), channel_id=1, source_target_pairs={{0,1},{1,2},{2,3},{3,4},{4,5},{5,6},{6,7},{7,8},{8,9},{9,10},{10,1... | collective-permute-start | bytes 737288 | tf_op jit(solution)/shard_map/ppermute | solution.py:769
  65.2 1.3 collective-permute-start.8
  66.5 8.7 %attend_back.1 = (bf16[768,512]{1,0:T(8,128)(2,1)S(1)}, f32[1152,512]{1,0:T(8,128)S(1)}, f32[1152,512]{1,0:T(8,128)S(1)}) custom-call(bf16[3,768,512]{2,1,0:T(8,128)(2,1)S(1)} %get-tuple-element.79.qkv, bf16[2,1152,512]{2,1,0:T(8,128)(2,1)S(1)} %get-tuple-element.101.padded, bf16[768,512]{1,0:T(8,128)(2,1)S(1)} %get-tuple-element.102.grad, ...), custom_call_target="tpu_custom_call" | custom-call | flops 8000000000 | bytes 9000000 | tf_op jit(solution)/shard_map/attend_back/pallas_call | solution.py:1083
  75.2 1.3 collective-permute-done.6
  76.6 2.6 %collective-permute-start.10 = (bf16[2,256,512]{2,1,0:T(8,128)(2,1)S(1)}, bf16[2,256,512]{2,1,0:T(8,128)(2,1)S(1)}, u32[]{:S(2)}, u32[]{:S(2)}) collective-permute-start(bf16[2,256,512]{2,1,0:T(8,128)(2,1)S(1)} %bitcast.47), channel_id=1, source_target_pairs={{0,1},{1,0},{2,6},{3,7},{4,5},{5,4},{6,2},{7,3},{8,9},{9,8},{10,14... | collective-permute-start | bytes 1572872 | tf_op jit(solution)/shard_map/ppermute | solution.py:777
  79.2 8.3 %attend_weights.1 = (f32[768,512]{1,0:T(8,128)}, bf16[2,2,2,2,80,512]{5,4,3,2,1,0:T(8,128)(2,1)S(1)}, bf16[2,2,2,2,80,512]{5,4,3,2,1,0:T(8,128)(2,1)S(1)}) custom-call(s32[5]{0:T(128)S(1)} %stack.23.scalars, bf16[2,256,512]{2,1,0:T(8,128)(2,1)S(1)} %bitcast.48, bf16[768,512]{1,0:T(8,128)(2,1)S(1)} %get-tuple-element.104.refs_2_.queries_in, ...), custom_call_target="tpu_custom_call" | custom-call | flops 6000000000 | bytes 9000000 | tf_op jit(solution)/shard_map/attend_weights/pallas_call | solution.py:1095
  87.6 1.6 collective-permute-start.12
  89.3 1.3 collective-permute-done.9
  90.5 0.3 receive.7
  90.8 1.8 %collective-permute-start.11 = (bf16[2,320,512]{2,1,0:T(8,128)(2,1)S(1)}, bf16[2,320,512]{2,1,0:T(8,128)(2,1)S(1)}, u32[]{:S(2)}, u32[]{:S(2)}) collective-permute-start(bf16[2,320,512]{2,1,0:T(8,128)(2,1)S(1)} %bitcast.45), channel_id=1, source_target_pairs={{0,4},{1,5},{2,10},{3,11},{4,0},{5,1},{6,14},{7,15},{8,12},{9,13},... | collective-permute-start | bytes 1966088 | tf_op jit(solution)/shard_map/ppermute | solution.py:777
  92.6 1.9 %collective-permute-done.12.refs_1_ = bf16[2,128,512]{2,1,0:T(8,128)(2,1)S(1)} collective-permute-done((bf16[2,128,512]{2,1,0:T(8,128)(2,1)S(1)}, bf16[2,128,512]{2,1,0:T(8,128)(2,1)S(1)}, u32[]{:S(2)}, u32[]{:S(2)}) %collective-permute-start.12) | collective-permute-done | bytes 262176 | tf_op jit(solution)/shard_map/ppermute | solution.py:777
  94.6 2.7 %collective-permute-start.14 = (bf16[2,128,512]{2,1,0:T(8,128)(2,1)S(1)}, bf16[2,128,512]{2,1,0:T(8,128)(2,1)S(1)}, u32[]{:S(2)}, u32[]{:S(2)}) collective-permute-start(bf16[2,128,512]{2,1,0:T(8,128)(2,1)S(1)} %total.2.refs_2_.refs_0_), channel_id=1, source_target_pairs={{0,16},{1,17},{2,18},{3,19},{4,20},{5,21},{6,22},{7,23},{8,24},{9,... | collective-permute-start | bytes 786440 | tf_op jit(solution)/shard_map/ppermute | solution.py:777
  97.2 4.2 %collective-permute-done.11.refs_1_ = bf16[2,320,512]{2,1,0:T(8,128)(2,1)S(1)} collective-permute-done((bf16[2,320,512]{2,1,0:T(8,128)(2,1)S(1)}, bf16[2,320,512]{2,1,0:T(8,128)(2,1)S(1)}, u32[]{:S(2)}, u32[]{:S(2)}) %collective-permute-start.11) | collective-permute-done | bytes 655392 | tf_op jit(solution)/shard_map/ppermute | solution.py:777
  101.7 4.1 %collective-permute-done.14.refs_1_ = bf16[2,128,512]{2,1,0:T(8,128)(2,1)S(1)} collective-permute-done((bf16[2,128,512]{2,1,0:T(8,128)(2,1)S(1)}, bf16[2,128,512]{2,1,0:T(8,128)(2,1)S(1)}, u32[]{:S(2)}, u32[]{:S(2)}) %collective-permute-start.14) | collective-permute-done | bytes 262176 | tf_op jit(solution)/shard_map/ppermute | solution.py:777
  105.9 3.4 %collective-permute-start.16 = (bf16[256,512]{1,0:T(8,128)(2,1)S(1)}, bf16[256,512]{1,0:T(8,128)(2,1)S(1)}, u32[]{:S(2)}, u32[]{:S(2)}) collective-permute-start(bf16[256,512]{1,0:T(8,128)(2,1)S(1)} %bitcast.54), channel_id=1, source_target_pairs={{0,8},{1,9},{2,3},{3,2},{4,12},{5,13},{6,7},{7,6},{8,0},{9,1},{10,... | collective-permute-start | bytes 786440 | tf_op jit(solution)/shard_map/ppermute | solution.py:777
  109.4 2.2 %collective-permute-start.15 = (bf16[2,80,512]{2,1,0:T(8,128)(2,1)S(1)}, bf16[2,80,512]{2,1,0:T(8,128)(2,1)S(1)}, u32[]{:S(2)}, u32[]{:S(2)}) collective-permute-start(bf16[2,80,512]{2,1,0:T(8,128)(2,1)S(1)} %bitcast.59), channel_id=1, source_target_pairs={{0,8},{1,9},{2,6},{3,7},{4,12},{5,13},{6,2},{7,3},{8,0},{9,1},{10,... | collective-permute-start | bytes 491528 | tf_op jit(solution)/shard_map/ppermute | solution.py:777
  111.6 2.1 %collective-permute-done.16.refs_1_ = bf16[256,512]{1,0:T(8,128)(2,1)S(1)} collective-permute-done((bf16[256,512]{1,0:T(8,128)(2,1)S(1)}, bf16[256,512]{1,0:T(8,128)(2,1)S(1)}, u32[]{:S(2)}, u32[]{:S(2)}) %collective-permute-start.16) | collective-permute-done | bytes 262176 | tf_op jit(solution)/shard_map/ppermute | solution.py:777
  113.7 1.0 collective-permute-start.18
  114.7 0.7 collective-permute-done.15.refs_1_
  115.5 3.4 %collective-permute-start.17 = (bf16[2,80,512]{2,1,0:T(8,128)(2,1)S(1)}, bf16[2,80,512]{2,1,0:T(8,128)(2,1)S(1)}, u32[]{:S(2)}, u32[]{:S(2)}) collective-permute-start(bf16[2,80,512]{2,1,0:T(8,128)(2,1)S(1)} %total.3.refs_2_.refs_0_), channel_id=1, source_target_pairs={{0,16},{1,17},{2,18},{3,19},{4,20},{5,21},{6,22},{7,23},{8,24},{9,... | collective-permute-start | bytes 491528 | tf_op jit(solution)/shard_map/ppermute | solution.py:777
  118.9 4.0 %collective-permute-done.18.refs_1_ = bf16[512,512]{1,0:T(8,128)(2,1)S(1)} collective-permute-done((bf16[512,512]{1,0:T(8,128)(2,1)S(1)}, bf16[512,512]{1,0:T(8,128)(2,1)S(1)}, u32[]{:S(2)}, u32[]{:S(2)}) %collective-permute-start.18) | collective-permute-done | bytes 524320 | tf_op jit(solution)/shard_map/ppermute | solution.py:777
  123.0 0.7 collective-permute-start.21
  123.7 2.8 %collective-permute-done.17.refs_1_ = bf16[2,80,512]{2,1,0:T(8,128)(2,1)S(1)} collective-permute-done((bf16[2,80,512]{2,1,0:T(8,128)(2,1)S(1)}, bf16[2,80,512]{2,1,0:T(8,128)(2,1)S(1)}, u32[]{:S(2)}, u32[]{:S(2)}) %collective-permute-start.17) | collective-permute-done | bytes 163872 | tf_op jit(solution)/shard_map/ppermute | solution.py:777
  126.6 1.3 collective-permute-start.19
  127.9 5.8 %collective-permute-done.19.refs_1_ = bf16[160,512]{1,0:T(8,128)(2,1)S(1)} collective-permute-done((bf16[160,512]{1,0:T(8,128)(2,1)S(1)}, bf16[160,512]{1,0:T(8,128)(2,1)S(1)}, u32[]{:S(2)}, u32[]{:S(2)}) %collective-permute-start.19) | collective-permute-done | bytes 163872 | tf_op jit(solution)/shard_map/ppermute | solution.py:777
  133.8 1.4 collective-permute-start.20
  135.1 4.5 %collective-permute-done.21 = bf16[1024,512]{1,0:T(8,128)(2,1)S(1)} collective-permute-done((bf16[1024,512]{1,0:T(8,128)(2,1)S(1)}, bf16[1024,512]{1,0:T(8,128)(2,1)S(1)}, u32[]{:S(2)}, u32[]{:S(2)}) %collective-permute-start.21) | collective-permute-done | bytes 1048608 | tf_op jit(solution)/shard_map/ppermute | solution.py:777
  139.6 6.5 %ortho_large.2 = (bf16[4,512,512]{2,1,0:T(8,128)(2,1)S(1)}, bf16[2,512,512]{2,1,0:T(8,128)(2,1)S(1)}) custom-call(s32[5]{0:T(128)S(1)} %stack.23.scalars, bf16[2,2,2,128,512]{4,3,2,1,0:T(8,128)(2,1)S(1)} %bitcast.34, bf16[2,2,2,128,512]{4,3,2,1,0:T(8,128)(2,1)S(1)} %bitcast.35, bf16[320,512]{1,0:T(8,128)(2,1)S(1)} %bitcast.30), custom_call_target="tpu_custom_call" | custom-call | flops 1000 | bytes 1000 | tf_op jit(solution)/shard_map/ortho_large/pallas_call | solution.py:1163
  146.1 1.0 collective-permute-start.23
  147.2 1.2 collective-permute-start.22
  148.4 5.9 %ortho_large.3.token.own = bf16[2,512,512]{2,1,0:T(8,128)(2,1)S(1)} custom-call(bf16[4,512,512]{2,1,0:T(8,128)(2,1)S(1)} %get-tuple-element.128.refs_2_.given, bf16[640,512]{1,0:T(8,128)(2,1)S(1)} %bitcast.37), custom_call_target="tpu_custom_call" | custom-call | flops 1000 | bytes 1000 | tf_op jit(solution)/shard_map/ortho_large/pallas_call | solution.py:1176
  154.6 3.3 %moment_large.1 = (f32[512,1024]{1,0:T(8,128)}, f32[1024,512]{1,0:T(8,128)}, f32[8,128]{1,0:T(8,128)S(1)}) custom-call(s32[5]{0:T(128)S(1)} %stack.23.scalars, bf16[2,512,512]{2,1,0:T(8,128)(2,1)S(1)} %get-tuple-element.129.own, bf16[2,512,512]{2,1,0:T(8,128)(2,1)S(1)} %collective-permute-done.23.got, f32[512,1024]{1,0:T(8,128)S(1)} %copy-done.1, ...), custom_call_target="tpu_custom_call" | custom-call | flops 1000 | bytes 1000 | tf_op jit(solution)/shard_map/moment_large/pallas_call | solution.py:1194
  157.9 0.7 unpack_small.1
  158.6 0.4 collective-permute-start.24
  159.0 0.5 copy-done.9
  159.5 0.6 copy-done.12
  160.1 11.3 %ortho_small.1 = (bf16[2,256,512]{2,1,0:T(8,128)(2,1)S(1)}, f32[512,1024]{1,0:T(8,128)}, f32[1024,512]{1,0:T(8,128)}) custom-call(s32[5]{0:T(128)S(1)} %stack.23.scalars, bf16[2,2,256,512]{3,2,1,0:T(8,128)(2,1)S(1)} %get-tuple-element.132.given, bf16[2,512,512]{2,1,0:T(8,128)(2,1)S(1)} %ortho_large.3.token.own, ...), custom_call_target="tpu_custom_call" | custom-call | flops 6000000000 | bytes 10000000 | tf_op jit(solution)/shard_map/ortho_small/pallas_call | solution.py:1231
  171.4 0.3 collective-permute-start.26
  171.7 2.6 %moment_small.1 = (f32[4,256,512]{2,1,0:T(8,128)}, f32[2,2,512]{2,1,0:T(2,128)}, f32[2,2,512]{2,1,0:T(2,128)}, f32[8,128]{1,0:T(8,128)S(1)}) custom-call(s32[5]{0:T(128)S(1)} %stack.23.scalars, bf16[2,272,512]{2,1,0:T(8,128)(2,1)S(1)} %get-tuple-element.131.mix.table, bf16[2,272,512]{2,1,0:T(8,128)(2,1)S(1)} %collective-permute-done.24.mix_got.table_got, ...), custom_call_target="tpu_custom_call" | custom-call | flops 10000000000 | bytes 10000000 | tf_op jit(solution)/shard_map/moment_small/pallas_call | solution.py:1246
  174.4 2.6 %update_small.1 = f32[4,256,512]{2,1,0:T(8,128)} custom-call(s32[5]{0:T(128)S(1)} %stack.23.scalars, bf16[2,256,512]{2,1,0:T(8,128)(2,1)S(1)} %get-tuple-element.133.token.own, bf16[2,256,512]{2,1,0:T(8,128)(2,1)S(1)} %collective-permute-done.26.got, f32[4,512,512]{2,1,0:T(8,128)S(1)} %copy-done.5, f32[8,128]{1,0:T(8,128)S(1)} %get-tuple-element.135.token), custom_call_target="tpu_custom_call" | custom-call | flops 10000000 | bytes 6000000 | tf_op jit(solution)/shard_map/update_small/pallas_call | solution.py:1276
  (66 shorter events, 2.0 us)
Async XLA Ops:
  0.6 3.0 %copy-start.13 = (bf16[768,512]{1,0:T(8,128)(2,1)S(1)}, bf16[768,512]{1,0:T(8,128)(2,1)}, u32[]{:S(2)}) copy-start(bf16[768,512]{1,0:T(8,128)(2,1)} %features.5) | copy-start | bytes 2359300
  3.7 12.3 %copy-start.6 = (f32[4,256,512]{2,1,0:T(8,128)S(1)}, f32[4,256,512]{2,1,0:T(8,128)}, u32[]{:S(2)}) copy-start(f32[4,256,512]{2,1,0:T(8,128)} %moment.1) | copy-start | bytes 6291460
  4.5 13.8 %collective-permute-start.1 = (bf16[192,640]{1,0:T(8,128)(2,1)}, bf16[192,640]{1,0:T(8,128)(2,1)S(1)}, u32[]{:S(2)}, u32[]{:S(2)}) collective-permute-start(bf16[192,640]{1,0:T(8,128)(2,1)} %get-tuple-element.144), channel_id=1, source_target_pairs={{1,0},{2,1},{3,2},{4,3},{5,4},{6,5},{7,6},{8,7},{9,8},{10,9},{11,1... | collective-permute-start | bytes 737288 | tf_op jit(solution)/shard_map/ppermute | solution.py:769
  5.8 14.2 %collective-permute-start = (bf16[192,640]{1,0:T(8,128)(2,1)}, bf16[192,640]{1,0:T(8,128)(2,1)}, u32[]{:S(2)}, u32[]{:S(2)}) collective-permute-start(bf16[192,640]{1,0:T(8,128)(2,1)} %get-tuple-element.145), channel_id=1, source_target_pairs={{0,1},{1,2},{2,3},{3,4},{4,5},{5,6},{6,7},{7,8},{8,9},{9,10},{10,1... | collective-permute-start | bytes 737288 | tf_op jit(solution)/shard_map/ppermute | solution.py:769
  12.1 1.6 copy-start.7
  13.7 1.6 copy-start.10
  15.3 1.6 copy-start
  15.3 2.2 %copy-start.2 = (f32[1024,512]{1,0:T(8,128)S(1)}, f32[1024,512]{1,0:T(8,128)}, u32[]{:S(2)}) copy-start(f32[1024,512]{1,0:T(8,128)} %down_moment.1) | copy-start | bytes 6291460
  17.5 5.0 %copy-start.4 = (f32[4,512,512]{2,1,0:T(8,128)S(1)}, f32[4,512,512]{2,1,0:T(8,128)}, u32[]{:S(2)}) copy-start(f32[4,512,512]{2,1,0:T(8,128)} %weight.1) | copy-start | bytes 12582916
  17.5 5.0 %copy-start.15 = (f32[2,4,512]{2,1,0:T(4,128)S(1)}, f32[2,4,512]{2,1,0:T(4,128)}, u32[]{:S(2)}) copy-start(f32[2,4,512]{2,1,0:T(4,128)} %modulation.1) | copy-start | bytes 49156
  20.0 26.3 %collective-permute-start.2 = (bf16[2,512,512]{2,1,0:T(8,128)(2,1)S(1)}, bf16[2,512,512]{2,1,0:T(8,128)(2,1)S(1)}, u32[]{:S(2)}, u32[]{:S(2)}) collective-permute-start(bf16[2,512,512]{2,1,0:T(8,128)(2,1)S(1)} %quarter.1), channel_id=1, source_target_pairs={{0,1},{1,0},{2,3},{3,2},{4,5},{5,4},{6,7},{7,6},{8,9},{9,8},{10,11... | collective-permute-start | bytes 3145736 | tf_op jit(solution)/shard_map/ppermute | solution.py:777
  28.4 10.0 %copy-start.8 = (f32[512,1024]{1,0:T(8,128)S(1)}, f32[512,1024]{1,0:T(8,128)}, u32[]{:S(2)}) copy-start(f32[512,1024]{1,0:T(8,128)} %up_weight.1) | copy-start | bytes 6291460
  28.4 10.0 %copy-start.11 = (f32[1024,512]{1,0:T(8,128)S(1)}, f32[1024,512]{1,0:T(8,128)}, u32[]{:S(2)}) copy-start(f32[1024,512]{1,0:T(8,128)} %down_weight.1) | copy-start | bytes 6291460
  28.5 10.0 %copy-start.14 = (bf16[768,512]{1,0:T(8,128)(2,1)S(1)}, bf16[768,512]{1,0:T(8,128)(2,1)}, u32[]{:S(2)}) copy-start(bf16[768,512]{1,0:T(8,128)(2,1)} %cotangent.5) | copy-start | bytes 2359300
  46.3 3.9 %collective-permute-start.3 = (bf16[2,512,512]{2,1,0:T(8,128)(2,1)S(1)}, bf16[2,512,512]{2,1,0:T(8,128)(2,1)S(1)}, u32[]{:S(2)}, u32[]{:S(2)}) collective-permute-start(bf16[2,512,512]{2,1,0:T(8,128)(2,1)S(1)} %collective-permute-done.2.near), channel_id=1, source_target_pairs={{0,2},{1,3},{2,0},{3,1},{4,6},{5,7},{6,4},{7,5},{8,10},{9,11},{10,... | collective-permute-start | bytes 3145736 | tf_op jit(solution)/shard_map/ppermute | solution.py:777
  46.3 9.7 %collective-permute-start.4 = (bf16[2,2,2,128,512]{4,3,2,1,0:T(8,128)(2,1)S(1)}, bf16[2,2,2,128,512]{4,3,2,1,0:T(8,128)(2,1)S(1)}, u32[]{:S(2)}, u32[]{:S(2)}) collective-permute-start(bf16[2,2,2,128,512]{4,3,2,1,0:T(8,128)(2,1)S(1)} %get-tuple-element.96), channel_id=1, source_target_pairs={{0,2},{1,3},{2,0},{3,1},{4,6},{5,7},{6,4},{7,5},{8,10},{9,11},{10,... | collective-permute-start | bytes 3145736 | tf_op jit(solution)/shard_map/ppermute | solution.py:777
  56.0 2.7 %collective-permute-start.5 = (bf16[2,2,2,128,512]{4,3,2,1,0:T(8,128)(2,1)S(1)}, bf16[2,2,2,128,512]{4,3,2,1,0:T(8,128)(2,1)S(1)}, u32[]{:S(2)}, u32[]{:S(2)}) collective-permute-start(bf16[2,2,2,128,512]{4,3,2,1,0:T(8,128)(2,1)S(1)} %get-tuple-element.98), channel_id=1, source_target_pairs={{0,2},{1,3},{2,0},{3,1},{4,6},{5,7},{6,4},{7,5},{8,10},{9,11},{10,... | collective-permute-start | bytes 3145736 | tf_op jit(solution)/shard_map/ppermute | solution.py:777
  59.7 16.7 %collective-permute-start.6 = (bf16[2,2,2,128,512]{4,3,2,1,0:T(8,128)(2,1)S(1)}, bf16[2,2,2,128,512]{4,3,2,1,0:T(8,128)(2,1)S(1)}, u32[]{:S(2)}, u32[]{:S(2)}) collective-permute-start(bf16[2,2,2,128,512]{4,3,2,1,0:T(8,128)(2,1)S(1)} %get-tuple-element.100.token), channel_id=1, source_target_pairs={{0,4},{1,5},{2,10},{3,11},{4,0},{5,1},{6,14},{7,15},{8,12},{9,13},... | collective-permute-start | bytes 3145736 | tf_op jit(solution)/shard_map/ppermute | solution.py:777
  61.5 17.7 %collective-permute-start.7 = (bf16[192,640]{1,0:T(8,128)(2,1)S(1)}, bf16[192,640]{1,0:T(8,128)(2,1)S(1)}, u32[]{:S(2)}, u32[]{:S(2)}) collective-permute-start(bf16[192,640]{1,0:T(8,128)(2,1)S(1)} %get-tuple-element.110), channel_id=1, source_target_pairs={{0,1},{1,2},{2,3},{3,4},{4,5},{5,6},{6,7},{7,8},{8,9},{9,10},{10,1... | collective-permute-start | bytes 737288 | tf_op jit(solution)/shard_map/ppermute | solution.py:769
  65.2 14.0 %collective-permute-start.8 = (bf16[192,640]{1,0:T(8,128)(2,1)S(1)}, bf16[192,640]{1,0:T(8,128)(2,1)S(1)}, u32[]{:S(2)}, u32[]{:S(2)}) collective-permute-start(bf16[192,640]{1,0:T(8,128)(2,1)S(1)} %get-tuple-element.111), channel_id=1, source_target_pairs={{1,0},{2,1},{3,2},{4,3},{5,4},{6,5},{7,6},{8,7},{9,8},{10,9},{11,1... | collective-permute-start | bytes 737288 | tf_op jit(solution)/shard_map/ppermute | solution.py:769
  76.6 10.9 %collective-permute-start.10 = (bf16[2,256,512]{2,1,0:T(8,128)(2,1)S(1)}, bf16[2,256,512]{2,1,0:T(8,128)(2,1)S(1)}, u32[]{:S(2)}, u32[]{:S(2)}) collective-permute-start(bf16[2,256,512]{2,1,0:T(8,128)(2,1)S(1)} %bitcast.47), channel_id=1, source_target_pairs={{0,1},{1,0},{2,6},{3,7},{4,5},{5,4},{6,2},{7,3},{8,9},{9,8},{10,14... | collective-permute-start | bytes 1572872 | tf_op jit(solution)/shard_map/ppermute | solution.py:777
  87.5 3.0 %collective-permute-start.9 = (bf16[2,2,2,2,80,512]{5,4,3,2,1,0:T(8,128)(2,1)S(1)}, bf16[2,2,2,2,80,512]{5,4,3,2,1,0:T(8,128)(2,1)S(1)}, u32[]{:S(2)}, u32[]{:S(2)}) collective-permute-start(bf16[2,2,2,2,80,512]{5,4,3,2,1,0:T(8,128)(2,1)S(1)} %get-tuple-element.117.refs_2_), channel_id=1, source_target_pairs={{0,2},{1,3},{2,0},{3,1},{4,6},{5,7},{6,4},{7,5},{8,10},{9,11},{10,... | collective-permute-start | bytes 3932168 | tf_op jit(solution)/shard_map/ppermute | solution.py:777
  87.6 6.9 %collective-permute-start.12 = (bf16[2,128,512]{2,1,0:T(8,128)(2,1)S(1)}, bf16[2,128,512]{2,1,0:T(8,128)(2,1)S(1)}, u32[]{:S(2)}, u32[]{:S(2)}) collective-permute-start(bf16[2,128,512]{2,1,0:T(8,128)(2,1)S(1)} %bitcast.57), channel_id=1, source_target_pairs={{0,8},{1,9},{2,3},{3,2},{4,12},{5,13},{6,7},{7,6},{8,0},{9,1},{10,... | collective-permute-start | bytes 786440 | tf_op jit(solution)/shard_map/ppermute | solution.py:777
  90.8 10.7 %collective-permute-start.11 = (bf16[2,320,512]{2,1,0:T(8,128)(2,1)S(1)}, bf16[2,320,512]{2,1,0:T(8,128)(2,1)S(1)}, u32[]{:S(2)}, u32[]{:S(2)}) collective-permute-start(bf16[2,320,512]{2,1,0:T(8,128)(2,1)S(1)} %bitcast.45), channel_id=1, source_target_pairs={{0,4},{1,5},{2,10},{3,11},{4,0},{5,1},{6,14},{7,15},{8,12},{9,13},... | collective-permute-start | bytes 1966088 | tf_op jit(solution)/shard_map/ppermute | solution.py:777
  94.6 11.2 %collective-permute-start.14 = (bf16[2,128,512]{2,1,0:T(8,128)(2,1)S(1)}, bf16[2,128,512]{2,1,0:T(8,128)(2,1)S(1)}, u32[]{:S(2)}, u32[]{:S(2)}) collective-permute-start(bf16[2,128,512]{2,1,0:T(8,128)(2,1)S(1)} %total.2.refs_2_.refs_0_), channel_id=1, source_target_pairs={{0,16},{1,17},{2,18},{3,19},{4,20},{5,21},{6,22},{7,23},{8,24},{9,... | collective-permute-start | bytes 786440 | tf_op jit(solution)/shard_map/ppermute | solution.py:777
  101.6 7.7 %collective-permute-start.13 = (bf16[2,160,512]{2,1,0:T(8,128)(2,1)S(1)}, bf16[2,160,512]{2,1,0:T(8,128)(2,1)S(1)}, u32[]{:S(2)}, u32[]{:S(2)}) collective-permute-start(bf16[2,160,512]{2,1,0:T(8,128)(2,1)S(1)} %bitcast.52), channel_id=1, source_target_pairs={{0,1},{1,0},{2,3},{3,2},{4,5},{5,4},{6,7},{7,6},{8,9},{9,8},{10,11... | collective-permute-start | bytes 983048 | tf_op jit(solution)/shard_map/ppermute | solution.py:777
  105.9 7.7 %collective-permute-start.16 = (bf16[256,512]{1,0:T(8,128)(2,1)S(1)}, bf16[256,512]{1,0:T(8,128)(2,1)S(1)}, u32[]{:S(2)}, u32[]{:S(2)}) collective-permute-start(bf16[256,512]{1,0:T(8,128)(2,1)S(1)} %bitcast.54), channel_id=1, source_target_pairs={{0,8},{1,9},{2,3},{3,2},{4,12},{5,13},{6,7},{7,6},{8,0},{9,1},{10,... | collective-permute-start | bytes 786440 | tf_op jit(solution)/shard_map/ppermute | solution.py:777
  109.4 6.0 %collective-permute-start.15 = (bf16[2,80,512]{2,1,0:T(8,128)(2,1)S(1)}, bf16[2,80,512]{2,1,0:T(8,128)(2,1)S(1)}, u32[]{:S(2)}, u32[]{:S(2)}) collective-permute-start(bf16[2,80,512]{2,1,0:T(8,128)(2,1)S(1)} %bitcast.59), channel_id=1, source_target_pairs={{0,8},{1,9},{2,6},{3,7},{4,12},{5,13},{6,2},{7,3},{8,0},{9,1},{10,... | collective-permute-start | bytes 491528 | tf_op jit(solution)/shard_map/ppermute | solution.py:777
  113.7 9.2 %collective-permute-start.18 = (bf16[512,512]{1,0:T(8,128)(2,1)S(1)}, bf16[512,512]{1,0:T(8,128)(2,1)S(1)}, u32[]{:S(2)}, u32[]{:S(2)}) collective-permute-start(bf16[512,512]{1,0:T(8,128)(2,1)S(1)} %bitcast.49), channel_id=1, source_target_pairs={{0,1},{1,0},{2,6},{3,7},{4,5},{5,4},{6,2},{7,3},{8,9},{9,8},{10,14... | collective-permute-start | bytes 1572872 | tf_op jit(solution)/shard_map/ppermute | solution.py:777
  115.5 11.1 %collective-permute-start.17 = (bf16[2,80,512]{2,1,0:T(8,128)(2,1)S(1)}, bf16[2,80,512]{2,1,0:T(8,128)(2,1)S(1)}, u32[]{:S(2)}, u32[]{:S(2)}) collective-permute-start(bf16[2,80,512]{2,1,0:T(8,128)(2,1)S(1)} %total.3.refs_2_.refs_0_), channel_id=1, source_target_pairs={{0,16},{1,17},{2,18},{3,19},{4,20},{5,21},{6,22},{7,23},{8,24},{9,... | collective-permute-start | bytes 491528 | tf_op jit(solution)/shard_map/ppermute | solution.py:777
  123.0 16.6 %collective-permute-start.21 = (bf16[1024,512]{1,0:T(8,128)(2,1)S(1)}, bf16[1024,512]{1,0:T(8,128)(2,1)S(1)}, u32[]{:S(2)}, u32[]{:S(2)}) collective-permute-start(bf16[1024,512]{1,0:T(8,128)(2,1)S(1)} %bitcast.32), channel_id=1, source_target_pairs={{0,4},{1,5},{2,10},{3,11},{4,0},{5,1},{6,14},{7,15},{8,12},{9,13},... | collective-permute-start | bytes 3145736 | tf_op jit(solution)/shard_map/ppermute | solution.py:777
  126.6 7.1 %collective-permute-start.19 = (bf16[160,512]{1,0:T(8,128)(2,1)S(1)}, bf16[160,512]{1,0:T(8,128)(2,1)S(1)}, u32[]{:S(2)}, u32[]{:S(2)}) collective-permute-start(bf16[160,512]{1,0:T(8,128)(2,1)S(1)} %bitcast.39), channel_id=1, source_target_pairs={{0,8},{1,9},{2,6},{3,7},{4,12},{5,13},{6,2},{7,3},{8,0},{9,1},{10,... | collective-permute-start | bytes 491528 | tf_op jit(solution)/shard_map/ppermute | solution.py:777
  133.8 13.4 %collective-permute-start.20 = (bf16[320,512]{1,0:T(8,128)(2,1)S(1)}, bf16[320,512]{1,0:T(8,128)(2,1)S(1)}, u32[]{:S(2)}, u32[]{:S(2)}) collective-permute-start(bf16[320,512]{1,0:T(8,128)(2,1)S(1)} %bitcast.29), channel_id=1, source_target_pairs={{0,1},{1,0},{2,3},{3,2},{4,5},{5,4},{6,7},{7,6},{8,9},{9,8},{10,11... | collective-permute-start | bytes 983048 | tf_op jit(solution)/shard_map/ppermute | solution.py:777
  146.1 8.4 %collective-permute-start.23 = (bf16[2,512,512]{2,1,0:T(8,128)(2,1)S(1)}, bf16[2,512,512]{2,1,0:T(8,128)(2,1)S(1)}, u32[]{:S(2)}, u32[]{:S(2)}) collective-permute-start(bf16[2,512,512]{2,1,0:T(8,128)(2,1)S(1)} %get-tuple-element.129.own), channel_id=1, source_target_pairs={{0,2},{1,3},{2,0},{3,1},{4,6},{5,7},{6,4},{7,5},{8,10},{9,11},{10,... | collective-permute-start | bytes 3145736 | tf_op jit(solution)/shard_map/ppermute | solution.py:777
  147.2 7.4 %copy-start.3 = (f32[1024,512]{1,0:T(8,128)S(1)}, f32[1024,512]{1,0:T(8,128)}, u32[]{:S(2)}) copy-start(f32[1024,512]{1,0:T(8,128)} %down_moment.1) | copy-start | bytes 6291460
  147.2 7.4 %copy-start.1 = (f32[512,1024]{1,0:T(8,128)S(1)}, f32[512,1024]{1,0:T(8,128)}, u32[]{:S(2)}) copy-start(f32[512,1024]{1,0:T(8,128)} %up_moment.1) | copy-start | bytes 6291460
  147.2 10.7 %collective-permute-start.22 = (bf16[640,512]{1,0:T(8,128)(2,1)S(1)}, bf16[640,512]{1,0:T(8,128)(2,1)S(1)}, u32[]{:S(2)}, u32[]{:S(2)}) collective-permute-start(bf16[640,512]{1,0:T(8,128)(2,1)S(1)} %bitcast.36), channel_id=1, source_target_pairs={{0,4},{1,5},{2,10},{3,11},{4,0},{5,1},{6,14},{7,15},{8,12},{9,13},... | collective-permute-start | bytes 1966088 | tf_op jit(solution)/shard_map/ppermute | solution.py:777
  154.3 4.6 %collective-permute-start.25 = (bf16[2,512,512]{2,1,0:T(8,128)(2,1)S(1)}, bf16[2,512,512]{2,1,0:T(8,128)(2,1)S(1)}, u32[]{:S(2)}, u32[]{:S(2)}) collective-permute-start(bf16[2,512,512]{2,1,0:T(8,128)(2,1)S(1)} %ortho_large.3.token.own), channel_id=1, source_target_pairs={{0,2},{1,3},{2,0},{3,1},{4,6},{5,7},{6,4},{7,5},{8,10},{9,11},{10,... | collective-permute-start | bytes 3145736 | tf_op jit(solution)/shard_map/ppermute | solution.py:777
  157.9 1.6 copy-start.9
  157.9 2.2 %copy-start.12 = (f32[1024,512]{1,0:T(8,128)S(1)}, f32[1024,512]{1,0:T(8,128)}, u32[]{:S(2)}) copy-start(f32[1024,512]{1,0:T(8,128)} %down_weight.1) | copy-start | bytes 6291460
  158.6 13.1 %collective-permute-start.24 = (bf16[2,272,512]{2,1,0:T(8,128)(2,1)S(1)}, bf16[2,272,512]{2,1,0:T(8,128)(2,1)S(1)}, u32[]{:S(2)}, u32[]{:S(2)}) collective-permute-start(bf16[2,272,512]{2,1,0:T(8,128)(2,1)S(1)} %get-tuple-element.131.mix.table), channel_id=1, source_target_pairs={{0,2},{1,3},{2,0},{3,1},{4,6},{5,7},{6,4},{7,5},{8,10},{9,11},{10,... | collective-permute-start | bytes 1671176 | tf_op jit(solution)/shard_map/ppermute | solution.py:777
  160.1 11.6 %copy-start.16 = (f32[2,4,512]{2,1,0:T(4,128)S(1)}, f32[2,4,512]{2,1,0:T(4,128)}, u32[]{:S(2)}) copy-start(f32[2,4,512]{2,1,0:T(4,128)} %modulation.1) | copy-start | bytes 49156
  160.1 11.6 %copy-start.17 = (f32[2,2,512]{2,1,0:T(2,128)S(1)}, f32[2,2,512]{2,1,0:T(2,128)}, u32[]{:S(2)}) copy-start(f32[2,2,512]{2,1,0:T(2,128)} %held_moment.1) | copy-start | bytes 24580
  171.4 2.9 %collective-permute-start.26 = (bf16[2,256,512]{2,1,0:T(8,128)(2,1)S(1)}, bf16[2,256,512]{2,1,0:T(8,128)(2,1)S(1)}, u32[]{:S(2)}, u32[]{:S(2)}) collective-permute-start(bf16[2,256,512]{2,1,0:T(8,128)(2,1)S(1)} %get-tuple-element.133.token.own), channel_id=1, source_target_pairs={{0,2},{1,3},{2,0},{3,1},{4,6},{5,7},{6,4},{7,5},{8,10},{9,11},{10,... | collective-permute-start | bytes 1572872 | tf_op jit(solution)/shard_map/ppermute | solution.py:777
  171.7 2.6 %copy-start.5 = (f32[4,512,512]{2,1,0:T(8,128)S(1)}, f32[4,512,512]{2,1,0:T(8,128)}, u32[]{:S(2)}) copy-start(f32[4,512,512]{2,1,0:T(8,128)} %weight.1) | copy-start | bytes 12582916

commit v2 on v1

--- a/solution.py
+++ b/solution.py
@@ -116,7 +116,7 @@
     return jnp.concatenate(pieces, axis=1).astype(bf16)
 
 
-def quarter_kernel(scalars, up, down, rounded):
+def quarter_kernel(scalars, up, down, token, rounded):
     rounded[0] = up[...].astype(bf16)
     rounded[1] = down[...].astype(bf16)
 
@@ -211,8 +211,8 @@
             peak = jnp.max(masked, axis=-1, keepdims=True)
             exponent = jnp.exp(masked - peak)
             total = jnp.sum(exponent * count, axis=-1, keepdims=True)
-            probs = (exponent / total).astype(bf16)
-            spread = (probs.astype(f32) * count).astype(bf16)
+            probs = (exponent * (1.0 / total)).astype(bf16)
+            spread = probs * counts[rows, :]
             attended[rows, cols] = nn(spread, padded[1, span, cols]).astype(bf16)
             stats = jnp.where(lanes == h, peak + jnp.log(total), stats)
         log_totals[rows, :] = stats
@@ -252,7 +252,7 @@
 
 
 def mlp_own_kernel(
-    scalars, second_in, cotangent, up, down, branch, grad_second, kept, sent, acts, grads
+    scalars, second_in, cotangent, up, down, token, branch, grad_second, kept, sent, acts, grads
 ):
     @pl.when(pl.program_id(0) == 0)
     def _():
@@ -371,11 +371,10 @@
         edge[:, D:] = (upper.astype(f32) + pltpu.roll(lower, 2 * HEADS, 1)).astype(bf16)
 
 
-def attention_terms(scores, grad_probs, count, log_total, delta):
-    probs = jnp.exp(jnp.where(count > 0.0, scores * score_scale, -1e30) - log_total)
-    slopes = (probs * (grad_probs - delta)).astype(bf16).astype(f32)
-    spread = (probs.astype(bf16).astype(f32) * count).astype(bf16)
-    return (slopes * count).astype(bf16), spread
+def attention_terms(scores, grad_probs, live, count, log_total, delta):
+    probs = jnp.exp(jnp.where(live, scores * score_scale, -1e30) - log_total)
+    slopes = (probs * (grad_probs - delta)).astype(bf16)
+    return slopes * count, probs.astype(bf16) * count
 
 
 def backward_kernel(qkv, padded, grad, stats, counts, token, grad_query, keys_total, values_total):
@@ -385,7 +384,8 @@
     def step(b, carry):
         rows = rows_of(b * BLOCK, BLOCK)
         span = pl.ds(pl.multiple_of(b * BLOCK, BLOCK), SPAN)
-        count = counts[rows, :].astype(f32)
+        count = counts[rows, :]
+        live = count.astype(f32) > 0.0
         columns = [slice(h * HD, (h + 1) * HD) for h in range(HEADS)]
         products = [
             (nt(qkv[0, rows, cols], padded[0, span, cols]), nt(grad[rows, cols], padded[1, span, cols]))
@@ -394,6 +394,7 @@
         terms = [
             attention_terms(
                 *products[h],
+                live,
                 count,
                 stats[rows, h : h + 1],
                 stats[rows, HEADS + h : HEADS + h + 1],
@@ -448,7 +449,8 @@
         span = slice(HALO + first, HALO + first + RIM)
         rows = slice(side * HALO, (side + 1) * HALO)
         known = grads[:, D:].astype(f32)
-        count = rim_counts[rows, :].astype(f32)
+        count = rim_counts[rows, :]
+        live = count.astype(f32) > 0.0
         products = [
             (nt(rim_query[rows, cols], padded[0, span, cols]), nt(grads[:, cols], padded[1, span, cols]))
             for cols in columns
@@ -457,7 +459,7 @@
         for h in range(HEADS):
             numbers = [known[:, i * HEADS + h : i * HEADS + h + 1] for i in range(4)]
             terms.append(
-                attention_terms(*products[h], count, numbers[0] + numbers[2], numbers[1] + numbers[3])
+                attention_terms(*products[h], live, count, numbers[0] + numbers[2], numbers[1] + numbers[3])
             )
         for (slopes, spread), cols in zip(terms, columns):
             keys_total[own_span, cols] += tn(slopes, rim_query[rows, cols])
@@ -783,8 +785,9 @@
         [offsets, levels[:, None], jnp.zeros((row_count, 128 - K - 1), jnp.int32)], axis=1
     ).astype(f32)
     rims = jnp.concatenate([features, pack.astype(bf16)], axis=1)
-    rim_low = along(rims[row_count - HALO :], 1)
-    rim_high = along(rims[:HALO], -1)
+    low_edge, high_edge = rims[row_count - HALO :], rims[:HALO]
+    rim_low = along(low_edge, 1)
+    rim_high = along(high_edge, -1)
 
     pack, scalars, is_first = lax.optimization_barrier((pack, scalars, is_first))
     mod = modulation
@@ -797,6 +800,7 @@
             in_specs=[
                 pl.BlockSpec((D, CHUNK), lambda g, s: (0, s[0])),
                 pl.BlockSpec((CHUNK, D), lambda g, s: (s[0], 0)),
+                pl.BlockSpec(memory_space=pl.ANY),
             ],
             out_specs=pl.BlockSpec((2, D, CHUNK), lambda g, s: (0, 0, 0)),
         ),
@@ -804,7 +808,7 @@
         cost_estimate=cost(1e6, 3e6),
         name="quarter",
         compiler_params=room(8),
-    )(scalars, up_weight, down_weight)
+    )(scalars, up_weight, down_weight, low_edge)
     large_past, small_past = pl.pallas_call(
         past_kernel,
         grid_spec=pltpu.PrefetchScalarGridSpec(
@@ -846,12 +850,12 @@
             pl.BlockSpec((row_count, SPAN), lambda g: (0, 0)),
             pl.BlockSpec((1, D, D), lambda g: (g, 0, 0)),
         ),
-        cost_estimate=cost(4e9, 4e6),
+        cost_estimate=cost(1e3, 1e3),
         name="project",
         compiler_params=room(10),
     )(features, pack, mod, attention_weight)
 
-    near = swap(after(quarter, rim_low, rim_high, large_past), 1)
+    near = swap(quarter, 1)
 
     attended, stream, second_in, padded, rim_queries, rim_counts, log_totals = pl.pallas_call(
         forward_kernel,
@@ -867,7 +871,7 @@
         in_specs=[VMEM] * 8,
         out_specs=(VMEM,) * 7,
         scratch_shapes=[pltpu.VMEM((2 * HALO, D), bf16)],
-        cost_estimate=cost(6e9, 8e6),
+        cost_estimate=cost(1e3, 1e3),
         name="attend",
         compiler_params=room(12),
     )(rim_low, rim_high, features, pack, mod, attn_bf, qkv, counts)
@@ -887,6 +891,7 @@
                 whole(row_count, D),
                 pl.BlockSpec((D, CHUNK), lambda g, s: (0, g)),
                 pl.BlockSpec((CHUNK, D), lambda g, s: (g, 0)),
+                pl.BlockSpec(memory_space=pl.ANY),
             ],
             out_specs=(
                 whole(row_count, D),
@@ -896,10 +901,10 @@
             ),
             scratch_shapes=[pltpu.VMEM((row_count, CHUNK), bf16)] * 2,
         ),
-        cost_estimate=cost(5e9, 8e6),
+        cost_estimate=cost(1e10, 1e3),
         name="mlp_own",
         compiler_params=room(14),
-    )(scalars, second_in, cotangent, up_weight, down_weight)
+    )(scalars, second_in, cotangent, up_weight, down_weight, small_past)
 
     def part(away):
         return pl.BlockSpec(

time: 177 us -> 174 us (0.983)
  waiting for transfers between devices: 38.3 us -> 42.2 us
  starting transfers between devices: 42.6 us -> 39 us
  local copies, waits for them, and re-layouts: 7.14 us -> 4.17 us
    ppermute x23, waiting for transfers between devices: 36.6 us -> 42.2 us  [swap(): return lax.ppermute(value, AXES, pairs)]
    ppermute x23, starting transfers between devices: 30.2 us -> 25.9 us  [swap(): return lax.ppermute(value, AXES, pairs)]
    unnamed x36 -> x32, local copies, waits for them, and re-layouts: 5.98 us -> 2.86 us
  transfers between devices with their start and end apart: 27 -> 27, of which waited for: 14 -> 13; matrix products, arithmetic and copies ran while one was open for 0% -> 0% of each run, Pallas kernels for 46% -> 47%
where the time goes in v2:
time: 174 us
  Pallas kernels  84.5 us (49%)
  waiting for transfers between devices  42.2 us (24%)
  starting transfers between devices  39 us (22%)
  local copies, waits for them, and re-layouts  4.17 us (2%)
  other arithmetic  2.63 us (2%)
    ppermute x23, waiting for transfers between devices, swap(): return lax.ppermute(value, AXES, pairs)  42.2 us
    ppermute x23, starting transfers between devices, swap(): return lax.ppermute(value, AXES, pairs)  25.9 us
    ppermute x4, starting transfers between devices, along(): return lax.ppermute(value, AXES, pairs)  13.2 us
    pallas_call x1, Pallas kernels, on_device(): pl.pallas_call(small_kernel, grid=(NS_STEPS,), out_shape=(struct((2, 256,...  11.3 us
    pallas_call x1, Pallas kernels, on_device(): pl.pallas_call(forward_kernel, out_shape=(struct((row_count, D), bf16), s...  9.92 us
    pallas_call x1, Pallas kernels, on_device(): pl.pallas_call(weights_kernel, out_shape=(struct((row_count, D), f32), pi...  8.26 us
    pallas_call x1, Pallas kernels, on_device(): pl.pallas_call(backward_kernel, out_shape=(struct((row_count, D), bf16),)...  8.13 us
    pallas_call x1, Pallas kernels, on_device(): pl.pallas_call(mlp_own_kernel, out_shape=(struct((row_count, D), f32), st...  6.82 us
  transfers between devices with their start and end apart: 27, of which 13 were waited for; matrix products, arithmetic and copies ran while one was open for 0% of the time, Pallas kernels for 47%

profile of v2, /device:TPU:0, one launch (start us, length us, event | category | flops | bytes accessed | tf_op | source)
XLA Modules:
  0.0 173.6 jit_solution(3701375498493511238)
XLA Ops:
  0.7 0.9 broadcast_subtract_fusion
  1.6 0.2 copy.30
  1.8 1.0 broadcast_in_dim.16
  2.8 0.9 fusion
  3.6 0.2 fusion.1
  3.9 0.7 pad_maximum_fusion
  4.6 1.3 collective-permute-start.1
  5.9 6.2 %collective-permute-start = (bf16[192,640]{1,0:T(8,128)(2,1)S(1)}, bf16[192,640]{1,0:T(8,128)(2,1)}, u32[]{:S(2)}, u32[]{:S(2)}) collective-permute-start(bf16[192,640]{1,0:T(8,128)(2,1)S(1)} %get-tuple-element.143.token), channel_id=1, source_target_pairs={{0,1},{1,2},{2,3},{3,4},{4,5},{5,6},{6,7},{7,8},{8,9},{9,10},{10,1... | collective-permute-start | bytes 737288 | tf_op jit(solution)/shard_map/ppermute | solution.py:771
  12.2 1.6 copy-done.10
  13.8 0.6 quarter.1
  14.5 1.1 collective-permute-start.2
  15.6 0.4 copy-done
  16.0 5.9 %project.1 = (bf16[768,512]{1,0:T(8,128)(2,1)S(1)}, bf16[3,768,512]{2,1,0:T(8,128)(2,1)S(1)}, bf16[768,512]{1,0:T(8,128)(2,1)S(1)}, bf16[4,512,512]{2,1,0:T(8,128)(2,1)S(1)}) custom-call(bf16[768,512]{1,0:T(8,128)(2,1)S(1)} %copy-done.6, f32[768,128]{1,0:T(8,128)S(1)} %get-tuple-element.76.pack, f32[2,4,512]{2,1,0:T(4,128)S(1)} %copy-done.13, ...), custom_call_target="tpu_custom_call" | custom-call | flops 1000 | bytes 1000 | tf_op jit(solution)/shard_map/project/pallas_call | solution.py:832
  21.9 0.8 past.1
  22.7 9.9 %attend.1 = (bf16[768,512]{1,0:T(8,128)(2,1)S(1)}, f32[768,512]{1,0:T(8,128)S(1)}, bf16[768,512]{1,0:T(8,128)(2,1)S(1)}, bf16[2,1152,512]{2,1,0:T(8,128)(2,1)S(1...) custom-call(bf16[192,640]{1,0:T(8,128)(2,1)} %collective-permute-done.rim_low, ...), custom_call_target="tpu_custom_call" | custom-call | flops 1000 | bytes 1000 | tf_op jit(solution)/shard_map/attend/pallas_call | solution.py:860
  32.7 6.8 %mlp_own.1 = (f32[768,512]{1,0:T(8,128)S(1)}, f32[768,512]{1,0:T(8,128)S(1)}, bf16[2,2,2,128,512]{4,3,2,1,0:T(8,128)(2,1)S(1)}, bf16[2,2,2,128,512]{4,3,2,1,0:T(8,128)(2,1)S(1)}) custom-call(s32[5]{0:T(128)S(1)} %stack.23.scalars, bf16[768,512]{1,0:T(8,128)(2,1)S(1)} %get-tuple-element.80.second_in, bf16[768,512]{1,0:T(8,128)(2,1)S(1)} %copy-done.14, ...), custom_call_target="tpu_custom_call" | custom-call | flops 10000000000 | bytes 1000 | tf_op jit(solution)/shard_map/mlp_own/pallas_call | solution.py:883
  39.5 3.9 %collective-permute-done.2.near = bf16[2,512,512]{2,1,0:T(8,128)(2,1)S(1)} collective-permute-done((bf16[2,512,512]{2,1,0:T(8,128)(2,1)S(1)}, bf16[2,512,512]{2,1,0:T(8,128)(2,1)S(1)}, u32[]{:S(2)}, u32[]{:S(2)}) %collective-permute-start.2) | collective-permute-done | bytes 1048608 | tf_op jit(solution)/shard_map/ppermute | solution.py:779
  43.4 0.5 collective-permute-start.4
  43.9 3.4 %mlp_near.1 = (f32[768,512]{1,0:T(8,128)S(1)}, f32[768,512]{1,0:T(8,128)S(1)}, bf16[2,2,2,128,512]{4,3,2,1,0:T(8,128)(2,1)S(1)}, bf16[2,2,2,128,512]{4,3,2,1,0:T(8,128)(2,1)S(1)}) custom-call(s32[5]{0:T(128)S(1)} %stack.23.scalars, bf16[768,512]{1,0:T(8,128)(2,1)S(1)} %get-tuple-element.80.second_in, bf16[768,512]{1,0:T(8,128)(2,1)S(1)} %copy-done.14, ...), custom_call_target="tpu_custom_call" | custom-call | flops 2500000000 | bytes 4000000 | tf_op jit(solution)/shard_map/mlp_near/pallas_call | solution.py:914
  47.2 5.7 %mlp_far.1 = (bf16[2,2,2,128,512]{4,3,2,1,0:T(8,128)(2,1)S(1)}, bf16[2,2,2,128,512]{4,3,2,1,0:T(8,128)(2,1)S(1)}, bf16[768,512]{1,0:T(8,128)(2,1)}, f32[768,512]...) custom-call(s32[5]{0:T(128)S(1)} %stack.23.scalars, ...), custom_call_target="tpu_custom_call", output_to_operand_aliasing={{0}: (12, {}), {1}: (13, {})} | custom-call | flops 4000000000 | bytes 8000000 | tf_op jit(solution)/shard_map/mlp_far/pallas_call | solution.py:945
  53.0 2.6 %collective-permute-done.5.rest_got = bf16[2,2,2,128,512]{4,3,2,1,0:T(8,128)(2,1)S(1)} collective-permute-done((bf16[2,2,2,128,512]{4,3,2,1,0:T(8,128)(2,1)S(1)}, bf16[2,2,2,128,512]{4,3,2,1,0:T(8,128)(2,1)S(1)}, u32[]{:S(2)}, u32[]{:S(2)}) %collective-permute-start.5) | collective-permute-done | bytes 1048608 | tf_op jit(solution)/shard_map/ppermute | solution.py:779
  55.7 1.0 large_sum.1
  56.7 1.3 collective-permute-start.6
  58.0 4.4 %collective-permute-start.7 = (bf16[192,640]{1,0:T(8,128)(2,1)S(1)}, bf16[192,640]{1,0:T(8,128)(2,1)S(1)}, u32[]{:S(2)}, u32[]{:S(2)}) collective-permute-start(bf16[192,640]{1,0:T(8,128)(2,1)S(1)} %get-tuple-element.108), channel_id=1, source_target_pairs={{0,1},{1,2},{2,3},{3,4},{4,5},{5,6},{6,7},{7,8},{8,9},{9,10},{10,1... | collective-permute-start | bytes 737288 | tf_op jit(solution)/shard_map/ppermute | solution.py:771
  62.4 1.3 collective-permute-start.8
  63.7 8.1 %attend_back.1 = (bf16[768,512]{1,0:T(8,128)(2,1)S(1)}, f32[1152,512]{1,0:T(8,128)S(1)}, f32[1152,512]{1,0:T(8,128)S(1)}) custom-call(bf16[3,768,512]{2,1,0:T(8,128)(2,1)S(1)} %get-tuple-element.78.qkv, bf16[2,1152,512]{2,1,0:T(8,128)(2,1)S(1)} %get-tuple-element.99.padded, bf16[768,512]{1,0:T(8,128)(2,1)S(1)} %get-tuple-element.100.grad, ...), custom_call_target="tpu_custom_call" | custom-call | flops 8000000000 | bytes 9000000 | tf_op jit(solution)/shard_map/attend_back/pallas_call | solution.py:1088
  71.8 1.1 collective-permute-done.6
  72.9 0.2 receive.5
  73.1 3.0 %collective-permute-start.10 = (bf16[2,256,512]{2,1,0:T(8,128)(2,1)S(1)}, bf16[2,256,512]{2,1,0:T(8,128)(2,1)S(1)}, u32[]{:S(2)}, u32[]{:S(2)}) collective-permute-start(bf16[2,256,512]{2,1,0:T(8,128)(2,1)S(1)} %bitcast.47), channel_id=1, source_target_pairs={{0,1},{1,0},{2,6},{3,7},{4,5},{5,4},{6,2},{7,3},{8,9},{9,8},{10,14... | collective-permute-start | bytes 1572872 | tf_op jit(solution)/shard_map/ppermute | solution.py:779
  76.1 8.3 %attend_weights.1 = (f32[768,512]{1,0:T(8,128)}, bf16[2,2,2,2,80,512]{5,4,3,2,1,0:T(8,128)(2,1)S(1)}, bf16[2,2,2,2,80,512]{5,4,3,2,1,0:T(8,128)(2,1)S(1)}) custom-call(s32[5]{0:T(128)S(1)} %stack.23.scalars, bf16[2,256,512]{2,1,0:T(8,128)(2,1)S(1)} %bitcast.48, bf16[768,512]{1,0:T(8,128)(2,1)S(1)} %get-tuple-element.102.refs_2_.queries_in, ...), custom_call_target="tpu_custom_call" | custom-call | flops 6000000000 | bytes 9000000 | tf_op jit(solution)/shard_map/attend_weights/pallas_call | solution.py:1100
  84.5 1.6 collective-permute-start.12
  86.1 1.3 collective-permute-done.9
  87.4 0.3 receive.7
  87.7 2.0 %collective-permute-start.11 = (bf16[2,320,512]{2,1,0:T(8,128)(2,1)S(1)}, bf16[2,320,512]{2,1,0:T(8,128)(2,1)S(1)}, u32[]{:S(2)}, u32[]{:S(2)}) collective-permute-start(bf16[2,320,512]{2,1,0:T(8,128)(2,1)S(1)} %bitcast.45), channel_id=1, source_target_pairs={{0,4},{1,5},{2,10},{3,11},{4,0},{5,1},{6,14},{7,15},{8,12},{9,13},... | collective-permute-start | bytes 1966088 | tf_op jit(solution)/shard_map/ppermute | solution.py:779
  89.8 1.6 collective-permute-done.12.refs_1_
  91.4 2.6 %collective-permute-start.14 = (bf16[2,128,512]{2,1,0:T(8,128)(2,1)S(1)}, bf16[2,128,512]{2,1,0:T(8,128)(2,1)S(1)}, u32[]{:S(2)}, u32[]{:S(2)}) collective-permute-start(bf16[2,128,512]{2,1,0:T(8,128)(2,1)S(1)} %total.2.refs_2_.refs_0_), channel_id=1, source_target_pairs={{0,16},{1,17},{2,18},{3,19},{4,20},{5,21},{6,22},{7,23},{8,24},{9,... | collective-permute-start | bytes 786440 | tf_op jit(solution)/shard_map/ppermute | solution.py:779
  94.0 4.4 %collective-permute-done.11.refs_1_ = bf16[2,320,512]{2,1,0:T(8,128)(2,1)S(1)} collective-permute-done((bf16[2,320,512]{2,1,0:T(8,128)(2,1)S(1)}, bf16[2,320,512]{2,1,0:T(8,128)(2,1)S(1)}, u32[]{:S(2)}, u32[]{:S(2)}) %collective-permute-start.11) | collective-permute-done | bytes 655392 | tf_op jit(solution)/shard_map/ppermute | solution.py:779
  98.4 0.1 receive.8
  98.6 4.1 %collective-permute-done.14.refs_1_ = bf16[2,128,512]{2,1,0:T(8,128)(2,1)S(1)} collective-permute-done((bf16[2,128,512]{2,1,0:T(8,128)(2,1)S(1)}, bf16[2,128,512]{2,1,0:T(8,128)(2,1)S(1)}, u32[]{:S(2)}, u32[]{:S(2)}) %collective-permute-start.14) | collective-permute-done | bytes 262176 | tf_op jit(solution)/shard_map/ppermute | solution.py:779
  102.8 3.9 %collective-permute-start.16 = (bf16[256,512]{1,0:T(8,128)(2,1)S(1)}, bf16[256,512]{1,0:T(8,128)(2,1)S(1)}, u32[]{:S(2)}, u32[]{:S(2)}) collective-permute-start(bf16[256,512]{1,0:T(8,128)(2,1)S(1)} %bitcast.54), channel_id=1, source_target_pairs={{0,8},{1,9},{2,3},{3,2},{4,12},{5,13},{6,7},{7,6},{8,0},{9,1},{10,... | collective-permute-start | bytes 786440 | tf_op jit(solution)/shard_map/ppermute | solution.py:779
  106.7 1.8 %collective-permute-start.15 = (bf16[2,80,512]{2,1,0:T(8,128)(2,1)S(1)}, bf16[2,80,512]{2,1,0:T(8,128)(2,1)S(1)}, u32[]{:S(2)}, u32[]{:S(2)}) collective-permute-start(bf16[2,80,512]{2,1,0:T(8,128)(2,1)S(1)} %bitcast.59), channel_id=1, source_target_pairs={{0,8},{1,9},{2,6},{3,7},{4,12},{5,13},{6,2},{7,3},{8,0},{9,1},{10,... | collective-permute-start | bytes 491528 | tf_op jit(solution)/shard_map/ppermute | solution.py:779
  108.5 2.5 %collective-permute-done.16.refs_1_ = bf16[256,512]{1,0:T(8,128)(2,1)S(1)} collective-permute-done((bf16[256,512]{1,0:T(8,128)(2,1)S(1)}, bf16[256,512]{1,0:T(8,128)(2,1)S(1)}, u32[]{:S(2)}, u32[]{:S(2)}) %collective-permute-start.16) | collective-permute-done | bytes 262176 | tf_op jit(solution)/shard_map/ppermute | solution.py:779
  111.1 0.3 collective-permute-start.18
  111.4 1.4 collective-permute-done.15.refs_1_
  112.8 3.4 %collective-permute-start.17 = (bf16[2,80,512]{2,1,0:T(8,128)(2,1)S(1)}, bf16[2,80,512]{2,1,0:T(8,128)(2,1)S(1)}, u32[]{:S(2)}, u32[]{:S(2)}) collective-permute-start(bf16[2,80,512]{2,1,0:T(8,128)(2,1)S(1)} %total.3.refs_2_.refs_0_), channel_id=1, source_target_pairs={{0,16},{1,17},{2,18},{3,19},{4,20},{5,21},{6,22},{7,23},{8,24},{9,... | collective-permute-start | bytes 491528 | tf_op jit(solution)/shard_map/ppermute | solution.py:779
  116.3 4.0 %collective-permute-done.18.refs_1_ = bf16[512,512]{1,0:T(8,128)(2,1)S(1)} collective-permute-done((bf16[512,512]{1,0:T(8,128)(2,1)S(1)}, bf16[512,512]{1,0:T(8,128)(2,1)S(1)}, u32[]{:S(2)}, u32[]{:S(2)}) %collective-permute-start.18) | collective-permute-done | bytes 524320 | tf_op jit(solution)/shard_map/ppermute | solution.py:779
  120.4 0.5 collective-permute-start.21
  120.8 3.8 %collective-permute-done.17.refs_1_ = bf16[2,80,512]{2,1,0:T(8,128)(2,1)S(1)} collective-permute-done((bf16[2,80,512]{2,1,0:T(8,128)(2,1)S(1)}, bf16[2,80,512]{2,1,0:T(8,128)(2,1)S(1)}, u32[]{:S(2)}, u32[]{:S(2)}) %collective-permute-start.17) | collective-permute-done | bytes 163872 | tf_op jit(solution)/shard_map/ppermute | solution.py:779
  124.7 0.6 collective-permute-start.19
  125.3 6.5 %collective-permute-done.19.refs_1_ = bf16[160,512]{1,0:T(8,128)(2,1)S(1)} collective-permute-done((bf16[160,512]{1,0:T(8,128)(2,1)S(1)}, bf16[160,512]{1,0:T(8,128)(2,1)S(1)}, u32[]{:S(2)}, u32[]{:S(2)}) %collective-permute-start.19) | collective-permute-done | bytes 163872 | tf_op jit(solution)/shard_map/ppermute | solution.py:779
  132.0 5.0 %collective-permute-done.21 = bf16[1024,512]{1,0:T(8,128)(2,1)S(1)} collective-permute-done((bf16[1024,512]{1,0:T(8,128)(2,1)S(1)}, bf16[1024,512]{1,0:T(8,128)(2,1)S(1)}, u32[]{:S(2)}, u32[]{:S(2)}) %collective-permute-start.21) | collective-permute-done | bytes 1048608 | tf_op jit(solution)/shard_map/ppermute | solution.py:779
  137.0 6.5 %ortho_large.2 = (bf16[4,512,512]{2,1,0:T(8,128)(2,1)S(1)}, bf16[2,512,512]{2,1,0:T(8,128)(2,1)S(1)}) custom-call(s32[5]{0:T(128)S(1)} %stack.23.scalars, bf16[2,2,2,128,512]{4,3,2,1,0:T(8,128)(2,1)S(1)} %bitcast.34, bf16[2,2,2,128,512]{4,3,2,1,0:T(8,128)(2,1)S(1)} %bitcast.35, bf16[320,512]{1,0:T(8,128)(2,1)S(1)} %bitcast.30), custom_call_target="tpu_custom_call" | custom-call | flops 1000 | bytes 1000 | tf_op jit(solution)/shard_map/ortho_large/pallas_call | solution.py:1168
  143.5 1.0 collective-permute-start.23
  144.6 1.1 collective-permute-start.22
  145.6 5.9 %ortho_large.3.token.own = bf16[2,512,512]{2,1,0:T(8,128)(2,1)S(1)} custom-call(bf16[4,512,512]{2,1,0:T(8,128)(2,1)S(1)} %get-tuple-element.126.refs_2_.given, bf16[640,512]{1,0:T(8,128)(2,1)S(1)} %bitcast.37), custom_call_target="tpu_custom_call" | custom-call | flops 1000 | bytes 1000 | tf_op jit(solution)/shard_map/ortho_large/pallas_call | solution.py:1181
  151.5 0.4 collective-permute-start.25
  151.9 3.3 %moment_large.1 = (f32[512,1024]{1,0:T(8,128)}, f32[1024,512]{1,0:T(8,128)}, f32[8,128]{1,0:T(8,128)S(1)}) custom-call(s32[5]{0:T(128)S(1)} %stack.23.scalars, bf16[2,512,512]{2,1,0:T(8,128)(2,1)S(1)} %get-tuple-element.127.own, bf16[2,512,512]{2,1,0:T(8,128)(2,1)S(1)} %collective-permute-done.23.got, f32[512,1024]{1,0:T(8,128)S(1)} %copy-done.3, ...), custom_call_target="tpu_custom_call" | custom-call | flops 1000 | bytes 1000 | tf_op jit(solution)/shard_map/moment_large/pallas_call | solution.py:1199
  155.2 0.7 unpack_small.1
  155.9 0.2 collective-permute-start.24
  156.2 0.7 copy-done.12
  156.8 11.3 %ortho_small.1 = (bf16[2,256,512]{2,1,0:T(8,128)(2,1)S(1)}, f32[512,1024]{1,0:T(8,128)}, f32[1024,512]{1,0:T(8,128)}) custom-call(s32[5]{0:T(128)S(1)} %stack.23.scalars, bf16[2,2,256,512]{3,2,1,0:T(8,128)(2,1)S(1)} %get-tuple-element.130.given, bf16[2,512,512]{2,1,0:T(8,128)(2,1)S(1)} %ortho_large.3.token.own, ...), custom_call_target="tpu_custom_call" | custom-call | flops 6000000000 | bytes 10000000 | tf_op jit(solution)/shard_map/ortho_small/pallas_call | solution.py:1236
  168.1 0.2 collective-permute-start.26
  168.3 2.5 %moment_small.1 = (f32[4,256,512]{2,1,0:T(8,128)}, f32[2,2,512]{2,1,0:T(2,128)}, f32[2,2,512]{2,1,0:T(2,128)}, f32[8,128]{1,0:T(8,128)S(1)}) custom-call(s32[5]{0:T(128)S(1)} %stack.23.scalars, bf16[2,272,512]{2,1,0:T(8,128)(2,1)S(1)} %get-tuple-element.129.mix.table, bf16[2,272,512]{2,1,0:T(8,128)(2,1)S(1)} %collective-permute-done.24.mix_got.table_got, ...), custom_call_target="tpu_custom_call" | custom-call | flops 10000000000 | bytes 10000000 | tf_op jit(solution)/shard_map/moment_small/pallas_call | solution.py:1251
  171.0 2.6 %update_small.1 = f32[4,256,512]{2,1,0:T(8,128)} custom-call(s32[5]{0:T(128)S(1)} %stack.23.scalars, bf16[2,256,512]{2,1,0:T(8,128)(2,1)S(1)} %get-tuple-element.131.token.own, bf16[2,256,512]{2,1,0:T(8,128)(2,1)S(1)} %collective-permute-done.26.got, f32[4,512,512]{2,1,0:T(8,128)S(1)} %copy-done.1, f32[8,128]{1,0:T(8,128)S(1)} %get-tuple-element.133.token), custom_call_target="tpu_custom_call" | custom-call | flops 10000000 | bytes 6000000 | tf_op jit(solution)/shard_map/update_small/pallas_call | solution.py:1281
  (62 shorter events, 1.3 us)
Async XLA Ops:
  0.6 3.2 %copy-start.6 = (bf16[768,512]{1,0:T(8,128)(2,1)S(1)}, bf16[768,512]{1,0:T(8,128)(2,1)}, u32[]{:S(2)}) copy-start(bf16[768,512]{1,0:T(8,128)(2,1)} %features.5) | copy-start | bytes 2359300
  1.8 10.4 %copy-start.9 = (f32[512,1024]{1,0:T(8,128)S(1)}, f32[512,1024]{1,0:T(8,128)}, u32[]{:S(2)}) copy-start(f32[512,1024]{1,0:T(8,128)} %up_weight.1) | copy-start | bytes 6291460
  3.8 11.7 %copy-start.13 = (f32[2,4,512]{2,1,0:T(4,128)S(1)}, f32[2,4,512]{2,1,0:T(4,128)}, u32[]{:S(2)}) copy-start(f32[2,4,512]{2,1,0:T(4,128)} %modulation.1) | copy-start | bytes 49156
  4.6 18.1 %collective-permute-start.1 = (bf16[192,640]{1,0:T(8,128)(2,1)}, bf16[192,640]{1,0:T(8,128)(2,1)}, u32[]{:S(2)}, u32[]{:S(2)}) collective-permute-start(bf16[192,640]{1,0:T(8,128)(2,1)} %get-tuple-element.142), channel_id=1, source_target_pairs={{1,0},{2,1},{3,2},{4,3},{5,4},{6,5},{7,6},{8,7},{9,8},{10,9},{11,1... | collective-permute-start | bytes 737288 | tf_op jit(solution)/shard_map/ppermute | solution.py:771
  5.9 16.8 %collective-permute-start = (bf16[192,640]{1,0:T(8,128)(2,1)S(1)}, bf16[192,640]{1,0:T(8,128)(2,1)}, u32[]{:S(2)}, u32[]{:S(2)}) collective-permute-start(bf16[192,640]{1,0:T(8,128)(2,1)S(1)} %get-tuple-element.143.token), channel_id=1, source_target_pairs={{0,1},{1,2},{2,3},{3,4},{4,5},{5,6},{6,7},{7,8},{8,9},{9,10},{10,1... | collective-permute-start | bytes 737288 | tf_op jit(solution)/shard_map/ppermute | solution.py:771
  12.2 1.6 copy-start.10
  13.8 2.2 %copy-start = (f32[4,512,512]{2,1,0:T(8,128)S(1)}, f32[4,512,512]{2,1,0:T(8,128)}, u32[]{:S(2)}) copy-start(f32[4,512,512]{2,1,0:T(8,128)} %weight.1) | copy-start | bytes 12582916
  13.8 8.1 %copy-start.7 = (f32[4,256,512]{2,1,0:T(8,128)S(1)}, f32[4,256,512]{2,1,0:T(8,128)}, u32[]{:S(2)}) copy-start(f32[4,256,512]{2,1,0:T(8,128)} %moment.1) | copy-start | bytes 6291460
  14.4 7.4 %copy-start.2 = (f32[512,1024]{1,0:T(8,128)S(1)}, f32[512,1024]{1,0:T(8,128)}, u32[]{:S(2)}) copy-start(f32[512,1024]{1,0:T(8,128)} %up_moment.1) | copy-start | bytes 6291460
  14.5 7.4 %copy-start.4 = (f32[1024,512]{1,0:T(8,128)S(1)}, f32[1024,512]{1,0:T(8,128)}, u32[]{:S(2)}) copy-start(f32[1024,512]{1,0:T(8,128)} %down_moment.1) | copy-start | bytes 6291460
  14.5 28.9 %collective-permute-start.2 = (bf16[2,512,512]{2,1,0:T(8,128)(2,1)S(1)}, bf16[2,512,512]{2,1,0:T(8,128)(2,1)S(1)}, u32[]{:S(2)}, u32[]{:S(2)}) collective-permute-start(bf16[2,512,512]{2,1,0:T(8,128)(2,1)S(1)} %quarter.1), channel_id=1, source_target_pairs={{0,1},{1,0},{2,3},{3,2},{4,5},{5,4},{6,7},{7,6},{8,9},{9,8},{10,11... | collective-permute-start | bytes 3145736 | tf_op jit(solution)/shard_map/ppermute | solution.py:779
  22.7 10.0 %copy-start.11 = (f32[1024,512]{1,0:T(8,128)S(1)}, f32[1024,512]{1,0:T(8,128)}, u32[]{:S(2)}) copy-start(f32[1024,512]{1,0:T(8,128)} %down_weight.1) | copy-start | bytes 6291460
  22.7 10.0 %copy-start.14 = (bf16[768,512]{1,0:T(8,128)(2,1)S(1)}, bf16[768,512]{1,0:T(8,128)(2,1)}, u32[]{:S(2)}) copy-start(bf16[768,512]{1,0:T(8,128)(2,1)} %cotangent.5) | copy-start | bytes 2359300
  43.3 3.9 %collective-permute-start.3 = (bf16[2,512,512]{2,1,0:T(8,128)(2,1)S(1)}, bf16[2,512,512]{2,1,0:T(8,128)(2,1)S(1)}, u32[]{:S(2)}, u32[]{:S(2)}) collective-permute-start(bf16[2,512,512]{2,1,0:T(8,128)(2,1)S(1)} %collective-permute-done.2.near), channel_id=1, source_target_pairs={{0,2},{1,3},{2,0},{3,1},{4,6},{5,7},{6,4},{7,5},{8,10},{9,11},{10,... | collective-permute-start | bytes 3145736 | tf_op jit(solution)/shard_map/ppermute | solution.py:779
  43.4 9.7 %collective-permute-start.4 = (bf16[2,2,2,128,512]{4,3,2,1,0:T(8,128)(2,1)S(1)}, bf16[2,2,2,128,512]{4,3,2,1,0:T(8,128)(2,1)S(1)}, u32[]{:S(2)}, u32[]{:S(2)}) collective-permute-start(bf16[2,2,2,128,512]{4,3,2,1,0:T(8,128)(2,1)S(1)} %get-tuple-element.94), channel_id=1, source_target_pairs={{0,2},{1,3},{2,0},{3,1},{4,6},{5,7},{6,4},{7,5},{8,10},{9,11},{10,... | collective-permute-start | bytes 3145736 | tf_op jit(solution)/shard_map/ppermute | solution.py:779
  53.0 2.7 %collective-permute-start.5 = (bf16[2,2,2,128,512]{4,3,2,1,0:T(8,128)(2,1)S(1)}, bf16[2,2,2,128,512]{4,3,2,1,0:T(8,128)(2,1)S(1)}, u32[]{:S(2)}, u32[]{:S(2)}) collective-permute-start(bf16[2,2,2,128,512]{4,3,2,1,0:T(8,128)(2,1)S(1)} %get-tuple-element.96), channel_id=1, source_target_pairs={{0,2},{1,3},{2,0},{3,1},{4,6},{5,7},{6,4},{7,5},{8,10},{9,11},{10,... | collective-permute-start | bytes 3145736 | tf_op jit(solution)/shard_map/ppermute | solution.py:779
  56.7 16.3 %collective-permute-start.6 = (bf16[2,2,2,128,512]{4,3,2,1,0:T(8,128)(2,1)S(1)}, bf16[2,2,2,128,512]{4,3,2,1,0:T(8,128)(2,1)S(1)}, u32[]{:S(2)}, u32[]{:S(2)}) collective-permute-start(bf16[2,2,2,128,512]{4,3,2,1,0:T(8,128)(2,1)S(1)} %get-tuple-element.98.token), channel_id=1, source_target_pairs={{0,4},{1,5},{2,10},{3,11},{4,0},{5,1},{6,14},{7,15},{8,12},{9,13},... | collective-permute-start | bytes 3145736 | tf_op jit(solution)/shard_map/ppermute | solution.py:779
  58.0 18.2 %collective-permute-start.7 = (bf16[192,640]{1,0:T(8,128)(2,1)S(1)}, bf16[192,640]{1,0:T(8,128)(2,1)S(1)}, u32[]{:S(2)}, u32[]{:S(2)}) collective-permute-start(bf16[192,640]{1,0:T(8,128)(2,1)S(1)} %get-tuple-element.108), channel_id=1, source_target_pairs={{0,1},{1,2},{2,3},{3,4},{4,5},{5,6},{6,7},{7,8},{8,9},{9,10},{10,1... | collective-permute-start | bytes 737288 | tf_op jit(solution)/shard_map/ppermute | solution.py:771
  62.4 13.8 %collective-permute-start.8 = (bf16[192,640]{1,0:T(8,128)(2,1)S(1)}, bf16[192,640]{1,0:T(8,128)(2,1)S(1)}, u32[]{:S(2)}, u32[]{:S(2)}) collective-permute-start(bf16[192,640]{1,0:T(8,128)(2,1)S(1)} %get-tuple-element.109), channel_id=1, source_target_pairs={{1,0},{2,1},{3,2},{4,3},{5,4},{6,5},{7,6},{8,7},{9,8},{10,9},{11,1... | collective-permute-start | bytes 737288 | tf_op jit(solution)/shard_map/ppermute | solution.py:771
  73.1 11.3 %collective-permute-start.10 = (bf16[2,256,512]{2,1,0:T(8,128)(2,1)S(1)}, bf16[2,256,512]{2,1,0:T(8,128)(2,1)S(1)}, u32[]{:S(2)}, u32[]{:S(2)}) collective-permute-start(bf16[2,256,512]{2,1,0:T(8,128)(2,1)S(1)} %bitcast.47), channel_id=1, source_target_pairs={{0,1},{1,0},{2,6},{3,7},{4,5},{5,4},{6,2},{7,3},{8,9},{9,8},{10,14... | collective-permute-start | bytes 1572872 | tf_op jit(solution)/shard_map/ppermute | solution.py:779
  84.4 3.0 %collective-permute-start.9 = (bf16[2,2,2,2,80,512]{5,4,3,2,1,0:T(8,128)(2,1)S(1)}, bf16[2,2,2,2,80,512]{5,4,3,2,1,0:T(8,128)(2,1)S(1)}, u32[]{:S(2)}, u32[]{:S(2)}) collective-permute-start(bf16[2,2,2,2,80,512]{5,4,3,2,1,0:T(8,128)(2,1)S(1)} %get-tuple-element.115.refs_2_), channel_id=1, source_target_pairs={{0,2},{1,3},{2,0},{3,1},{4,6},{5,7},{6,4},{7,5},{8,10},{9,11},{10,... | collective-permute-start | bytes 3932168 | tf_op jit(solution)/shard_map/ppermute | solution.py:779
  84.5 6.9 %collective-permute-start.12 = (bf16[2,128,512]{2,1,0:T(8,128)(2,1)S(1)}, bf16[2,128,512]{2,1,0:T(8,128)(2,1)S(1)}, u32[]{:S(2)}, u32[]{:S(2)}) collective-permute-start(bf16[2,128,512]{2,1,0:T(8,128)(2,1)S(1)} %bitcast.57), channel_id=1, source_target_pairs={{0,8},{1,9},{2,3},{3,2},{4,12},{5,13},{6,7},{7,6},{8,0},{9,1},{10,... | collective-permute-start | bytes 786440 | tf_op jit(solution)/shard_map/ppermute | solution.py:779
  87.7 10.7 %collective-permute-start.11 = (bf16[2,320,512]{2,1,0:T(8,128)(2,1)S(1)}, bf16[2,320,512]{2,1,0:T(8,128)(2,1)S(1)}, u32[]{:S(2)}, u32[]{:S(2)}) collective-permute-start(bf16[2,320,512]{2,1,0:T(8,128)(2,1)S(1)} %bitcast.45), channel_id=1, source_target_pairs={{0,4},{1,5},{2,10},{3,11},{4,0},{5,1},{6,14},{7,15},{8,12},{9,13},... | collective-permute-start | bytes 1966088 | tf_op jit(solution)/shard_map/ppermute | solution.py:779
  91.4 11.3 %collective-permute-start.14 = (bf16[2,128,512]{2,1,0:T(8,128)(2,1)S(1)}, bf16[2,128,512]{2,1,0:T(8,128)(2,1)S(1)}, u32[]{:S(2)}, u32[]{:S(2)}) collective-permute-start(bf16[2,128,512]{2,1,0:T(8,128)(2,1)S(1)} %total.2.refs_2_.refs_0_), channel_id=1, source_target_pairs={{0,16},{1,17},{2,18},{3,19},{4,20},{5,21},{6,22},{7,23},{8,24},{9,... | collective-permute-start | bytes 786440 | tf_op jit(solution)/shard_map/ppermute | solution.py:779
  98.5 8.2 %collective-permute-start.13 = (bf16[2,160,512]{2,1,0:T(8,128)(2,1)S(1)}, bf16[2,160,512]{2,1,0:T(8,128)(2,1)S(1)}, u32[]{:S(2)}, u32[]{:S(2)}) collective-permute-start(bf16[2,160,512]{2,1,0:T(8,128)(2,1)S(1)} %bitcast.52), channel_id=1, source_target_pairs={{0,1},{1,0},{2,3},{3,2},{4,5},{5,4},{6,7},{7,6},{8,9},{9,8},{10,11... | collective-permute-start | bytes 983048 | tf_op jit(solution)/shard_map/ppermute | solution.py:779
  102.8 8.2 %collective-permute-start.16 = (bf16[256,512]{1,0:T(8,128)(2,1)S(1)}, bf16[256,512]{1,0:T(8,128)(2,1)S(1)}, u32[]{:S(2)}, u32[]{:S(2)}) collective-permute-start(bf16[256,512]{1,0:T(8,128)(2,1)S(1)} %bitcast.54), channel_id=1, source_target_pairs={{0,8},{1,9},{2,3},{3,2},{4,12},{5,13},{6,7},{7,6},{8,0},{9,1},{10,... | collective-permute-start | bytes 786440 | tf_op jit(solution)/shard_map/ppermute | solution.py:779
  106.7 6.0 %collective-permute-start.15 = (bf16[2,80,512]{2,1,0:T(8,128)(2,1)S(1)}, bf16[2,80,512]{2,1,0:T(8,128)(2,1)S(1)}, u32[]{:S(2)}, u32[]{:S(2)}) collective-permute-start(bf16[2,80,512]{2,1,0:T(8,128)(2,1)S(1)} %bitcast.59), channel_id=1, source_target_pairs={{0,8},{1,9},{2,6},{3,7},{4,12},{5,13},{6,2},{7,3},{8,0},{9,1},{10,... | collective-permute-start | bytes 491528 | tf_op jit(solution)/shard_map/ppermute | solution.py:779
  111.1 9.2 %collective-permute-start.18 = (bf16[512,512]{1,0:T(8,128)(2,1)S(1)}, bf16[512,512]{1,0:T(8,128)(2,1)S(1)}, u32[]{:S(2)}, u32[]{:S(2)}) collective-permute-start(bf16[512,512]{1,0:T(8,128)(2,1)S(1)} %bitcast.49), channel_id=1, source_target_pairs={{0,1},{1,0},{2,6},{3,7},{4,5},{5,4},{6,2},{7,3},{8,9},{9,8},{10,14... | collective-permute-start | bytes 1572872 | tf_op jit(solution)/shard_map/ppermute | solution.py:779
  112.8 11.8 %collective-permute-start.17 = (bf16[2,80,512]{2,1,0:T(8,128)(2,1)S(1)}, bf16[2,80,512]{2,1,0:T(8,128)(2,1)S(1)}, u32[]{:S(2)}, u32[]{:S(2)}) collective-permute-start(bf16[2,80,512]{2,1,0:T(8,128)(2,1)S(1)} %total.3.refs_2_.refs_0_), channel_id=1, source_target_pairs={{0,16},{1,17},{2,18},{3,19},{4,20},{5,21},{6,22},{7,23},{8,24},{9,... | collective-permute-start | bytes 491528 | tf_op jit(solution)/shard_map/ppermute | solution.py:779
  120.4 16.6 %collective-permute-start.21 = (bf16[1024,512]{1,0:T(8,128)(2,1)S(1)}, bf16[1024,512]{1,0:T(8,128)(2,1)S(1)}, u32[]{:S(2)}, u32[]{:S(2)}) collective-permute-start(bf16[1024,512]{1,0:T(8,128)(2,1)S(1)} %bitcast.32), channel_id=1, source_target_pairs={{0,4},{1,5},{2,10},{3,11},{4,0},{5,1},{6,14},{7,15},{8,12},{9,13},... | collective-permute-start | bytes 3145736 | tf_op jit(solution)/shard_map/ppermute | solution.py:779
  124.7 7.1 %collective-permute-start.19 = (bf16[160,512]{1,0:T(8,128)(2,1)S(1)}, bf16[160,512]{1,0:T(8,128)(2,1)S(1)}, u32[]{:S(2)}, u32[]{:S(2)}) collective-permute-start(bf16[160,512]{1,0:T(8,128)(2,1)S(1)} %bitcast.39), channel_id=1, source_target_pairs={{0,8},{1,9},{2,6},{3,7},{4,12},{5,13},{6,2},{7,3},{8,0},{9,1},{10,... | collective-permute-start | bytes 491528 | tf_op jit(solution)/shard_map/ppermute | solution.py:779
  131.9 12.6 %collective-permute-start.20 = (bf16[320,512]{1,0:T(8,128)(2,1)S(1)}, bf16[320,512]{1,0:T(8,128)(2,1)S(1)}, u32[]{:S(2)}, u32[]{:S(2)}) collective-permute-start(bf16[320,512]{1,0:T(8,128)(2,1)S(1)} %bitcast.29), channel_id=1, source_target_pairs={{0,1},{1,0},{2,3},{3,2},{4,5},{5,4},{6,7},{7,6},{8,9},{9,8},{10,11... | collective-permute-start | bytes 983048 | tf_op jit(solution)/shard_map/ppermute | solution.py:779
  143.5 8.4 %collective-permute-start.23 = (bf16[2,512,512]{2,1,0:T(8,128)(2,1)S(1)}, bf16[2,512,512]{2,1,0:T(8,128)(2,1)S(1)}, u32[]{:S(2)}, u32[]{:S(2)}) collective-permute-start(bf16[2,512,512]{2,1,0:T(8,128)(2,1)S(1)} %get-tuple-element.127.own), channel_id=1, source_target_pairs={{0,2},{1,3},{2,0},{3,1},{4,6},{5,7},{6,4},{7,5},{8,10},{9,11},{10,... | collective-permute-start | bytes 3145736 | tf_op jit(solution)/shard_map/ppermute | solution.py:779
  144.5 7.4 %copy-start.5 = (f32[1024,512]{1,0:T(8,128)S(1)}, f32[1024,512]{1,0:T(8,128)}, u32[]{:S(2)}) copy-start(f32[1024,512]{1,0:T(8,128)} %down_moment.1) | copy-start | bytes 6291460
  144.6 7.4 %copy-start.3 = (f32[512,1024]{1,0:T(8,128)S(1)}, f32[512,1024]{1,0:T(8,128)}, u32[]{:S(2)}) copy-start(f32[512,1024]{1,0:T(8,128)} %up_moment.1) | copy-start | bytes 6291460
  144.6 10.7 %collective-permute-start.22 = (bf16[640,512]{1,0:T(8,128)(2,1)S(1)}, bf16[640,512]{1,0:T(8,128)(2,1)S(1)}, u32[]{:S(2)}, u32[]{:S(2)}) collective-permute-start(bf16[640,512]{1,0:T(8,128)(2,1)S(1)} %bitcast.36), channel_id=1, source_target_pairs={{0,4},{1,5},{2,10},{3,11},{4,0},{5,1},{6,14},{7,15},{8,12},{9,13},... | collective-permute-start | bytes 1966088 | tf_op jit(solution)/shard_map/ppermute | solution.py:779
  151.5 4.6 %collective-permute-start.25 = (bf16[2,512,512]{2,1,0:T(8,128)(2,1)S(1)}, bf16[2,512,512]{2,1,0:T(8,128)(2,1)S(1)}, u32[]{:S(2)}, u32[]{:S(2)}) collective-permute-start(bf16[2,512,512]{2,1,0:T(8,128)(2,1)S(1)} %ortho_large.3.token.own), channel_id=1, source_target_pairs={{0,2},{1,3},{2,0},{3,1},{4,6},{5,7},{6,4},{7,5},{8,10},{9,11},{10,... | collective-permute-start | bytes 3145736 | tf_op jit(solution)/shard_map/ppermute | solution.py:779
  155.2 1.6 copy-start.12
  155.9 12.3 %collective-permute-start.24 = (bf16[2,272,512]{2,1,0:T(8,128)(2,1)S(1)}, bf16[2,272,512]{2,1,0:T(8,128)(2,1)S(1)}, u32[]{:S(2)}, u32[]{:S(2)}) collective-permute-start(bf16[2,272,512]{2,1,0:T(8,128)(2,1)S(1)} %get-tuple-element.129.mix.table), channel_id=1, source_target_pairs={{0,2},{1,3},{2,0},{3,1},{4,6},{5,7},{6,4},{7,5},{8,10},{9,11},{10,... | collective-permute-start | bytes 1671176 | tf_op jit(solution)/shard_map/ppermute | solution.py:779
  156.8 11.5 %copy-start.8 = (f32[4,256,512]{2,1,0:T(8,128)S(1)}, f32[4,256,512]{2,1,0:T(8,128)}, u32[]{:S(2)}) copy-start(f32[4,256,512]{2,1,0:T(8,128)} %moment.1) | copy-start | bytes 6291460
  156.8 11.5 %copy-start.15 = (f32[2,2,512]{2,1,0:T(2,128)S(1)}, f32[2,2,512]{2,1,0:T(2,128)}, u32[]{:S(2)}) copy-start(f32[2,2,512]{2,1,0:T(2,128)} %held_moment.1) | copy-start | bytes 24580
  168.1 2.7 %collective-permute-start.26 = (bf16[2,256,512]{2,1,0:T(8,128)(2,1)S(1)}, bf16[2,256,512]{2,1,0:T(8,128)(2,1)S(1)}, u32[]{:S(2)}, u32[]{:S(2)}) collective-permute-start(bf16[2,256,512]{2,1,0:T(8,128)(2,1)S(1)} %get-tuple-element.131.token.own), channel_id=1, source_target_pairs={{0,2},{1,3},{2,0},{3,1},{4,6},{5,7},{6,4},{7,5},{8,10},{9,11},{10,... | collective-permute-start | bytes 1572872 | tf_op jit(solution)/shard_map/ppermute | solution.py:779
  168.3 2.7 %copy-start.1 = (f32[4,512,512]{2,1,0:T(8,128)S(1)}, f32[4,512,512]{2,1,0:T(8,128)}, u32[]{:S(2)}) copy-start(f32[4,512,512]{2,1,0:T(8,128)} %weight.1) | copy-start | bytes 12582916

commit v3 on v2

--- a/solution.py
+++ b/solution.py
@@ -159,6 +159,8 @@
 def forward_kernel(
     rim_low,
     rim_high,
+    info_low,
+    info_high,
     features,
     pack,
     mod,
@@ -175,14 +177,14 @@
     rim_in,
 ):
     row_count = features.shape[0]
-    for side, rim in enumerate((rim_low, rim_high)):
+    for side, (rim, rim_info) in enumerate(((rim_low, info_low), (rim_high, info_high))):
 
         def rim_step(b, carry):
             rows = rows_of(b * 64, 64)
             target = pl.ds(pl.multiple_of(side * HALO + b * 64, 64), 64)
-            info = rim[rows, D:].astype(f32)
+            info = rim_info[rows, :].astype(f32)
             rim_in[target, :] = modulated(
-                rim[rows, :D].astype(f32), info[:, K : K + 1], mod, 0
+                rim[rows, :].astype(f32), info[:, K : K + 1], mod, 0
             ).astype(bf16)
             rim_counts[target, :] = slot_counts(
                 info, 64, RIM, b * 64 + (-HALO if side == 0 else RIM)
@@ -784,10 +786,11 @@
     pack = jnp.concatenate(
         [offsets, levels[:, None], jnp.zeros((row_count, 128 - K - 1), jnp.int32)], axis=1
     ).astype(f32)
-    rims = jnp.concatenate([features, pack.astype(bf16)], axis=1)
-    low_edge, high_edge = rims[row_count - HALO :], rims[:HALO]
-    rim_low = along(low_edge, 1)
-    rim_high = along(high_edge, -1)
+    rim_low = along(features[row_count - HALO :], 1)
+    rim_high = along(features[:HALO], -1)
+    low_edge = pack[row_count - HALO :].astype(bf16)
+    info_low = along(low_edge, 1)
+    info_high = along(pack[:HALO].astype(bf16), -1)
 
     pack, scalars, is_first = lax.optimization_barrier((pack, scalars, is_first))
     mod = modulation
@@ -868,13 +871,13 @@
             struct((2 * HALO, RIM), bf16),
             struct((row_count, 128), f32),
         ),
-        in_specs=[VMEM] * 8,
+        in_specs=[VMEM] * 10,
         out_specs=(VMEM,) * 7,
         scratch_shapes=[pltpu.VMEM((2 * HALO, D), bf16)],
         cost_estimate=cost(1e3, 1e3),
         name="attend",
         compiler_params=room(12),
-    )(rim_low, rim_high, features, pack, mod, attn_bf, qkv, counts)
+    )(rim_low, rim_high, info_low, info_high, features, pack, mod, attn_bf, qkv, counts)
 
     def whole(*shape):
         return pl.BlockSpec(shape, lambda g, s: (0,) * len(shape))
@@ -901,7 +904,7 @@
             ),
             scratch_shapes=[pltpu.VMEM((row_count, CHUNK), bf16)] * 2,
         ),
-        cost_estimate=cost(1e10, 1e3),
+        cost_estimate=cost(1.3e10, 1e3),
         name="mlp_own",
         compiler_params=room(14),
     )(scalars, second_in, cotangent, up_weight, down_weight, small_past)

time: 174 us -> 180 us (1.034)
  starting transfers between devices: 39 us -> 48.7 us
  waiting for transfers between devices: 42.2 us -> 37.3 us
  local copies, waits for them, and re-layouts: 4.17 us -> 6.71 us
    ppermute x23, starting transfers between devices: 25.9 us -> 31 us  [swap(): return lax.ppermute(value, AXES, pairs)]
    ppermute x23, waiting for transfers between devices: 42.2 us -> 37.2 us  [swap(): return lax.ppermute(value, AXES, pairs)]
    ppermute x4 -> x6, starting transfers between devices: 13.2 us -> 17.7 us  [along(): return lax.ppermute(value, AXES, pairs)]
    unnamed x32 -> x34, local copies, waits for them, and re-layouts: 2.86 us -> 4.48 us
  transfers between devices with their start and end apart: 27 -> 29, of which waited for: 13 -> 13; matrix products, arithmetic and copies ran while one was open for 0% -> 2% of each run, Pallas kernels for 47% -> 45%
where the time goes in v3:
time: 180 us; the launch traced here: 179 us
  Pallas kernels  83.3 us (46%)
  starting transfers between devices  48.7 us (27%)
  waiting for transfers between devices  37.3 us (21%)
  local copies, waits for them, and re-layouts  6.71 us (4%)
  other arithmetic  1.98 us (1%)
    ppermute x23, waiting for transfers between devices, swap(): return lax.ppermute(value, AXES, pairs)  37.2 us
    ppermute x23, starting transfers between devices, swap(): return lax.ppermute(value, AXES, pairs)  31 us
    ppermute x6, starting transfers between devices, along(): return lax.ppermute(value, AXES, pairs)  17.7 us
    pallas_call x1, Pallas kernels, on_device(): pl.pallas_call(small_kernel, grid=(NS_STEPS,), out_shape=(struct((2, 256,...  11.3 us
    pallas_call x1, Pallas kernels, on_device(): pl.pallas_call(forward_kernel, out_shape=(struct((row_count, D), bf16), s...  8.7 us
    pallas_call x1, Pallas kernels, on_device(): pl.pallas_call(weights_kernel, out_shape=(struct((row_count, D), f32), pi...  8.26 us
    pallas_call x1, Pallas kernels, on_device(): pl.pallas_call(backward_kernel, out_shape=(struct((row_count, D), bf16),)...  8.13 us
    pallas_call x1, Pallas kernels, on_device(): pl.pallas_call(mlp_own_kernel, out_shape=(struct((row_count, D), f32), st...  6.81 us
  transfers between devices with their start and end apart: 29, of which 13 were waited for; matrix products, arithmetic and copies ran while one was open for 2% of the time, Pallas kernels for 45%

profile of v3, /device:TPU:0, one launch (start us, length us, event | category | flops | bytes accessed | tf_op | source)
XLA Modules:
  0.0 179.1 jit_solution(3875374836688437161)
XLA Ops:
  0.6 1.1 fusion.2
  1.7 1.3 collective-permute-start.1
  3.0 5.5 %collective-permute-start = (bf16[192,512]{1,0:T(8,128)(2,1)S(1)}, bf16[192,512]{1,0:T(8,128)(2,1)S(1)}, u32[]{:S(2)}, u32[]{:S(2)}) collective-permute-start(bf16[192,512]{1,0:T(8,128)(2,1)S(1)} %get-tuple-element.143), channel_id=1, source_target_pairs={{0,1},{1,2},{2,3},{3,4},{4,5},{5,6},{6,7},{7,8},{8,9},{9,10},{10,1... | collective-permute-start | bytes 589832 | tf_op jit(solution)/shard_map/ppermute | solution.py:773
  8.6 0.8 broadcast_subtract_fusion
  9.6 0.8 broadcast_in_dim.16
  10.4 1.0 fusion
  11.7 1.3 collective-permute-start.3
  13.0 4.5 %collective-permute-start.2 = (bf16[192,128]{1,0:T(8,128)(2,1)S(1)}, bf16[192,128]{1,0:T(8,128)(2,1)S(1)}, u32[]{:S(2)}, u32[]{:S(2)}) collective-permute-start(bf16[192,128]{1,0:T(8,128)(2,1)S(1)} %get-tuple-element.145.token), channel_id=1, source_target_pairs={{0,1},{1,2},{2,3},{3,4},{4,5},{5,6},{6,7},{7,8},{8,9},{9,10},{10,1... | collective-permute-start | bytes 147464 | tf_op jit(solution)/shard_map/ppermute | solution.py:773
  17.6 1.6 copy-done.8
  19.2 1.6 copy-done.11
  20.8 0.6 quarter.1
  21.5 1.5 collective-permute-start.4
  23.0 0.2 copy-done.6
  23.2 5.9 %project.1 = (bf16[768,512]{1,0:T(8,128)(2,1)S(1)}, bf16[3,768,512]{2,1,0:T(8,128)(2,1)S(1)}, bf16[768,512]{1,0:T(8,128)(2,1)S(1)}, bf16[4,512,512]{2,1,0:T(8,128)(2,1)S(1)}) custom-call(bf16[768,512]{1,0:T(8,128)(2,1)S(1)} %copy-done.6, f32[768,128]{1,0:T(8,128)S(1)} %get-tuple-element.76.pack, f32[2,4,512]{2,1,0:T(4,128)S(1)} %copy-done.14, ...), custom_call_target="tpu_custom_call" | custom-call | flops 1000 | bytes 1000 | tf_op jit(solution)/shard_map/project/pallas_call | solution.py:835
  29.1 0.8 past.1
  30.0 8.7 %attend.1 = (bf16[768,512]{1,0:T(8,128)(2,1)S(1)}, f32[768,512]{1,0:T(8,128)S(1)}, bf16[768,512]{1,0:T(8,128)(2,1)S(1)}, bf16[2,1152,512]{2,1,0:T(8,128)(2,1)S(1...) custom-call(bf16[192,512]{1,0:T(8,128)(2,1)S(1)} %collective-permute-done.rim_low, ...), custom_call_target="tpu_custom_call" | custom-call | flops 1000 | bytes 1000 | tf_op jit(solution)/shard_map/attend/pallas_call | solution.py:863
  38.7 6.8 %mlp_own.1 = (f32[768,512]{1,0:T(8,128)S(1)}, f32[768,512]{1,0:T(8,128)S(1)}, bf16[2,2,2,128,512]{4,3,2,1,0:T(8,128)(2,1)S(1)}, bf16[2,2,2,128,512]{4,3,2,1,0:T(8,128)(2,1)S(1)}) custom-call(s32[5]{0:T(128)S(1)} %stack.23.scalars, bf16[768,512]{1,0:T(8,128)(2,1)S(1)} %get-tuple-element.80.second_in, bf16[768,512]{1,0:T(8,128)(2,1)S(1)} %copy-done.15, ...), custom_call_target="tpu_custom_call" | custom-call | flops 12999999488 | bytes 1000 | tf_op jit(solution)/shard_map/mlp_own/pallas_call | solution.py:886
  45.5 1.7 collective-permute-done.4.near
  47.4 0.3 collective-permute-start.6
  47.7 3.4 %mlp_near.1 = (f32[768,512]{1,0:T(8,128)S(1)}, f32[768,512]{1,0:T(8,128)S(1)}, bf16[2,2,2,128,512]{4,3,2,1,0:T(8,128)(2,1)S(1)}, bf16[2,2,2,128,512]{4,3,2,1,0:T(8,128)(2,1)S(1)}) custom-call(s32[5]{0:T(128)S(1)} %stack.23.scalars, bf16[768,512]{1,0:T(8,128)(2,1)S(1)} %get-tuple-element.80.second_in, bf16[768,512]{1,0:T(8,128)(2,1)S(1)} %copy-done.15, ...), custom_call_target="tpu_custom_call" | custom-call | flops 2500000000 | bytes 4000000 | tf_op jit(solution)/shard_map/mlp_near/pallas_call | solution.py:917
  51.1 5.7 %mlp_far.1 = (bf16[2,2,2,128,512]{4,3,2,1,0:T(8,128)(2,1)S(1)}, bf16[2,2,2,128,512]{4,3,2,1,0:T(8,128)(2,1)S(1)}, bf16[768,512]{1,0:T(8,128)(2,1)}, f32[768,512]...) custom-call(s32[5]{0:T(128)S(1)} %stack.23.scalars, ...), custom_call_target="tpu_custom_call", output_to_operand_aliasing={{0}: (12, {}), {1}: (13, {})} | custom-call | flops 4000000000 | bytes 8000000 | tf_op jit(solution)/shard_map/mlp_far/pallas_call | solution.py:948
  56.8 0.2 collective-permute-start.7
  57.1 2.5 %collective-permute-done.7.rest_got = bf16[2,2,2,128,512]{4,3,2,1,0:T(8,128)(2,1)S(1)} collective-permute-done((bf16[2,2,2,128,512]{4,3,2,1,0:T(8,128)(2,1)S(1)}, bf16[2,2,2,128,512]{4,3,2,1,0:T(8,128)(2,1)S(1)}, u32[]{:S(2)}, u32[]{:S(2)}) %collective-permute-start.7) | collective-permute-done | bytes 1048608 | tf_op jit(solution)/shard_map/ppermute | solution.py:781
  59.5 1.0 large_sum.1
  60.5 2.6 %collective-permute-start.8 = (bf16[2,2,2,128,512]{4,3,2,1,0:T(8,128)(2,1)S(1)}, bf16[2,2,2,128,512]{4,3,2,1,0:T(8,128)(2,1)S(1)}, u32[]{:S(2)}, u32[]{:S(2)}) collective-permute-start(bf16[2,2,2,128,512]{4,3,2,1,0:T(8,128)(2,1)S(1)} %get-tuple-element.98.token), channel_id=1, source_target_pairs={{0,4},{1,5},{2,10},{3,11},{4,0},{5,1},{6,14},{7,15},{8,12},{9,13},... | collective-permute-start | bytes 3145736 | tf_op jit(solution)/shard_map/ppermute | solution.py:781
  63.1 3.8 %collective-permute-start.9 = (bf16[192,640]{1,0:T(8,128)(2,1)S(1)}, bf16[192,640]{1,0:T(8,128)(2,1)S(1)}, u32[]{:S(2)}, u32[]{:S(2)}) collective-permute-start(bf16[192,640]{1,0:T(8,128)(2,1)S(1)} %get-tuple-element.108), channel_id=1, source_target_pairs={{0,1},{1,2},{2,3},{3,4},{4,5},{5,6},{6,7},{7,8},{8,9},{9,10},{10,1... | collective-permute-start | bytes 737288 | tf_op jit(solution)/shard_map/ppermute | solution.py:773
  66.9 1.3 collective-permute-start.10
  68.2 8.1 %attend_back.1 = (bf16[768,512]{1,0:T(8,128)(2,1)S(1)}, f32[1152,512]{1,0:T(8,128)S(1)}, f32[1152,512]{1,0:T(8,128)S(1)}) custom-call(bf16[3,768,512]{2,1,0:T(8,128)(2,1)S(1)} %get-tuple-element.78.qkv, bf16[2,1152,512]{2,1,0:T(8,128)(2,1)S(1)} %get-tuple-element.99.padded, bf16[768,512]{1,0:T(8,128)(2,1)S(1)} %get-tuple-element.100.grad, ...), custom_call_target="tpu_custom_call" | custom-call | flops 8000000000 | bytes 9000000 | tf_op jit(solution)/shard_map/attend_back/pallas_call | solution.py:1091
  76.4 1.7 collective-permute-done.8
  78.2 2.4 %collective-permute-start.12 = (bf16[2,256,512]{2,1,0:T(8,128)(2,1)S(1)}, bf16[2,256,512]{2,1,0:T(8,128)(2,1)S(1)}, u32[]{:S(2)}, u32[]{:S(2)}) collective-permute-start(bf16[2,256,512]{2,1,0:T(8,128)(2,1)S(1)} %bitcast.47), channel_id=1, source_target_pairs={{0,1},{1,0},{2,6},{3,7},{4,5},{5,4},{6,2},{7,3},{8,9},{9,8},{10,14... | collective-permute-start | bytes 1572872 | tf_op jit(solution)/shard_map/ppermute | solution.py:781
  80.7 8.3 %attend_weights.1 = (f32[768,512]{1,0:T(8,128)}, bf16[2,2,2,2,80,512]{5,4,3,2,1,0:T(8,128)(2,1)S(1)}, bf16[2,2,2,2,80,512]{5,4,3,2,1,0:T(8,128)(2,1)S(1)}) custom-call(s32[5]{0:T(128)S(1)} %stack.23.scalars, bf16[2,256,512]{2,1,0:T(8,128)(2,1)S(1)} %bitcast.48, bf16[768,512]{1,0:T(8,128)(2,1)S(1)} %get-tuple-element.102.refs_2_.queries_in, ...), custom_call_target="tpu_custom_call" | custom-call | flops 6000000000 | bytes 9000000 | tf_op jit(solution)/shard_map/attend_weights/pallas_call | solution.py:1103
  89.1 1.8 collective-permute-start.14
  90.8 1.1 collective-permute-done.11
  92.0 0.3 receive.7
  92.3 2.1 %collective-permute-start.13 = (bf16[2,320,512]{2,1,0:T(8,128)(2,1)S(1)}, bf16[2,320,512]{2,1,0:T(8,128)(2,1)S(1)}, u32[]{:S(2)}, u32[]{:S(2)}) collective-permute-start(bf16[2,320,512]{2,1,0:T(8,128)(2,1)S(1)} %bitcast.45), channel_id=1, source_target_pairs={{0,4},{1,5},{2,10},{3,11},{4,0},{5,1},{6,14},{7,15},{8,12},{9,13},... | collective-permute-start | bytes 1966088 | tf_op jit(solution)/shard_map/ppermute | solution.py:781
  94.3 1.6 collective-permute-done.14.refs_1_
  96.0 2.7 %collective-permute-start.16 = (bf16[2,128,512]{2,1,0:T(8,128)(2,1)S(1)}, bf16[2,128,512]{2,1,0:T(8,128)(2,1)S(1)}, u32[]{:S(2)}, u32[]{:S(2)}) collective-permute-start(bf16[2,128,512]{2,1,0:T(8,128)(2,1)S(1)} %total.2.refs_2_.refs_0_), channel_id=1, source_target_pairs={{0,16},{1,17},{2,18},{3,19},{4,20},{5,21},{6,22},{7,23},{8,24},{9,... | collective-permute-start | bytes 786440 | tf_op jit(solution)/shard_map/ppermute | solution.py:781
  98.7 4.2 %collective-permute-done.13.refs_1_ = bf16[2,320,512]{2,1,0:T(8,128)(2,1)S(1)} collective-permute-done((bf16[2,320,512]{2,1,0:T(8,128)(2,1)S(1)}, bf16[2,320,512]{2,1,0:T(8,128)(2,1)S(1)}, u32[]{:S(2)}, u32[]{:S(2)}) %collective-permute-start.13) | collective-permute-done | bytes 655392 | tf_op jit(solution)/shard_map/ppermute | solution.py:781
  103.2 4.0 %collective-permute-done.16.refs_1_ = bf16[2,128,512]{2,1,0:T(8,128)(2,1)S(1)} collective-permute-done((bf16[2,128,512]{2,1,0:T(8,128)(2,1)S(1)}, bf16[2,128,512]{2,1,0:T(8,128)(2,1)S(1)}, u32[]{:S(2)}, u32[]{:S(2)}) %collective-permute-start.16) | collective-permute-done | bytes 262176 | tf_op jit(solution)/shard_map/ppermute | solution.py:781
  107.3 3.2 %collective-permute-start.18 = (bf16[256,512]{1,0:T(8,128)(2,1)S(1)}, bf16[256,512]{1,0:T(8,128)(2,1)S(1)}, u32[]{:S(2)}, u32[]{:S(2)}) collective-permute-start(bf16[256,512]{1,0:T(8,128)(2,1)S(1)} %bitcast.54), channel_id=1, source_target_pairs={{0,8},{1,9},{2,3},{3,2},{4,12},{5,13},{6,7},{7,6},{8,0},{9,1},{10,... | collective-permute-start | bytes 786440 | tf_op jit(solution)/shard_map/ppermute | solution.py:781
  110.6 2.7 %collective-permute-start.17 = (bf16[2,80,512]{2,1,0:T(8,128)(2,1)S(1)}, bf16[2,80,512]{2,1,0:T(8,128)(2,1)S(1)}, u32[]{:S(2)}, u32[]{:S(2)}) collective-permute-start(bf16[2,80,512]{2,1,0:T(8,128)(2,1)S(1)} %bitcast.59), channel_id=1, source_target_pairs={{0,8},{1,9},{2,6},{3,7},{4,12},{5,13},{6,2},{7,3},{8,0},{9,1},{10,... | collective-permute-start | bytes 491528 | tf_op jit(solution)/shard_map/ppermute | solution.py:781
  113.3 1.6 collective-permute-done.18.refs_1_
  114.9 0.8 collective-permute-start.20
  115.6 1.0 collective-permute-done.17.refs_1_
  116.6 4.1 %collective-permute-start.19 = (bf16[2,80,512]{2,1,0:T(8,128)(2,1)S(1)}, bf16[2,80,512]{2,1,0:T(8,128)(2,1)S(1)}, u32[]{:S(2)}, u32[]{:S(2)}) collective-permute-start(bf16[2,80,512]{2,1,0:T(8,128)(2,1)S(1)} %total.3.refs_2_.refs_0_), channel_id=1, source_target_pairs={{0,16},{1,17},{2,18},{3,19},{4,20},{5,21},{6,22},{7,23},{8,24},{9,... | collective-permute-start | bytes 491528 | tf_op jit(solution)/shard_map/ppermute | solution.py:781
  120.8 3.3 %collective-permute-done.20.refs_1_ = bf16[512,512]{1,0:T(8,128)(2,1)S(1)} collective-permute-done((bf16[512,512]{1,0:T(8,128)(2,1)S(1)}, bf16[512,512]{1,0:T(8,128)(2,1)S(1)}, u32[]{:S(2)}, u32[]{:S(2)}) %collective-permute-start.20) | collective-permute-done | bytes 524320 | tf_op jit(solution)/shard_map/ppermute | solution.py:781
  124.2 1.3 collective-permute-start.23
  125.5 3.4 %collective-permute-done.19.refs_1_ = bf16[2,80,512]{2,1,0:T(8,128)(2,1)S(1)} collective-permute-done((bf16[2,80,512]{2,1,0:T(8,128)(2,1)S(1)}, bf16[2,80,512]{2,1,0:T(8,128)(2,1)S(1)}, u32[]{:S(2)}, u32[]{:S(2)}) %collective-permute-start.19) | collective-permute-done | bytes 163872 | tf_op jit(solution)/shard_map/ppermute | solution.py:781
  128.9 0.6 collective-permute-start.21
  129.5 6.6 %collective-permute-done.21.refs_1_ = bf16[160,512]{1,0:T(8,128)(2,1)S(1)} collective-permute-done((bf16[160,512]{1,0:T(8,128)(2,1)S(1)}, bf16[160,512]{1,0:T(8,128)(2,1)S(1)}, u32[]{:S(2)}, u32[]{:S(2)}) %collective-permute-start.21) | collective-permute-done | bytes 163872 | tf_op jit(solution)/shard_map/ppermute | solution.py:781
  136.2 4.7 %collective-permute-done.23 = bf16[1024,512]{1,0:T(8,128)(2,1)S(1)} collective-permute-done((bf16[1024,512]{1,0:T(8,128)(2,1)S(1)}, bf16[1024,512]{1,0:T(8,128)(2,1)S(1)}, u32[]{:S(2)}, u32[]{:S(2)}) %collective-permute-start.23) | collective-permute-done | bytes 1048608 | tf_op jit(solution)/shard_map/ppermute | solution.py:781
  140.8 6.5 %ortho_large.2 = (bf16[4,512,512]{2,1,0:T(8,128)(2,1)S(1)}, bf16[2,512,512]{2,1,0:T(8,128)(2,1)S(1)}) custom-call(s32[5]{0:T(128)S(1)} %stack.23.scalars, bf16[2,2,2,128,512]{4,3,2,1,0:T(8,128)(2,1)S(1)} %bitcast.34, bf16[2,2,2,128,512]{4,3,2,1,0:T(8,128)(2,1)S(1)} %bitcast.35, bf16[320,512]{1,0:T(8,128)(2,1)S(1)} %bitcast.30), custom_call_target="tpu_custom_call" | custom-call | flops 1000 | bytes 1000 | tf_op jit(solution)/shard_map/ortho_large/pallas_call | solution.py:1171
  147.3 1.7 collective-permute-start.25
  149.1 1.5 collective-permute-start.24
  150.6 5.9 %ortho_large.3.token.own = bf16[2,512,512]{2,1,0:T(8,128)(2,1)S(1)} custom-call(bf16[4,512,512]{2,1,0:T(8,128)(2,1)S(1)} %get-tuple-element.126.refs_2_.given, bf16[640,512]{1,0:T(8,128)(2,1)S(1)} %bitcast.37), custom_call_target="tpu_custom_call" | custom-call | flops 1000 | bytes 1000 | tf_op jit(solution)/shard_map/ortho_large/pallas_call | solution.py:1184
  156.6 3.3 %moment_large.1 = (f32[512,1024]{1,0:T(8,128)}, f32[1024,512]{1,0:T(8,128)}, f32[8,128]{1,0:T(8,128)S(1)}) custom-call(s32[5]{0:T(128)S(1)} %stack.23.scalars, bf16[2,512,512]{2,1,0:T(8,128)(2,1)S(1)} %get-tuple-element.127.own, bf16[2,512,512]{2,1,0:T(8,128)(2,1)S(1)} %collective-permute-done.25.got, f32[512,1024]{1,0:T(8,128)S(1)} %copy-done.3, ...), custom_call_target="tpu_custom_call" | custom-call | flops 1000 | bytes 1000 | tf_op jit(solution)/shard_map/moment_large/pallas_call | solution.py:1202
  159.9 0.7 unpack_small.1
  160.6 0.5 collective-permute-start.26
  161.1 0.3 copy-done.10
  161.5 0.6 copy-done.13
  162.1 11.3 %ortho_small.1 = (bf16[2,256,512]{2,1,0:T(8,128)(2,1)S(1)}, f32[512,1024]{1,0:T(8,128)}, f32[1024,512]{1,0:T(8,128)}) custom-call(s32[5]{0:T(128)S(1)} %stack.23.scalars, bf16[2,2,256,512]{3,2,1,0:T(8,128)(2,1)S(1)} %get-tuple-element.130.given, bf16[2,512,512]{2,1,0:T(8,128)(2,1)S(1)} %ortho_large.3.token.own, ...), custom_call_target="tpu_custom_call" | custom-call | flops 6000000000 | bytes 10000000 | tf_op jit(solution)/shard_map/ortho_small/pallas_call | solution.py:1239
  173.4 0.5 collective-permute-start.28
  173.8 2.6 %moment_small.1 = (f32[4,256,512]{2,1,0:T(8,128)}, f32[2,2,512]{2,1,0:T(2,128)}, f32[2,2,512]{2,1,0:T(2,128)}, f32[8,128]{1,0:T(8,128)S(1)}) custom-call(s32[5]{0:T(128)S(1)} %stack.23.scalars, bf16[2,272,512]{2,1,0:T(8,128)(2,1)S(1)} %get-tuple-element.129.mix.table, bf16[2,272,512]{2,1,0:T(8,128)(2,1)S(1)} %collective-permute-done.26.mix_got.table_got, ...), custom_call_target="tpu_custom_call" | custom-call | flops 10000000000 | bytes 10000000 | tf_op jit(solution)/shard_map/moment_small/pallas_call | solution.py:1254
  176.5 2.6 %update_small.1 = f32[4,256,512]{2,1,0:T(8,128)} custom-call(s32[5]{0:T(128)S(1)} %stack.23.scalars, bf16[2,256,512]{2,1,0:T(8,128)(2,1)S(1)} %get-tuple-element.131.token.own, bf16[2,256,512]{2,1,0:T(8,128)(2,1)S(1)} %collective-permute-done.28.got, f32[4,512,512]{2,1,0:T(8,128)S(1)} %copy-done.1, f32[8,128]{1,0:T(8,128)S(1)} %get-tuple-element.133.token), custom_call_target="tpu_custom_call" | custom-call | flops 10000000 | bytes 6000000 | tf_op jit(solution)/shard_map/update_small/pallas_call | solution.py:1284
  (69 shorter events, 2.1 us)
Async XLA Ops:
  1.7 28.2 %collective-permute-start.1 = (bf16[192,512]{1,0:T(8,128)(2,1)S(1)}, bf16[192,512]{1,0:T(8,128)(2,1)S(1)}, u32[]{:S(2)}, u32[]{:S(2)}) collective-permute-start(bf16[192,512]{1,0:T(8,128)(2,1)S(1)} %get-tuple-element.142), channel_id=1, source_target_pairs={{1,0},{2,1},{3,2},{4,3},{5,4},{6,5},{7,6},{8,7},{9,8},{10,9},{11,1... | collective-permute-start | bytes 589832 | tf_op jit(solution)/shard_map/ppermute | solution.py:773
  3.0 26.9 %collective-permute-start = (bf16[192,512]{1,0:T(8,128)(2,1)S(1)}, bf16[192,512]{1,0:T(8,128)(2,1)S(1)}, u32[]{:S(2)}, u32[]{:S(2)}) collective-permute-start(bf16[192,512]{1,0:T(8,128)(2,1)S(1)} %get-tuple-element.143), channel_id=1, source_target_pairs={{0,1},{1,2},{2,3},{3,4},{4,5},{5,6},{6,7},{7,8},{8,9},{9,10},{10,1... | collective-permute-start | bytes 589832 | tf_op jit(solution)/shard_map/ppermute | solution.py:773
  10.4 18.7 %copy-start.7 = (f32[4,256,512]{2,1,0:T(8,128)S(1)}, f32[4,256,512]{2,1,0:T(8,128)}, u32[]{:S(2)}) copy-start(f32[4,256,512]{2,1,0:T(8,128)} %moment.1) | copy-start | bytes 6291460
  11.7 18.2 %collective-permute-start.3 = (bf16[192,128]{1,0:T(8,128)(2,1)S(1)}, bf16[192,128]{1,0:T(8,128)(2,1)S(1)}, u32[]{:S(2)}, u32[]{:S(2)}) collective-permute-start(bf16[192,128]{1,0:T(8,128)(2,1)S(1)} %get-tuple-element.144), channel_id=1, source_target_pairs={{1,0},{2,1},{3,2},{4,3},{5,4},{6,5},{7,6},{8,7},{9,8},{10,9},{11,1... | collective-permute-start | bytes 147464 | tf_op jit(solution)/shard_map/ppermute | solution.py:773
  13.0 16.9 %collective-permute-start.2 = (bf16[192,128]{1,0:T(8,128)(2,1)S(1)}, bf16[192,128]{1,0:T(8,128)(2,1)S(1)}, u32[]{:S(2)}, u32[]{:S(2)}) collective-permute-start(bf16[192,128]{1,0:T(8,128)(2,1)S(1)} %get-tuple-element.145.token), channel_id=1, source_target_pairs={{0,1},{1,2},{2,3},{3,4},{4,5},{5,6},{6,7},{7,8},{8,9},{9,10},{10,1... | collective-permute-start | bytes 147464 | tf_op jit(solution)/shard_map/ppermute | solution.py:773
  17.6 1.6 copy-start.8
  19.2 1.6 copy-start.11
  20.8 2.2 %copy-start = (f32[4,512,512]{2,1,0:T(8,128)S(1)}, f32[4,512,512]{2,1,0:T(8,128)}, u32[]{:S(2)}) copy-start(f32[4,512,512]{2,1,0:T(8,128)} %weight.1) | copy-start | bytes 12582916
  20.8 2.4 %copy-start.6 = (bf16[768,512]{1,0:T(8,128)(2,1)S(1)}, bf16[768,512]{1,0:T(8,128)(2,1)}, u32[]{:S(2)}) copy-start(bf16[768,512]{1,0:T(8,128)(2,1)} %features.5) | copy-start | bytes 2359300
  20.8 2.4 %copy-start.14 = (f32[2,4,512]{2,1,0:T(4,128)S(1)}, f32[2,4,512]{2,1,0:T(4,128)}, u32[]{:S(2)}) copy-start(f32[2,4,512]{2,1,0:T(4,128)} %modulation.1) | copy-start | bytes 49156
  21.4 7.7 %copy-start.2 = (f32[512,1024]{1,0:T(8,128)S(1)}, f32[512,1024]{1,0:T(8,128)}, u32[]{:S(2)}) copy-start(f32[512,1024]{1,0:T(8,128)} %up_moment.1) | copy-start | bytes 6291460
  21.5 7.6 %copy-start.4 = (f32[1024,512]{1,0:T(8,128)S(1)}, f32[1024,512]{1,0:T(8,128)}, u32[]{:S(2)}) copy-start(f32[1024,512]{1,0:T(8,128)} %down_moment.1) | copy-start | bytes 6291460
  21.5 25.7 %collective-permute-start.4 = (bf16[2,512,512]{2,1,0:T(8,128)(2,1)S(1)}, bf16[2,512,512]{2,1,0:T(8,128)(2,1)S(1)}, u32[]{:S(2)}, u32[]{:S(2)}) collective-permute-start(bf16[2,512,512]{2,1,0:T(8,128)(2,1)S(1)} %quarter.1), channel_id=1, source_target_pairs={{0,1},{1,0},{2,3},{3,2},{4,5},{5,4},{6,7},{7,6},{8,9},{9,8},{10,11... | collective-permute-start | bytes 3145736 | tf_op jit(solution)/shard_map/ppermute | solution.py:781
  29.9 8.7 %copy-start.9 = (f32[512,1024]{1,0:T(8,128)S(1)}, f32[512,1024]{1,0:T(8,128)}, u32[]{:S(2)}) copy-start(f32[512,1024]{1,0:T(8,128)} %up_weight.1) | copy-start | bytes 6291460
  29.9 8.7 %copy-start.12 = (f32[1024,512]{1,0:T(8,128)S(1)}, f32[1024,512]{1,0:T(8,128)}, u32[]{:S(2)}) copy-start(f32[1024,512]{1,0:T(8,128)} %down_weight.1) | copy-start | bytes 6291460
  30.0 8.7 %copy-start.15 = (bf16[768,512]{1,0:T(8,128)(2,1)S(1)}, bf16[768,512]{1,0:T(8,128)(2,1)}, u32[]{:S(2)}) copy-start(bf16[768,512]{1,0:T(8,128)(2,1)} %cotangent.5) | copy-start | bytes 2359300
  47.2 3.9 %collective-permute-start.5 = (bf16[2,512,512]{2,1,0:T(8,128)(2,1)S(1)}, bf16[2,512,512]{2,1,0:T(8,128)(2,1)S(1)}, u32[]{:S(2)}, u32[]{:S(2)}) collective-permute-start(bf16[2,512,512]{2,1,0:T(8,128)(2,1)S(1)} %collective-permute-done.4.near), channel_id=1, source_target_pairs={{0,2},{1,3},{2,0},{3,1},{4,6},{5,7},{6,4},{7,5},{8,10},{9,11},{10,... | collective-permute-start | bytes 3145736 | tf_op jit(solution)/shard_map/ppermute | solution.py:781
  47.4 9.7 %collective-permute-start.6 = (bf16[2,2,2,128,512]{4,3,2,1,0:T(8,128)(2,1)S(1)}, bf16[2,2,2,128,512]{4,3,2,1,0:T(8,128)(2,1)S(1)}, u32[]{:S(2)}, u32[]{:S(2)}) collective-permute-start(bf16[2,2,2,128,512]{4,3,2,1,0:T(8,128)(2,1)S(1)} %get-tuple-element.94), channel_id=1, source_target_pairs={{0,2},{1,3},{2,0},{3,1},{4,6},{5,7},{6,4},{7,5},{8,10},{9,11},{10,... | collective-permute-start | bytes 3145736 | tf_op jit(solution)/shard_map/ppermute | solution.py:781
  56.8 2.7 %collective-permute-start.7 = (bf16[2,2,2,128,512]{4,3,2,1,0:T(8,128)(2,1)S(1)}, bf16[2,2,2,128,512]{4,3,2,1,0:T(8,128)(2,1)S(1)}, u32[]{:S(2)}, u32[]{:S(2)}) collective-permute-start(bf16[2,2,2,128,512]{4,3,2,1,0:T(8,128)(2,1)S(1)} %get-tuple-element.96), channel_id=1, source_target_pairs={{0,2},{1,3},{2,0},{3,1},{4,6},{5,7},{6,4},{7,5},{8,10},{9,11},{10,... | collective-permute-start | bytes 3145736 | tf_op jit(solution)/shard_map/ppermute | solution.py:781
  60.5 17.5 %collective-permute-start.8 = (bf16[2,2,2,128,512]{4,3,2,1,0:T(8,128)(2,1)S(1)}, bf16[2,2,2,128,512]{4,3,2,1,0:T(8,128)(2,1)S(1)}, u32[]{:S(2)}, u32[]{:S(2)}) collective-permute-start(bf16[2,2,2,128,512]{4,3,2,1,0:T(8,128)(2,1)S(1)} %get-tuple-element.98.token), channel_id=1, source_target_pairs={{0,4},{1,5},{2,10},{3,11},{4,0},{5,1},{6,14},{7,15},{8,12},{9,13},... | collective-permute-start | bytes 3145736 | tf_op jit(solution)/shard_map/ppermute | solution.py:781
  63.1 17.6 %collective-permute-start.9 = (bf16[192,640]{1,0:T(8,128)(2,1)S(1)}, bf16[192,640]{1,0:T(8,128)(2,1)S(1)}, u32[]{:S(2)}, u32[]{:S(2)}) collective-permute-start(bf16[192,640]{1,0:T(8,128)(2,1)S(1)} %get-tuple-element.108), channel_id=1, source_target_pairs={{0,1},{1,2},{2,3},{3,4},{4,5},{5,6},{6,7},{7,8},{8,9},{9,10},{10,1... | collective-permute-start | bytes 737288 | tf_op jit(solution)/shard_map/ppermute | solution.py:773
  66.9 13.7 %collective-permute-start.10 = (bf16[192,640]{1,0:T(8,128)(2,1)S(1)}, bf16[192,640]{1,0:T(8,128)(2,1)S(1)}, u32[]{:S(2)}, u32[]{:S(2)}) collective-permute-start(bf16[192,640]{1,0:T(8,128)(2,1)S(1)} %get-tuple-element.109), channel_id=1, source_target_pairs={{1,0},{2,1},{3,2},{4,3},{5,4},{6,5},{7,6},{8,7},{9,8},{10,9},{11,1... | collective-permute-start | bytes 737288 | tf_op jit(solution)/shard_map/ppermute | solution.py:773
  78.2 10.7 %collective-permute-start.12 = (bf16[2,256,512]{2,1,0:T(8,128)(2,1)S(1)}, bf16[2,256,512]{2,1,0:T(8,128)(2,1)S(1)}, u32[]{:S(2)}, u32[]{:S(2)}) collective-permute-start(bf16[2,256,512]{2,1,0:T(8,128)(2,1)S(1)} %bitcast.47), channel_id=1, source_target_pairs={{0,1},{1,0},{2,6},{3,7},{4,5},{5,4},{6,2},{7,3},{8,9},{9,8},{10,14... | collective-permute-start | bytes 1572872 | tf_op jit(solution)/shard_map/ppermute | solution.py:781
  88.9 3.0 %collective-permute-start.11 = (bf16[2,2,2,2,80,512]{5,4,3,2,1,0:T(8,128)(2,1)S(1)}, bf16[2,2,2,2,80,512]{5,4,3,2,1,0:T(8,128)(2,1)S(1)}, u32[]{:S(2)}, u32[]{:S(2)}) collective-permute-start(bf16[2,2,2,2,80,512]{5,4,3,2,1,0:T(8,128)(2,1)S(1)} %get-tuple-element.115.refs_2_), channel_id=1, source_target_pairs={{0,2},{1,3},{2,0},{3,1},{4,6},{5,7},{6,4},{7,5},{8,10},{9,11},{10,... | collective-permute-start | bytes 3932168 | tf_op jit(solution)/shard_map/ppermute | solution.py:781
  89.1 6.9 %collective-permute-start.14 = (bf16[2,128,512]{2,1,0:T(8,128)(2,1)S(1)}, bf16[2,128,512]{2,1,0:T(8,128)(2,1)S(1)}, u32[]{:S(2)}, u32[]{:S(2)}) collective-permute-start(bf16[2,128,512]{2,1,0:T(8,128)(2,1)S(1)} %bitcast.57), channel_id=1, source_target_pairs={{0,8},{1,9},{2,3},{3,2},{4,12},{5,13},{6,7},{7,6},{8,0},{9,1},{10,... | collective-permute-start | bytes 786440 | tf_op jit(solution)/shard_map/ppermute | solution.py:781
  92.3 10.7 %collective-permute-start.13 = (bf16[2,320,512]{2,1,0:T(8,128)(2,1)S(1)}, bf16[2,320,512]{2,1,0:T(8,128)(2,1)S(1)}, u32[]{:S(2)}, u32[]{:S(2)}) collective-permute-start(bf16[2,320,512]{2,1,0:T(8,128)(2,1)S(1)} %bitcast.45), channel_id=1, source_target_pairs={{0,4},{1,5},{2,10},{3,11},{4,0},{5,1},{6,14},{7,15},{8,12},{9,13},... | collective-permute-start | bytes 1966088 | tf_op jit(solution)/shard_map/ppermute | solution.py:781
  96.0 11.2 %collective-permute-start.16 = (bf16[2,128,512]{2,1,0:T(8,128)(2,1)S(1)}, bf16[2,128,512]{2,1,0:T(8,128)(2,1)S(1)}, u32[]{:S(2)}, u32[]{:S(2)}) collective-permute-start(bf16[2,128,512]{2,1,0:T(8,128)(2,1)S(1)} %total.2.refs_2_.refs_0_), channel_id=1, source_target_pairs={{0,16},{1,17},{2,18},{3,19},{4,20},{5,21},{6,22},{7,23},{8,24},{9,... | collective-permute-start | bytes 786440 | tf_op jit(solution)/shard_map/ppermute | solution.py:781
  103.0 7.5 %collective-permute-start.15 = (bf16[2,160,512]{2,1,0:T(8,128)(2,1)S(1)}, bf16[2,160,512]{2,1,0:T(8,128)(2,1)S(1)}, u32[]{:S(2)}, u32[]{:S(2)}) collective-permute-start(bf16[2,160,512]{2,1,0:T(8,128)(2,1)S(1)} %bitcast.52), channel_id=1, source_target_pairs={{0,1},{1,0},{2,3},{3,2},{4,5},{5,4},{6,7},{7,6},{8,9},{9,8},{10,11... | collective-permute-start | bytes 983048 | tf_op jit(solution)/shard_map/ppermute | solution.py:781
  107.3 7.5 %collective-permute-start.18 = (bf16[256,512]{1,0:T(8,128)(2,1)S(1)}, bf16[256,512]{1,0:T(8,128)(2,1)S(1)}, u32[]{:S(2)}, u32[]{:S(2)}) collective-permute-start(bf16[256,512]{1,0:T(8,128)(2,1)S(1)} %bitcast.54), channel_id=1, source_target_pairs={{0,8},{1,9},{2,3},{3,2},{4,12},{5,13},{6,7},{7,6},{8,0},{9,1},{10,... | collective-permute-start | bytes 786440 | tf_op jit(solution)/shard_map/ppermute | solution.py:781
  110.6 6.0 %collective-permute-start.17 = (bf16[2,80,512]{2,1,0:T(8,128)(2,1)S(1)}, bf16[2,80,512]{2,1,0:T(8,128)(2,1)S(1)}, u32[]{:S(2)}, u32[]{:S(2)}) collective-permute-start(bf16[2,80,512]{2,1,0:T(8,128)(2,1)S(1)} %bitcast.59), channel_id=1, source_target_pairs={{0,8},{1,9},{2,6},{3,7},{4,12},{5,13},{6,2},{7,3},{8,0},{9,1},{10,... | collective-permute-start | bytes 491528 | tf_op jit(solution)/shard_map/ppermute | solution.py:781
  114.9 9.2 %collective-permute-start.20 = (bf16[512,512]{1,0:T(8,128)(2,1)S(1)}, bf16[512,512]{1,0:T(8,128)(2,1)S(1)}, u32[]{:S(2)}, u32[]{:S(2)}) collective-permute-start(bf16[512,512]{1,0:T(8,128)(2,1)S(1)} %bitcast.49), channel_id=1, source_target_pairs={{0,1},{1,0},{2,6},{3,7},{4,5},{5,4},{6,2},{7,3},{8,9},{9,8},{10,14... | collective-permute-start | bytes 1572872 | tf_op jit(solution)/shard_map/ppermute | solution.py:781
  116.6 12.2 %collective-permute-start.19 = (bf16[2,80,512]{2,1,0:T(8,128)(2,1)S(1)}, bf16[2,80,512]{2,1,0:T(8,128)(2,1)S(1)}, u32[]{:S(2)}, u32[]{:S(2)}) collective-permute-start(bf16[2,80,512]{2,1,0:T(8,128)(2,1)S(1)} %total.3.refs_2_.refs_0_), channel_id=1, source_target_pairs={{0,16},{1,17},{2,18},{3,19},{4,20},{5,21},{6,22},{7,23},{8,24},{9,... | collective-permute-start | bytes 491528 | tf_op jit(solution)/shard_map/ppermute | solution.py:781
  124.2 16.6 %collective-permute-start.23 = (bf16[1024,512]{1,0:T(8,128)(2,1)S(1)}, bf16[1024,512]{1,0:T(8,128)(2,1)S(1)}, u32[]{:S(2)}, u32[]{:S(2)}) collective-permute-start(bf16[1024,512]{1,0:T(8,128)(2,1)S(1)} %bitcast.32), channel_id=1, source_target_pairs={{0,4},{1,5},{2,10},{3,11},{4,0},{5,1},{6,14},{7,15},{8,12},{9,13},... | collective-permute-start | bytes 3145736 | tf_op jit(solution)/shard_map/ppermute | solution.py:781
  128.9 7.1 %collective-permute-start.21 = (bf16[160,512]{1,0:T(8,128)(2,1)S(1)}, bf16[160,512]{1,0:T(8,128)(2,1)S(1)}, u32[]{:S(2)}, u32[]{:S(2)}) collective-permute-start(bf16[160,512]{1,0:T(8,128)(2,1)S(1)} %bitcast.39), channel_id=1, source_target_pairs={{0,8},{1,9},{2,6},{3,7},{4,12},{5,13},{6,2},{7,3},{8,0},{9,1},{10,... | collective-permute-start | bytes 491528 | tf_op jit(solution)/shard_map/ppermute | solution.py:781
  136.1 13.0 %collective-permute-start.22 = (bf16[320,512]{1,0:T(8,128)(2,1)S(1)}, bf16[320,512]{1,0:T(8,128)(2,1)S(1)}, u32[]{:S(2)}, u32[]{:S(2)}) collective-permute-start(bf16[320,512]{1,0:T(8,128)(2,1)S(1)} %bitcast.29), channel_id=1, source_target_pairs={{0,1},{1,0},{2,3},{3,2},{4,5},{5,4},{6,7},{7,6},{8,9},{9,8},{10,11... | collective-permute-start | bytes 983048 | tf_op jit(solution)/shard_map/ppermute | solution.py:781
  147.3 9.2 %collective-permute-start.25 = (bf16[2,512,512]{2,1,0:T(8,128)(2,1)S(1)}, bf16[2,512,512]{2,1,0:T(8,128)(2,1)S(1)}, u32[]{:S(2)}, u32[]{:S(2)}) collective-permute-start(bf16[2,512,512]{2,1,0:T(8,128)(2,1)S(1)} %get-tuple-element.127.own), channel_id=1, source_target_pairs={{0,2},{1,3},{2,0},{3,1},{4,6},{5,7},{6,4},{7,5},{8,10},{9,11},{10,... | collective-permute-start | bytes 3145736 | tf_op jit(solution)/shard_map/ppermute | solution.py:781
  149.0 7.5 %copy-start.5 = (f32[1024,512]{1,0:T(8,128)S(1)}, f32[1024,512]{1,0:T(8,128)}, u32[]{:S(2)}) copy-start(f32[1024,512]{1,0:T(8,128)} %down_moment.1) | copy-start | bytes 6291460
  149.1 7.5 %copy-start.3 = (f32[512,1024]{1,0:T(8,128)S(1)}, f32[512,1024]{1,0:T(8,128)}, u32[]{:S(2)}) copy-start(f32[512,1024]{1,0:T(8,128)} %up_moment.1) | copy-start | bytes 6291460
  149.1 10.8 %collective-permute-start.24 = (bf16[640,512]{1,0:T(8,128)(2,1)S(1)}, bf16[640,512]{1,0:T(8,128)(2,1)S(1)}, u32[]{:S(2)}, u32[]{:S(2)}) collective-permute-start(bf16[640,512]{1,0:T(8,128)(2,1)S(1)} %bitcast.36), channel_id=1, source_target_pairs={{0,4},{1,5},{2,10},{3,11},{4,0},{5,1},{6,14},{7,15},{8,12},{9,13},... | collective-permute-start | bytes 1966088 | tf_op jit(solution)/shard_map/ppermute | solution.py:781
  156.5 4.6 %collective-permute-start.27 = (bf16[2,512,512]{2,1,0:T(8,128)(2,1)S(1)}, bf16[2,512,512]{2,1,0:T(8,128)(2,1)S(1)}, u32[]{:S(2)}, u32[]{:S(2)}) collective-permute-start(bf16[2,512,512]{2,1,0:T(8,128)(2,1)S(1)} %ortho_large.3.token.own), channel_id=1, source_target_pairs={{0,2},{1,3},{2,0},{3,1},{4,6},{5,7},{6,4},{7,5},{8,10},{9,11},{10,... | collective-permute-start | bytes 3145736 | tf_op jit(solution)/shard_map/ppermute | solution.py:781
  159.9 1.6 copy-start.10
  159.9 2.2 %copy-start.13 = (f32[1024,512]{1,0:T(8,128)S(1)}, f32[1024,512]{1,0:T(8,128)}, u32[]{:S(2)}) copy-start(f32[1024,512]{1,0:T(8,128)} %down_weight.1) | copy-start | bytes 6291460
  160.6 13.3 %collective-permute-start.26 = (bf16[2,272,512]{2,1,0:T(8,128)(2,1)S(1)}, bf16[2,272,512]{2,1,0:T(8,128)(2,1)S(1)}, u32[]{:S(2)}, u32[]{:S(2)}) collective-permute-start(bf16[2,272,512]{2,1,0:T(8,128)(2,1)S(1)} %get-tuple-element.129.mix.table), channel_id=1, source_target_pairs={{0,2},{1,3},{2,0},{3,1},{4,6},{5,7},{6,4},{7,5},{8,10},{9,11},{10,... | collective-permute-start | bytes 1671176 | tf_op jit(solution)/shard_map/ppermute | solution.py:781
  162.1 11.7 %copy-start.16 = (f32[2,2,512]{2,1,0:T(2,128)S(1)}, f32[2,2,512]{2,1,0:T(2,128)}, u32[]{:S(2)}) copy-start(f32[2,2,512]{2,1,0:T(2,128)} %held_moment.1) | copy-start | bytes 24580
  173.4 3.1 %collective-permute-start.28 = (bf16[2,256,512]{2,1,0:T(8,128)(2,1)S(1)}, bf16[2,256,512]{2,1,0:T(8,128)(2,1)S(1)}, u32[]{:S(2)}, u32[]{:S(2)}) collective-permute-start(bf16[2,256,512]{2,1,0:T(8,128)(2,1)S(1)} %get-tuple-element.131.token.own), channel_id=1, source_target_pairs={{0,2},{1,3},{2,0},{3,1},{4,6},{5,7},{6,4},{7,5},{8,10},{9,11},{10,... | collective-permute-start | bytes 1572872 | tf_op jit(solution)/shard_map/ppermute | solution.py:781
  173.8 2.6 %copy-start.1 = (f32[4,512,512]{2,1,0:T(8,128)S(1)}, f32[4,512,512]{2,1,0:T(8,128)}, u32[]{:S(2)}) copy-start(f32[4,512,512]{2,1,0:T(8,128)} %weight.1) | copy-start | bytes 12582916

commit v4 on v2

--- a/solution.py
+++ b/solution.py
@@ -525,6 +525,10 @@
     send[...] = (kept[1].astype(f32) + got[1].astype(f32)).astype(bf16)
 
 
+def relay_kernel(*refs):
+    refs[-1][...] = jnp.zeros_like(refs[-1])
+
+
 def total_kernel(*refs):
     kept, got, total = refs[0], refs[1], refs[-1]
     total[...] = (kept[...] + got[...].astype(f32)).astype(bf16)
@@ -1090,11 +1094,14 @@
         out_shape=(struct((row_count, D), bf16),) + (struct((padded_rows, D), f32),) * 2,
         in_specs=[VMEM] * 5 + [pl.BlockSpec(memory_space=pl.ANY)],
         out_specs=(VMEM,) * 3,
-        cost_estimate=cost(8e9, 9e6),
+        cost_estimate=cost(1e3, 1e3),
         name="attend_back",
         compiler_params=room(10),
     )(qkv, padded, grad_attended, stats, counts, large_send)
-    large_keep, large_send = receive(large_keep, large_got, grad_queries)
+    edges_here = ordered(
+        relay_kernel, (), (grad_low, grad_high, grad_queries), struct((8, 128), f32), "relay"
+    )
+    large_keep, large_send = receive(large_keep, large_got, edges_here)
     large_got = swap(large_send, *large_routes[1])
     piece_shape = struct((2, 2, 2, 2, 80, D), bf16)
     features_grad, small_kept, small_sent = pl.pallas_call(

time: 174 us -> 178 us (1.023)
  starting transfers between devices: 39 us -> 42.8 us
    ppermute x23, starting transfers between devices: 25.9 us -> 30 us  [swap(): return lax.ppermute(value, AXES, pairs)]
  transfers between devices with their start and end apart: 27 -> 27, of which waited for: 13 -> 13; matrix products, arithmetic and copies ran while one was open for 0% -> 0% of each run, Pallas kernels for 47% -> 46%
where the time goes in v4:
time: 178 us; the launch traced here: 177 us
  Pallas kernels  84.4 us (47%)
  starting transfers between devices  42.8 us (24%)
  waiting for transfers between devices  42.1 us (24%)
  local copies, waits for them, and re-layouts  4.33 us (2%)
  other arithmetic  2.63 us (1%)
    ppermute x23, waiting for transfers between devices, swap(): return lax.ppermute(value, AXES, pairs)  42.1 us
    ppermute x23, starting transfers between devices, swap(): return lax.ppermute(value, AXES, pairs)  30 us
    ppermute x4, starting transfers between devices, along(): return lax.ppermute(value, AXES, pairs)  12.8 us
    pallas_call x1, Pallas kernels, on_device(): pl.pallas_call(small_kernel, grid=(NS_STEPS,), out_shape=(struct((2, 256,...  11.3 us
    pallas_call x1, Pallas kernels, on_device(): pl.pallas_call(forward_kernel, out_shape=(struct((row_count, D), bf16), s...  9.92 us
    pallas_call x1, Pallas kernels, on_device(): pl.pallas_call(weights_kernel, out_shape=(struct((row_count, D), f32), pi...  8.26 us
    pallas_call x1, Pallas kernels, on_device(): pl.pallas_call(backward_kernel, out_shape=(struct((row_count, D), bf16),)...  7.95 us
    pallas_call x1, Pallas kernels, on_device(): pl.pallas_call(mlp_own_kernel, out_shape=(struct((row_count, D), f32), st...  6.82 us
  transfers between devices with their start and end apart: 27, of which 13 were waited for; matrix products, arithmetic and copies ran while one was open for 0% of the time, Pallas kernels for 46%

profile of v4, /device:TPU:0, one launch (start us, length us, event | category | flops | bytes accessed | tf_op | source)
XLA Modules:
  0.0 177.3 jit_solution(8811675440267924625)
XLA Ops:
  0.7 0.9 broadcast_subtract_fusion
  1.6 0.2 copy.30
  1.8 1.0 broadcast_in_dim.16
  2.8 0.9 fusion
  3.6 0.2 fusion.1
  3.9 0.7 pad_maximum_fusion
  4.6 1.3 collective-permute-start.1
  5.9 6.2 %collective-permute-start = (bf16[192,640]{1,0:T(8,128)(2,1)S(1)}, bf16[192,640]{1,0:T(8,128)(2,1)}, u32[]{:S(2)}, u32[]{:S(2)}) collective-permute-start(bf16[192,640]{1,0:T(8,128)(2,1)S(1)} %get-tuple-element.143.token), channel_id=1, source_target_pairs={{0,1},{1,2},{2,3},{3,4},{4,5},{5,6},{6,7},{7,8},{8,9},{9,10},{10,1... | collective-permute-start | bytes 737288 | tf_op jit(solution)/shard_map/ppermute | solution.py:775
  12.2 1.6 copy-done.10
  13.8 0.6 quarter.1
  14.5 1.1 collective-permute-start.2
  15.6 0.4 copy-done
  16.0 5.9 %project.1 = (bf16[768,512]{1,0:T(8,128)(2,1)S(1)}, bf16[3,768,512]{2,1,0:T(8,128)(2,1)S(1)}, bf16[768,512]{1,0:T(8,128)(2,1)S(1)}, bf16[4,512,512]{2,1,0:T(8,128)(2,1)S(1)}) custom-call(bf16[768,512]{1,0:T(8,128)(2,1)S(1)} %copy-done.6, f32[768,128]{1,0:T(8,128)S(1)} %get-tuple-element.76.pack, f32[2,4,512]{2,1,0:T(4,128)S(1)} %copy-done.13, ...), custom_call_target="tpu_custom_call" | custom-call | flops 1000 | bytes 1000 | tf_op jit(solution)/shard_map/project/pallas_call | solution.py:836
  21.9 0.8 past.1
  22.7 9.9 %attend.1 = (bf16[768,512]{1,0:T(8,128)(2,1)S(1)}, f32[768,512]{1,0:T(8,128)S(1)}, bf16[768,512]{1,0:T(8,128)(2,1)S(1)}, bf16[2,1152,512]{2,1,0:T(8,128)(2,1)S(1...) custom-call(bf16[192,640]{1,0:T(8,128)(2,1)} %collective-permute-done.rim_low, ...), custom_call_target="tpu_custom_call" | custom-call | flops 1000 | bytes 1000 | tf_op jit(solution)/shard_map/attend/pallas_call | solution.py:864
  32.7 6.8 %mlp_own.1 = (f32[768,512]{1,0:T(8,128)S(1)}, f32[768,512]{1,0:T(8,128)S(1)}, bf16[2,2,2,128,512]{4,3,2,1,0:T(8,128)(2,1)S(1)}, bf16[2,2,2,128,512]{4,3,2,1,0:T(8,128)(2,1)S(1)}) custom-call(s32[5]{0:T(128)S(1)} %stack.23.scalars, bf16[768,512]{1,0:T(8,128)(2,1)S(1)} %get-tuple-element.80.second_in, bf16[768,512]{1,0:T(8,128)(2,1)S(1)} %copy-done.14, ...), custom_call_target="tpu_custom_call" | custom-call | flops 10000000000 | bytes 1000 | tf_op jit(solution)/shard_map/mlp_own/pallas_call | solution.py:887
  39.5 3.9 %collective-permute-done.2.near = bf16[2,512,512]{2,1,0:T(8,128)(2,1)S(1)} collective-permute-done((bf16[2,512,512]{2,1,0:T(8,128)(2,1)S(1)}, bf16[2,512,512]{2,1,0:T(8,128)(2,1)S(1)}, u32[]{:S(2)}, u32[]{:S(2)}) %collective-permute-start.2) | collective-permute-done | bytes 1048608 | tf_op jit(solution)/shard_map/ppermute | solution.py:783
  43.4 0.5 collective-permute-start.4
  43.9 3.4 %mlp_near.1 = (f32[768,512]{1,0:T(8,128)S(1)}, f32[768,512]{1,0:T(8,128)S(1)}, bf16[2,2,2,128,512]{4,3,2,1,0:T(8,128)(2,1)S(1)}, bf16[2,2,2,128,512]{4,3,2,1,0:T(8,128)(2,1)S(1)}) custom-call(s32[5]{0:T(128)S(1)} %stack.23.scalars, bf16[768,512]{1,0:T(8,128)(2,1)S(1)} %get-tuple-element.80.second_in, bf16[768,512]{1,0:T(8,128)(2,1)S(1)} %copy-done.14, ...), custom_call_target="tpu_custom_call" | custom-call | flops 2500000000 | bytes 4000000 | tf_op jit(solution)/shard_map/mlp_near/pallas_call | solution.py:918
  47.2 5.7 %mlp_far.1 = (bf16[2,2,2,128,512]{4,3,2,1,0:T(8,128)(2,1)S(1)}, bf16[2,2,2,128,512]{4,3,2,1,0:T(8,128)(2,1)S(1)}, bf16[768,512]{1,0:T(8,128)(2,1)}, f32[768,512]...) custom-call(s32[5]{0:T(128)S(1)} %stack.23.scalars, ...), custom_call_target="tpu_custom_call", output_to_operand_aliasing={{0}: (12, {}), {1}: (13, {})} | custom-call | flops 4000000000 | bytes 8000000 | tf_op jit(solution)/shard_map/mlp_far/pallas_call | solution.py:949
  53.0 4.0 %collective-permute-start.7 = (bf16[192,640]{1,0:T(8,128)(2,1)S(1)}, bf16[192,640]{1,0:T(8,128)(2,1)S(1)}, u32[]{:S(2)}, u32[]{:S(2)}) collective-permute-start(bf16[192,640]{1,0:T(8,128)(2,1)S(1)} %get-tuple-element.99), channel_id=1, source_target_pairs={{0,1},{1,2},{2,3},{3,4},{4,5},{5,6},{6,7},{7,8},{8,9},{9,10},{10,1... | collective-permute-start | bytes 737288 | tf_op jit(solution)/shard_map/ppermute | solution.py:775
  57.0 1.3 collective-permute-start.8
  58.3 1.0 large_sum.1
  59.3 2.6 %collective-permute-start.6 = (bf16[2,2,2,128,512]{4,3,2,1,0:T(8,128)(2,1)S(1)}, bf16[2,2,2,128,512]{4,3,2,1,0:T(8,128)(2,1)S(1)}, u32[]{:S(2)}, u32[]{:S(2)}) collective-permute-start(bf16[2,2,2,128,512]{4,3,2,1,0:T(8,128)(2,1)S(1)} %get-tuple-element.98.token), channel_id=1, source_target_pairs={{0,4},{1,5},{2,10},{3,11},{4,0},{5,1},{6,14},{7,15},{8,12},{9,13},... | collective-permute-start | bytes 3145736 | tf_op jit(solution)/shard_map/ppermute | solution.py:783
  62.0 7.9 %attend_back.1 = (bf16[768,512]{1,0:T(8,128)(2,1)S(1)}, f32[1152,512]{1,0:T(8,128)S(1)}, f32[1152,512]{1,0:T(8,128)S(1)}) custom-call(bf16[3,768,512]{2,1,0:T(8,128)(2,1)S(1)} %get-tuple-element.78.qkv, bf16[2,1152,512]{2,1,0:T(8,128)(2,1)S(1)} %get-tuple-element.101.padded, bf16[768,512]{1,0:T(8,128)(2,1)S(1)} %get-tuple-element.102.grad, ...), custom_call_target="tpu_custom_call" | custom-call | flops 1000 | bytes 1000 | tf_op jit(solution)/shard_map/attend_back/pallas_call | solution.py:1092
  70.0 4.8 %collective-permute-done.6 = bf16[2,2,2,128,512]{4,3,2,1,0:T(8,128)(2,1)S(1)} collective-permute-done((bf16[2,2,2,128,512]{4,3,2,1,0:T(8,128)(2,1)S(1)}, bf16[2,2,2,128,512]{4,3,2,1,0:T(8,128)(2,1)S(1)}, u32[]{:S(2)}, u32[]{:S(2)}) %collective-permute-start.6) | collective-permute-done | bytes 1048608 | tf_op jit(solution)/shard_map/ppermute | solution.py:783
  74.8 0.2 receive.5
  75.0 5.6 %collective-permute-start.10 = (bf16[2,256,512]{2,1,0:T(8,128)(2,1)S(1)}, bf16[2,256,512]{2,1,0:T(8,128)(2,1)S(1)}, u32[]{:S(2)}, u32[]{:S(2)}) collective-permute-start(bf16[2,256,512]{2,1,0:T(8,128)(2,1)S(1)} %bitcast.47), channel_id=1, source_target_pairs={{0,1},{1,0},{2,6},{3,7},{4,5},{5,4},{6,2},{7,3},{8,9},{9,8},{10,14... | collective-permute-start | bytes 1572872 | tf_op jit(solution)/shard_map/ppermute | solution.py:783
  80.6 8.3 %attend_weights.1 = (f32[768,512]{1,0:T(8,128)}, bf16[2,2,2,2,80,512]{5,4,3,2,1,0:T(8,128)(2,1)S(1)}, bf16[2,2,2,2,80,512]{5,4,3,2,1,0:T(8,128)(2,1)S(1)}) custom-call(s32[5]{0:T(128)S(1)} %stack.23.scalars, bf16[2,256,512]{2,1,0:T(8,128)(2,1)S(1)} %bitcast.48, bf16[768,512]{1,0:T(8,128)(2,1)S(1)} %get-tuple-element.104.refs_2_.queries_in, ...), custom_call_target="tpu_custom_call" | custom-call | flops 6000000000 | bytes 9000000 | tf_op jit(solution)/shard_map/attend_weights/pallas_call | solution.py:1107
  88.9 1.6 collective-permute-start.12
  90.5 1.3 collective-permute-done.9
  91.9 0.3 receive.7
  92.1 1.1 collective-permute-start.11
  93.2 2.6 %collective-permute-done.12.refs_1_ = bf16[2,128,512]{2,1,0:T(8,128)(2,1)S(1)} collective-permute-done((bf16[2,128,512]{2,1,0:T(8,128)(2,1)S(1)}, bf16[2,128,512]{2,1,0:T(8,128)(2,1)S(1)}, u32[]{:S(2)}, u32[]{:S(2)}) %collective-permute-start.12) | collective-permute-done | bytes 262176 | tf_op jit(solution)/shard_map/ppermute | solution.py:783
  95.9 2.6 %collective-permute-start.14 = (bf16[2,128,512]{2,1,0:T(8,128)(2,1)S(1)}, bf16[2,128,512]{2,1,0:T(8,128)(2,1)S(1)}, u32[]{:S(2)}, u32[]{:S(2)}) collective-permute-start(bf16[2,128,512]{2,1,0:T(8,128)(2,1)S(1)} %total.2.refs_2_.refs_0_), channel_id=1, source_target_pairs={{0,16},{1,17},{2,18},{3,19},{4,20},{5,21},{6,22},{7,23},{8,24},{9,... | collective-permute-start | bytes 786440 | tf_op jit(solution)/shard_map/ppermute | solution.py:783
  98.5 4.3 %collective-permute-done.11.refs_1_ = bf16[2,320,512]{2,1,0:T(8,128)(2,1)S(1)} collective-permute-done((bf16[2,320,512]{2,1,0:T(8,128)(2,1)S(1)}, bf16[2,320,512]{2,1,0:T(8,128)(2,1)S(1)}, u32[]{:S(2)}, u32[]{:S(2)}) %collective-permute-start.11) | collective-permute-done | bytes 655392 | tf_op jit(solution)/shard_map/ppermute | solution.py:783
  103.0 4.1 %collective-permute-done.14.refs_1_ = bf16[2,128,512]{2,1,0:T(8,128)(2,1)S(1)} collective-permute-done((bf16[2,128,512]{2,1,0:T(8,128)(2,1)S(1)}, bf16[2,128,512]{2,1,0:T(8,128)(2,1)S(1)}, u32[]{:S(2)}, u32[]{:S(2)}) %collective-permute-start.14) | collective-permute-done | bytes 262176 | tf_op jit(solution)/shard_map/ppermute | solution.py:783
  107.1 0.1 blend.2
  107.2 3.0 %collective-permute-start.16 = (bf16[256,512]{1,0:T(8,128)(2,1)S(1)}, bf16[256,512]{1,0:T(8,128)(2,1)S(1)}, u32[]{:S(2)}, u32[]{:S(2)}) collective-permute-start(bf16[256,512]{1,0:T(8,128)(2,1)S(1)} %bitcast.54), channel_id=1, source_target_pairs={{0,8},{1,9},{2,3},{3,2},{4,12},{5,13},{6,7},{7,6},{8,0},{9,1},{10,... | collective-permute-start | bytes 786440 | tf_op jit(solution)/shard_map/ppermute | solution.py:783
  110.4 2.5 %collective-permute-start.15 = (bf16[2,80,512]{2,1,0:T(8,128)(2,1)S(1)}, bf16[2,80,512]{2,1,0:T(8,128)(2,1)S(1)}, u32[]{:S(2)}, u32[]{:S(2)}) collective-permute-start(bf16[2,80,512]{2,1,0:T(8,128)(2,1)S(1)} %bitcast.59), channel_id=1, source_target_pairs={{0,8},{1,9},{2,6},{3,7},{4,12},{5,13},{6,2},{7,3},{8,0},{9,1},{10,... | collective-permute-start | bytes 491528 | tf_op jit(solution)/shard_map/ppermute | solution.py:783
  112.9 1.7 collective-permute-done.16.refs_1_
  114.7 0.7 collective-permute-start.18
  115.4 1.0 collective-permute-done.15.refs_1_
  116.4 3.7 %collective-permute-start.17 = (bf16[2,80,512]{2,1,0:T(8,128)(2,1)S(1)}, bf16[2,80,512]{2,1,0:T(8,128)(2,1)S(1)}, u32[]{:S(2)}, u32[]{:S(2)}) collective-permute-start(bf16[2,80,512]{2,1,0:T(8,128)(2,1)S(1)} %total.3.refs_2_.refs_0_), channel_id=1, source_target_pairs={{0,16},{1,17},{2,18},{3,19},{4,20},{5,21},{6,22},{7,23},{8,24},{9,... | collective-permute-start | bytes 491528 | tf_op jit(solution)/shard_map/ppermute | solution.py:783
  120.1 3.8 %collective-permute-done.18.refs_1_ = bf16[512,512]{1,0:T(8,128)(2,1)S(1)} collective-permute-done((bf16[512,512]{1,0:T(8,128)(2,1)S(1)}, bf16[512,512]{1,0:T(8,128)(2,1)S(1)}, u32[]{:S(2)}, u32[]{:S(2)}) %collective-permute-start.18) | collective-permute-done | bytes 524320 | tf_op jit(solution)/shard_map/ppermute | solution.py:783
  124.0 0.1 collective-permute-start.21
  124.1 3.6 %collective-permute-done.17.refs_1_ = bf16[2,80,512]{2,1,0:T(8,128)(2,1)S(1)} collective-permute-done((bf16[2,80,512]{2,1,0:T(8,128)(2,1)S(1)}, bf16[2,80,512]{2,1,0:T(8,128)(2,1)S(1)}, u32[]{:S(2)}, u32[]{:S(2)}) %collective-permute-start.17) | collective-permute-done | bytes 163872 | tf_op jit(solution)/shard_map/ppermute | solution.py:783
  127.8 1.1 collective-permute-start.19
  128.9 6.0 %collective-permute-done.19.refs_1_ = bf16[160,512]{1,0:T(8,128)(2,1)S(1)} collective-permute-done((bf16[160,512]{1,0:T(8,128)(2,1)S(1)}, bf16[160,512]{1,0:T(8,128)(2,1)S(1)}, u32[]{:S(2)}, u32[]{:S(2)}) %collective-permute-start.19) | collective-permute-done | bytes 163872 | tf_op jit(solution)/shard_map/ppermute | solution.py:783
  134.9 0.9 collective-permute-start.20
  135.9 4.8 %collective-permute-done.21 = bf16[1024,512]{1,0:T(8,128)(2,1)S(1)} collective-permute-done((bf16[1024,512]{1,0:T(8,128)(2,1)S(1)}, bf16[1024,512]{1,0:T(8,128)(2,1)S(1)}, u32[]{:S(2)}, u32[]{:S(2)}) %collective-permute-start.21) | collective-permute-done | bytes 1048608 | tf_op jit(solution)/shard_map/ppermute | solution.py:783
  140.6 6.5 %ortho_large.2 = (bf16[4,512,512]{2,1,0:T(8,128)(2,1)S(1)}, bf16[2,512,512]{2,1,0:T(8,128)(2,1)S(1)}) custom-call(s32[5]{0:T(128)S(1)} %stack.23.scalars, bf16[2,2,2,128,512]{4,3,2,1,0:T(8,128)(2,1)S(1)} %bitcast.34, bf16[2,2,2,128,512]{4,3,2,1,0:T(8,128)(2,1)S(1)} %bitcast.35, bf16[320,512]{1,0:T(8,128)(2,1)S(1)} %bitcast.30), custom_call_target="tpu_custom_call" | custom-call | flops 1000 | bytes 1000 | tf_op jit(solution)/shard_map/ortho_large/pallas_call | solution.py:1175
  147.1 1.2 collective-permute-start.23
  148.4 0.8 collective-permute-start.22
  149.3 5.9 %ortho_large.3.token.own = bf16[2,512,512]{2,1,0:T(8,128)(2,1)S(1)} custom-call(bf16[4,512,512]{2,1,0:T(8,128)(2,1)S(1)} %get-tuple-element.126.refs_2_.given, bf16[640,512]{1,0:T(8,128)(2,1)S(1)} %bitcast.37), custom_call_target="tpu_custom_call" | custom-call | flops 1000 | bytes 1000 | tf_op jit(solution)/shard_map/ortho_large/pallas_call | solution.py:1188
  155.2 0.4 collective-permute-start.25
  155.6 3.3 %moment_large.1 = (f32[512,1024]{1,0:T(8,128)}, f32[1024,512]{1,0:T(8,128)}, f32[8,128]{1,0:T(8,128)S(1)}) custom-call(s32[5]{0:T(128)S(1)} %stack.23.scalars, bf16[2,512,512]{2,1,0:T(8,128)(2,1)S(1)} %get-tuple-element.127.own, bf16[2,512,512]{2,1,0:T(8,128)(2,1)S(1)} %collective-permute-done.23.got, f32[512,1024]{1,0:T(8,128)S(1)} %copy-done.3, ...), custom_call_target="tpu_custom_call" | custom-call | flops 1000 | bytes 1000 | tf_op jit(solution)/shard_map/moment_large/pallas_call | solution.py:1206
  158.9 0.2 collective-permute-done.22
  159.1 0.7 unpack_small.1
  159.9 0.8 copy-done.12
  160.7 11.3 %ortho_small.1 = (bf16[2,256,512]{2,1,0:T(8,128)(2,1)S(1)}, f32[512,1024]{1,0:T(8,128)}, f32[1024,512]{1,0:T(8,128)}) custom-call(s32[5]{0:T(128)S(1)} %stack.23.scalars, bf16[2,2,256,512]{3,2,1,0:T(8,128)(2,1)S(1)} %get-tuple-element.130.given, bf16[2,512,512]{2,1,0:T(8,128)(2,1)S(1)} %ortho_large.3.token.own, ...), custom_call_target="tpu_custom_call" | custom-call | flops 6000000000 | bytes 10000000 | tf_op jit(solution)/shard_map/ortho_small/pallas_call | solution.py:1243
  172.0 2.5 %moment_small.1 = (f32[4,256,512]{2,1,0:T(8,128)}, f32[2,2,512]{2,1,0:T(2,128)}, f32[2,2,512]{2,1,0:T(2,128)}, f32[8,128]{1,0:T(8,128)S(1)}) custom-call(s32[5]{0:T(128)S(1)} %stack.23.scalars, bf16[2,272,512]{2,1,0:T(8,128)(2,1)S(1)} %get-tuple-element.129.mix.table, bf16[2,272,512]{2,1,0:T(8,128)(2,1)S(1)} %collective-permute-done.24.mix_got.table_got, ...), custom_call_target="tpu_custom_call" | custom-call | flops 10000000000 | bytes 10000000 | tf_op jit(solution)/shard_map/moment_small/pallas_call | solution.py:1258
  174.5 0.1 copy-done.1
  174.7 2.6 %update_small.1 = f32[4,256,512]{2,1,0:T(8,128)} custom-call(s32[5]{0:T(128)S(1)} %stack.23.scalars, bf16[2,256,512]{2,1,0:T(8,128)(2,1)S(1)} %get-tuple-element.131.token.own, bf16[2,256,512]{2,1,0:T(8,128)(2,1)S(1)} %collective-permute-done.26.got, f32[4,512,512]{2,1,0:T(8,128)S(1)} %copy-done.1, f32[8,128]{1,0:T(8,128)S(1)} %get-tuple-element.133.token), custom_call_target="tpu_custom_call" | custom-call | flops 10000000 | bytes 6000000 | tf_op jit(solution)/shard_map/update_small/pallas_call | solution.py:1288
  (63 shorter events, 1.1 us)
Async XLA Ops:
  0.6 3.2 %copy-start.6 = (bf16[768,512]{1,0:T(8,128)(2,1)S(1)}, bf16[768,512]{1,0:T(8,128)(2,1)}, u32[]{:S(2)}) copy-start(bf16[768,512]{1,0:T(8,128)(2,1)} %features.5) | copy-start | bytes 2359300
  1.8 10.4 %copy-start.9 = (f32[512,1024]{1,0:T(8,128)S(1)}, f32[512,1024]{1,0:T(8,128)}, u32[]{:S(2)}) copy-start(f32[512,1024]{1,0:T(8,128)} %up_weight.1) | copy-start | bytes 6291460
  3.8 11.7 %copy-start.13 = (f32[2,4,512]{2,1,0:T(4,128)S(1)}, f32[2,4,512]{2,1,0:T(4,128)}, u32[]{:S(2)}) copy-start(f32[2,4,512]{2,1,0:T(4,128)} %modulation.1) | copy-start | bytes 49156
  4.6 18.1 %collective-permute-start.1 = (bf16[192,640]{1,0:T(8,128)(2,1)}, bf16[192,640]{1,0:T(8,128)(2,1)}, u32[]{:S(2)}, u32[]{:S(2)}) collective-permute-start(bf16[192,640]{1,0:T(8,128)(2,1)} %get-tuple-element.142), channel_id=1, source_target_pairs={{1,0},{2,1},{3,2},{4,3},{5,4},{6,5},{7,6},{8,7},{9,8},{10,9},{11,1... | collective-permute-start | bytes 737288 | tf_op jit(solution)/shard_map/ppermute | solution.py:775
  5.9 16.8 %collective-permute-start = (bf16[192,640]{1,0:T(8,128)(2,1)S(1)}, bf16[192,640]{1,0:T(8,128)(2,1)}, u32[]{:S(2)}, u32[]{:S(2)}) collective-permute-start(bf16[192,640]{1,0:T(8,128)(2,1)S(1)} %get-tuple-element.143.token), channel_id=1, source_target_pairs={{0,1},{1,2},{2,3},{3,4},{4,5},{5,6},{6,7},{7,8},{8,9},{9,10},{10,1... | collective-permute-start | bytes 737288 | tf_op jit(solution)/shard_map/ppermute | solution.py:775
  12.2 1.6 copy-start.10
  13.8 2.2 %copy-start = (f32[4,512,512]{2,1,0:T(8,128)S(1)}, f32[4,512,512]{2,1,0:T(8,128)}, u32[]{:S(2)}) copy-start(f32[4,512,512]{2,1,0:T(8,128)} %weight.1) | copy-start | bytes 12582916
  13.8 8.1 %copy-start.7 = (f32[4,256,512]{2,1,0:T(8,128)S(1)}, f32[4,256,512]{2,1,0:T(8,128)}, u32[]{:S(2)}) copy-start(f32[4,256,512]{2,1,0:T(8,128)} %moment.1) | copy-start | bytes 6291460
  14.4 7.4 %copy-start.2 = (f32[512,1024]{1,0:T(8,128)S(1)}, f32[512,1024]{1,0:T(8,128)}, u32[]{:S(2)}) copy-start(f32[512,1024]{1,0:T(8,128)} %up_moment.1) | copy-start | bytes 6291460
  14.5 7.4 %copy-start.4 = (f32[1024,512]{1,0:T(8,128)S(1)}, f32[1024,512]{1,0:T(8,128)}, u32[]{:S(2)}) copy-start(f32[1024,512]{1,0:T(8,128)} %down_moment.1) | copy-start | bytes 6291460
  14.5 28.9 %collective-permute-start.2 = (bf16[2,512,512]{2,1,0:T(8,128)(2,1)S(1)}, bf16[2,512,512]{2,1,0:T(8,128)(2,1)S(1)}, u32[]{:S(2)}, u32[]{:S(2)}) collective-permute-start(bf16[2,512,512]{2,1,0:T(8,128)(2,1)S(1)} %quarter.1), channel_id=1, source_target_pairs={{0,1},{1,0},{2,3},{3,2},{4,5},{5,4},{6,7},{7,6},{8,9},{9,8},{10,11... | collective-permute-start | bytes 3145736 | tf_op jit(solution)/shard_map/ppermute | solution.py:783
  22.7 10.0 %copy-start.11 = (f32[1024,512]{1,0:T(8,128)S(1)}, f32[1024,512]{1,0:T(8,128)}, u32[]{:S(2)}) copy-start(f32[1024,512]{1,0:T(8,128)} %down_weight.1) | copy-start | bytes 6291460
  22.7 10.0 %copy-start.14 = (bf16[768,512]{1,0:T(8,128)(2,1)S(1)}, bf16[768,512]{1,0:T(8,128)(2,1)}, u32[]{:S(2)}) copy-start(bf16[768,512]{1,0:T(8,128)(2,1)} %cotangent.5) | copy-start | bytes 2359300
  43.3 3.9 %collective-permute-start.3 = (bf16[2,512,512]{2,1,0:T(8,128)(2,1)S(1)}, bf16[2,512,512]{2,1,0:T(8,128)(2,1)S(1)}, u32[]{:S(2)}, u32[]{:S(2)}) collective-permute-start(bf16[2,512,512]{2,1,0:T(8,128)(2,1)S(1)} %collective-permute-done.2.near), channel_id=1, source_target_pairs={{0,2},{1,3},{2,0},{3,1},{4,6},{5,7},{6,4},{7,5},{8,10},{9,11},{10,... | collective-permute-start | bytes 3145736 | tf_op jit(solution)/shard_map/ppermute | solution.py:783
  43.4 15.0 %collective-permute-start.4 = (bf16[2,2,2,128,512]{4,3,2,1,0:T(8,128)(2,1)S(1)}, bf16[2,2,2,128,512]{4,3,2,1,0:T(8,128)(2,1)S(1)}, u32[]{:S(2)}, u32[]{:S(2)}) collective-permute-start(bf16[2,2,2,128,512]{4,3,2,1,0:T(8,128)(2,1)S(1)} %get-tuple-element.94), channel_id=1, source_target_pairs={{0,2},{1,3},{2,0},{3,1},{4,6},{5,7},{6,4},{7,5},{8,10},{9,11},{10,... | collective-permute-start | bytes 3145736 | tf_op jit(solution)/shard_map/ppermute | solution.py:783
  53.0 5.4 %collective-permute-start.5 = (bf16[2,2,2,128,512]{4,3,2,1,0:T(8,128)(2,1)S(1)}, bf16[2,2,2,128,512]{4,3,2,1,0:T(8,128)(2,1)S(1)}, u32[]{:S(2)}, u32[]{:S(2)}) collective-permute-start(bf16[2,2,2,128,512]{4,3,2,1,0:T(8,128)(2,1)S(1)} %get-tuple-element.96), channel_id=1, source_target_pairs={{0,2},{1,3},{2,0},{3,1},{4,6},{5,7},{6,4},{7,5},{8,10},{9,11},{10,... | collective-permute-start | bytes 3145736 | tf_op jit(solution)/shard_map/ppermute | solution.py:783
  53.0 16.9 %collective-permute-start.7 = (bf16[192,640]{1,0:T(8,128)(2,1)S(1)}, bf16[192,640]{1,0:T(8,128)(2,1)S(1)}, u32[]{:S(2)}, u32[]{:S(2)}) collective-permute-start(bf16[192,640]{1,0:T(8,128)(2,1)S(1)} %get-tuple-element.99), channel_id=1, source_target_pairs={{0,1},{1,2},{2,3},{3,4},{4,5},{5,6},{6,7},{7,8},{8,9},{9,10},{10,1... | collective-permute-start | bytes 737288 | tf_op jit(solution)/shard_map/ppermute | solution.py:775
  57.0 12.9 %collective-permute-start.8 = (bf16[192,640]{1,0:T(8,128)(2,1)S(1)}, bf16[192,640]{1,0:T(8,128)(2,1)S(1)}, u32[]{:S(2)}, u32[]{:S(2)}) collective-permute-start(bf16[192,640]{1,0:T(8,128)(2,1)S(1)} %get-tuple-element.100), channel_id=1, source_target_pairs={{1,0},{2,1},{3,2},{4,3},{5,4},{6,5},{7,6},{8,7},{9,8},{10,9},{11,1... | collective-permute-start | bytes 737288 | tf_op jit(solution)/shard_map/ppermute | solution.py:775
  59.3 15.4 %collective-permute-start.6 = (bf16[2,2,2,128,512]{4,3,2,1,0:T(8,128)(2,1)S(1)}, bf16[2,2,2,128,512]{4,3,2,1,0:T(8,128)(2,1)S(1)}, u32[]{:S(2)}, u32[]{:S(2)}) collective-permute-start(bf16[2,2,2,128,512]{4,3,2,1,0:T(8,128)(2,1)S(1)} %get-tuple-element.98.token), channel_id=1, source_target_pairs={{0,4},{1,5},{2,10},{3,11},{4,0},{5,1},{6,14},{7,15},{8,12},{9,13},... | collective-permute-start | bytes 3145736 | tf_op jit(solution)/shard_map/ppermute | solution.py:783
  75.0 13.8 %collective-permute-start.10 = (bf16[2,256,512]{2,1,0:T(8,128)(2,1)S(1)}, bf16[2,256,512]{2,1,0:T(8,128)(2,1)S(1)}, u32[]{:S(2)}, u32[]{:S(2)}) collective-permute-start(bf16[2,256,512]{2,1,0:T(8,128)(2,1)S(1)} %bitcast.47), channel_id=1, source_target_pairs={{0,1},{1,0},{2,6},{3,7},{4,5},{5,4},{6,2},{7,3},{8,9},{9,8},{10,14... | collective-permute-start | bytes 1572872 | tf_op jit(solution)/shard_map/ppermute | solution.py:783
  88.8 3.0 %collective-permute-start.9 = (bf16[2,2,2,2,80,512]{5,4,3,2,1,0:T(8,128)(2,1)S(1)}, bf16[2,2,2,2,80,512]{5,4,3,2,1,0:T(8,128)(2,1)S(1)}, u32[]{:S(2)}, u32[]{:S(2)}) collective-permute-start(bf16[2,2,2,2,80,512]{5,4,3,2,1,0:T(8,128)(2,1)S(1)} %get-tuple-element.115.refs_2_), channel_id=1, source_target_pairs={{0,2},{1,3},{2,0},{3,1},{4,6},{5,7},{6,4},{7,5},{8,10},{9,11},{10,... | collective-permute-start | bytes 3932168 | tf_op jit(solution)/shard_map/ppermute | solution.py:783
  88.9 6.9 %collective-permute-start.12 = (bf16[2,128,512]{2,1,0:T(8,128)(2,1)S(1)}, bf16[2,128,512]{2,1,0:T(8,128)(2,1)S(1)}, u32[]{:S(2)}, u32[]{:S(2)}) collective-permute-start(bf16[2,128,512]{2,1,0:T(8,128)(2,1)S(1)} %bitcast.57), channel_id=1, source_target_pairs={{0,8},{1,9},{2,3},{3,2},{4,12},{5,13},{6,7},{7,6},{8,0},{9,1},{10,... | collective-permute-start | bytes 786440 | tf_op jit(solution)/shard_map/ppermute | solution.py:783
  92.1 10.7 %collective-permute-start.11 = (bf16[2,320,512]{2,1,0:T(8,128)(2,1)S(1)}, bf16[2,320,512]{2,1,0:T(8,128)(2,1)S(1)}, u32[]{:S(2)}, u32[]{:S(2)}) collective-permute-start(bf16[2,320,512]{2,1,0:T(8,128)(2,1)S(1)} %bitcast.45), channel_id=1, source_target_pairs={{0,4},{1,5},{2,10},{3,11},{4,0},{5,1},{6,14},{7,15},{8,12},{9,13},... | collective-permute-start | bytes 1966088 | tf_op jit(solution)/shard_map/ppermute | solution.py:783
  95.9 11.3 %collective-permute-start.14 = (bf16[2,128,512]{2,1,0:T(8,128)(2,1)S(1)}, bf16[2,128,512]{2,1,0:T(8,128)(2,1)S(1)}, u32[]{:S(2)}, u32[]{:S(2)}) collective-permute-start(bf16[2,128,512]{2,1,0:T(8,128)(2,1)S(1)} %total.2.refs_2_.refs_0_), channel_id=1, source_target_pairs={{0,16},{1,17},{2,18},{3,19},{4,20},{5,21},{6,22},{7,23},{8,24},{9,... | collective-permute-start | bytes 786440 | tf_op jit(solution)/shard_map/ppermute | solution.py:783
  102.9 7.4 %collective-permute-start.13 = (bf16[2,160,512]{2,1,0:T(8,128)(2,1)S(1)}, bf16[2,160,512]{2,1,0:T(8,128)(2,1)S(1)}, u32[]{:S(2)}, u32[]{:S(2)}) collective-permute-start(bf16[2,160,512]{2,1,0:T(8,128)(2,1)S(1)} %bitcast.52), channel_id=1, source_target_pairs={{0,1},{1,0},{2,3},{3,2},{4,5},{5,4},{6,7},{7,6},{8,9},{9,8},{10,11... | collective-permute-start | bytes 983048 | tf_op jit(solution)/shard_map/ppermute | solution.py:783
  107.2 7.4 %collective-permute-start.16 = (bf16[256,512]{1,0:T(8,128)(2,1)S(1)}, bf16[256,512]{1,0:T(8,128)(2,1)S(1)}, u32[]{:S(2)}, u32[]{:S(2)}) collective-permute-start(bf16[256,512]{1,0:T(8,128)(2,1)S(1)} %bitcast.54), channel_id=1, source_target_pairs={{0,8},{1,9},{2,3},{3,2},{4,12},{5,13},{6,7},{7,6},{8,0},{9,1},{10,... | collective-permute-start | bytes 786440 | tf_op jit(solution)/shard_map/ppermute | solution.py:783
  110.4 6.0 %collective-permute-start.15 = (bf16[2,80,512]{2,1,0:T(8,128)(2,1)S(1)}, bf16[2,80,512]{2,1,0:T(8,128)(2,1)S(1)}, u32[]{:S(2)}, u32[]{:S(2)}) collective-permute-start(bf16[2,80,512]{2,1,0:T(8,128)(2,1)S(1)} %bitcast.59), channel_id=1, source_target_pairs={{0,8},{1,9},{2,6},{3,7},{4,12},{5,13},{6,2},{7,3},{8,0},{9,1},{10,... | collective-permute-start | bytes 491528 | tf_op jit(solution)/shard_map/ppermute | solution.py:783
  114.7 9.2 %collective-permute-start.18 = (bf16[512,512]{1,0:T(8,128)(2,1)S(1)}, bf16[512,512]{1,0:T(8,128)(2,1)S(1)}, u32[]{:S(2)}, u32[]{:S(2)}) collective-permute-start(bf16[512,512]{1,0:T(8,128)(2,1)S(1)} %bitcast.49), channel_id=1, source_target_pairs={{0,1},{1,0},{2,6},{3,7},{4,5},{5,4},{6,2},{7,3},{8,9},{9,8},{10,14... | collective-permute-start | bytes 1572872 | tf_op jit(solution)/shard_map/ppermute | solution.py:783
  116.4 11.3 %collective-permute-start.17 = (bf16[2,80,512]{2,1,0:T(8,128)(2,1)S(1)}, bf16[2,80,512]{2,1,0:T(8,128)(2,1)S(1)}, u32[]{:S(2)}, u32[]{:S(2)}) collective-permute-start(bf16[2,80,512]{2,1,0:T(8,128)(2,1)S(1)} %total.3.refs_2_.refs_0_), channel_id=1, source_target_pairs={{0,16},{1,17},{2,18},{3,19},{4,20},{5,21},{6,22},{7,23},{8,24},{9,... | collective-permute-start | bytes 491528 | tf_op jit(solution)/shard_map/ppermute | solution.py:783
  124.0 16.6 %collective-permute-start.21 = (bf16[1024,512]{1,0:T(8,128)(2,1)S(1)}, bf16[1024,512]{1,0:T(8,128)(2,1)S(1)}, u32[]{:S(2)}, u32[]{:S(2)}) collective-permute-start(bf16[1024,512]{1,0:T(8,128)(2,1)S(1)} %bitcast.32), channel_id=1, source_target_pairs={{0,4},{1,5},{2,10},{3,11},{4,0},{5,1},{6,14},{7,15},{8,12},{9,13},... | collective-permute-start | bytes 3145736 | tf_op jit(solution)/shard_map/ppermute | solution.py:783
  127.8 7.1 %collective-permute-start.19 = (bf16[160,512]{1,0:T(8,128)(2,1)S(1)}, bf16[160,512]{1,0:T(8,128)(2,1)S(1)}, u32[]{:S(2)}, u32[]{:S(2)}) collective-permute-start(bf16[160,512]{1,0:T(8,128)(2,1)S(1)} %bitcast.39), channel_id=1, source_target_pairs={{0,8},{1,9},{2,6},{3,7},{4,12},{5,13},{6,2},{7,3},{8,0},{9,1},{10,... | collective-permute-start | bytes 491528 | tf_op jit(solution)/shard_map/ppermute | solution.py:783
  134.9 13.4 %collective-permute-start.20 = (bf16[320,512]{1,0:T(8,128)(2,1)S(1)}, bf16[320,512]{1,0:T(8,128)(2,1)S(1)}, u32[]{:S(2)}, u32[]{:S(2)}) collective-permute-start(bf16[320,512]{1,0:T(8,128)(2,1)S(1)} %bitcast.29), channel_id=1, source_target_pairs={{0,1},{1,0},{2,3},{3,2},{4,5},{5,4},{6,7},{7,6},{8,9},{9,8},{10,11... | collective-permute-start | bytes 983048 | tf_op jit(solution)/shard_map/ppermute | solution.py:783
  147.1 8.4 %collective-permute-start.23 = (bf16[2,512,512]{2,1,0:T(8,128)(2,1)S(1)}, bf16[2,512,512]{2,1,0:T(8,128)(2,1)S(1)}, u32[]{:S(2)}, u32[]{:S(2)}) collective-permute-start(bf16[2,512,512]{2,1,0:T(8,128)(2,1)S(1)} %get-tuple-element.127.own), channel_id=1, source_target_pairs={{0,2},{1,3},{2,0},{3,1},{4,6},{5,7},{6,4},{7,5},{8,10},{9,11},{10,... | collective-permute-start | bytes 3145736 | tf_op jit(solution)/shard_map/ppermute | solution.py:783
  148.4 7.2 %copy-start.5 = (f32[1024,512]{1,0:T(8,128)S(1)}, f32[1024,512]{1,0:T(8,128)}, u32[]{:S(2)}) copy-start(f32[1024,512]{1,0:T(8,128)} %down_moment.1) | copy-start | bytes 6291460
  148.4 7.1 %copy-start.3 = (f32[512,1024]{1,0:T(8,128)S(1)}, f32[512,1024]{1,0:T(8,128)}, u32[]{:S(2)}) copy-start(f32[512,1024]{1,0:T(8,128)} %up_moment.1) | copy-start | bytes 6291460
  148.4 10.7 %collective-permute-start.22 = (bf16[640,512]{1,0:T(8,128)(2,1)S(1)}, bf16[640,512]{1,0:T(8,128)(2,1)S(1)}, u32[]{:S(2)}, u32[]{:S(2)}) collective-permute-start(bf16[640,512]{1,0:T(8,128)(2,1)S(1)} %bitcast.36), channel_id=1, source_target_pairs={{0,4},{1,5},{2,10},{3,11},{4,0},{5,1},{6,14},{7,15},{8,12},{9,13},... | collective-permute-start | bytes 1966088 | tf_op jit(solution)/shard_map/ppermute | solution.py:783
  155.2 4.7 %collective-permute-start.25 = (bf16[2,512,512]{2,1,0:T(8,128)(2,1)S(1)}, bf16[2,512,512]{2,1,0:T(8,128)(2,1)S(1)}, u32[]{:S(2)}, u32[]{:S(2)}) collective-permute-start(bf16[2,512,512]{2,1,0:T(8,128)(2,1)S(1)} %ortho_large.3.token.own), channel_id=1, source_target_pairs={{0,2},{1,3},{2,0},{3,1},{4,6},{5,7},{6,4},{7,5},{8,10},{9,11},{10,... | collective-permute-start | bytes 3145736 | tf_op jit(solution)/shard_map/ppermute | solution.py:783
  159.1 1.6 copy-start.12
  159.8 12.2 %collective-permute-start.24 = (bf16[2,272,512]{2,1,0:T(8,128)(2,1)S(1)}, bf16[2,272,512]{2,1,0:T(8,128)(2,1)S(1)}, u32[]{:S(2)}, u32[]{:S(2)}) collective-permute-start(bf16[2,272,512]{2,1,0:T(8,128)(2,1)S(1)} %get-tuple-element.129.mix.table), channel_id=1, source_target_pairs={{0,2},{1,3},{2,0},{3,1},{4,6},{5,7},{6,4},{7,5},{8,10},{9,11},{10,... | collective-permute-start | bytes 1671176 | tf_op jit(solution)/shard_map/ppermute | solution.py:783
  160.7 11.3 %copy-start.8 = (f32[4,256,512]{2,1,0:T(8,128)S(1)}, f32[4,256,512]{2,1,0:T(8,128)}, u32[]{:S(2)}) copy-start(f32[4,256,512]{2,1,0:T(8,128)} %moment.1) | copy-start | bytes 6291460
  160.7 11.3 %copy-start.15 = (f32[2,2,512]{2,1,0:T(2,128)S(1)}, f32[2,2,512]{2,1,0:T(2,128)}, u32[]{:S(2)}) copy-start(f32[2,2,512]{2,1,0:T(2,128)} %held_moment.1) | copy-start | bytes 24580
  172.0 2.6 %collective-permute-start.26 = (bf16[2,256,512]{2,1,0:T(8,128)(2,1)S(1)}, bf16[2,256,512]{2,1,0:T(8,128)(2,1)S(1)}, u32[]{:S(2)}, u32[]{:S(2)}) collective-permute-start(bf16[2,256,512]{2,1,0:T(8,128)(2,1)S(1)} %get-tuple-element.131.token.own), channel_id=1, source_target_pairs={{0,2},{1,3},{2,0},{3,1},{4,6},{5,7},{6,4},{7,5},{8,10},{9,11},{10,... | collective-permute-start | bytes 1572872 | tf_op jit(solution)/shard_map/ppermute | solution.py:783
  172.0 2.7 %copy-start.1 = (f32[4,512,512]{2,1,0:T(8,128)S(1)}, f32[4,512,512]{2,1,0:T(8,128)}, u32[]{:S(2)}) copy-start(f32[4,512,512]{2,1,0:T(8,128)} %weight.1) | copy-start | bytes 12582916
